TPU v7x, 32 devices: a whole 2x2x4 slice. The times are simulated.
32 devices in a mesh: mem: 4 (over y, x), col: 8 (over z, core).
Axes of the slice: x: 2, y: 2, z: 4, core: 2. Of those that a mesh axis runs over, the one named last changes fastest.
Arguments:
- increment: float32 [8, 131072], P(None, 'col'), may hold values from -6 to 6
- ensemble: bfloat16 [64, 8, 131072], P('mem', None, 'col'), may hold values from -15 to 15
- climate: float32 [8, 131072], P(None, 'col'), may hold values from 0.5 to 2
- restrict_dest: int32 [2048, 1], replicated, may hold values from 0 to 7; in each aligned block of 256 rows (0 to 255, 256 to 511, ...) at most 64 rows name the same one
- restrict_local: int32 [2048], replicated, may hold values from 0 to 255
- restrict_weight: float32 [131072], P('col'), may hold values from 0.05 to 0.2
- conv_blocks: bfloat16 [16, 4, 128, 128], P('col'), may hold values from -0.25 to 0.25
- neighbours: int32 [16, 4], P('col'), may hold values from 0 to 15, as said below
- interp_dest: int32 [2048, 2], replicated, may hold values from 0 to 7, all different within a row; in each aligned block of 256 rows (0 to 255, 256 to 511, ...) at most 128 rows name the same one
- interp_local: int32 [2048, 2], replicated, may hold values from 0 to 255
- interp_weight: float32 [2, 131072], P(None, 'col'), may hold values from 0.2 to 1
Outputs:
- once_applied: float32 [8, 131072], P(None, 'col')
- twice_applied: float32 [8, 131072], P(None, 'col')
Inputs may be any that keep to these rules, and one draw needn't show every extreme that they name: `restrict_dest`: in each aligned block of 256 rows (the tiles of one index of col) no device number appears in more than 64 rows. `interp_dest`: the two entries of a row differ. In each aligned block of 256 rows no device number appears in more than 128 rows. `neighbours`: the 4 entries of row b are distinct blocks among b - 2 to b + 2, taken modulo 16.
All inputs are finite; a program needn't handle non-finite values.
Results may differ from a plain program's by a relative error of at most 0.008.
Values may be sent and summed in bfloat16 or wider, within the bound.
No kernel may reach another device: no remote copies, remote signals or barrier semaphores. Data moves between devices by JAX's collectives and lax.ppermute only.
A program may use at most 128 MiB of HBM per device.

v0:
```python
import jax
import jax.numpy as jnp
from jax import lax
from jax.sharding import PartitionSpec as P

TILE = 64


def padded(array, sides, width):
    for axis, dim in sides:
        size, length = (lax.axis_size(axis), array.shape[dim])
        up = [(i, (i + 1) % size) for i in range(size)]
        down = [(j, i) for i, j in up]
        last = lax.slice_in_dim(array, length - width, length, axis=dim)
        leading = lax.slice_in_dim(array, 0, width, axis=dim)
        before = lax.ppermute(last, axis, up)
        after = lax.ppermute(leading, axis, down)
        array = jnp.concatenate([before, array, after], axis=dim)
    return array


def rank_slots(targets, count_all):
    onehot = (targets[:, None] == jnp.arange(count_all)[None, :]).astype(jnp.int32)
    before = jnp.cumsum(onehot, axis=0) - onehot
    return jnp.sum(before * onehot, axis=1)


def slot_nodes(targets, node_ids, myself, capacity):
    to_me = (targets == myself).astype(jnp.int32)
    before = jnp.cumsum(to_me, axis=1) - to_me
    slot_hits = to_me[:, :, None] * (
        before[:, :, None] == jnp.arange(capacity)[None, None, :]
    ).astype(jnp.int32)
    node_of = jnp.sum(slot_hits * node_ids[:, :, None], axis=1)
    filled = jnp.sum(slot_hits, axis=1)
    return (node_of.reshape(-1), filled.reshape(-1))


def unpack_matrix(node_of, filled, node_count):
    matched = (node_of[None, :] == jnp.arange(node_count)[:, None]) & (filled[None, :] > 0)
    return matched.astype(jnp.float32)


def pair_table(width):
    halves = jnp.arange(2 * width) // width
    return (halves[:, None] == jnp.arange(2)[None, :]).astype(jnp.float32)


def apply_once(
    state,
    ensemble,
    climate,
    restrict_dest,
    restrict_local,
    restrict_weight,
    conv_blocks,
    neighbours,
    interp_dest,
    interp_local,
    interp_weight,
):
    col_count = lax.axis_size("col")
    myself = lax.axis_index("col")
    members_here, levels, fine_local = ensemble.shape
    coarse_local = fine_local // TILE
    block_count = neighbours.shape[0]
    node_block = coarse_local // block_count
    capacity = max(2, 2 * coarse_local // col_count)
    feature = members_here * levels
    halves = pair_table(TILE)
    weighted = state * restrict_weight[None, :]
    product = ensemble.astype(jnp.float32) * weighted[None, :, :]
    paired = product.reshape(feature * (coarse_local // 2), 2 * TILE)
    tile_totals = jnp.dot(paired, halves, precision=lax.Precision.HIGHEST)
    partial_value = tile_totals.reshape(feature, coarse_local).T
    owner_all = restrict_dest[:, 0].reshape(col_count, coarse_local)
    local_all = restrict_local.reshape(col_count, coarse_local)
    my_owner = lax.dynamic_index_in_dim(owner_all, myself, 0, keepdims=False)
    slot_index = my_owner * capacity + rank_slots(my_owner, col_count)
    packing = (slot_index[None, :] == jnp.arange(col_count * capacity)[:, None]).astype(jnp.float32)
    outgoing = jnp.dot(packing, partial_value, precision=lax.Precision.HIGHEST).reshape(
        col_count, capacity, feature
    )
    incoming = lax.all_to_all(
        outgoing.astype(jnp.bfloat16), "col", split_axis=0, concat_axis=0, tiled=True
    ).astype(outgoing.dtype)
    node_of, filled = slot_nodes(owner_all, local_all, myself, capacity)
    unpack = unpack_matrix(node_of, filled, coarse_local)
    coarse = jnp.dot(unpack, incoming.reshape(-1, feature), precision=lax.Precision.HIGHEST)
    coarse_half = coarse.astype(jnp.bfloat16)
    extended = padded(coarse_half, (("col", 0),), coarse_local)
    block_total = block_count * col_count
    relative = (neighbours - (myself - 1) * block_count) % block_total
    chooser = (relative[:, :, None] == jnp.arange(3 * block_count)[None, None, :]).astype(
        jnp.bfloat16
    )
    picked = jnp.einsum(
        "bkr,rcm->bkcm",
        chooser,
        extended.reshape(3 * block_count, node_block, feature),
        preferred_element_type=jnp.float32,
    ).astype(jnp.bfloat16)
    convolved = jnp.einsum(
        "bkij,bkjm->bim", conv_blocks, picked, preferred_element_type=jnp.float32
    )
    node_values = convolved.reshape(coarse_local, feature).astype(jnp.bfloat16)
    capacity_pair = 2 * capacity
    targets_pair = interp_dest.reshape(col_count, 2 * coarse_local)
    nodes_pair = interp_local.reshape(col_count, 2 * coarse_local)
    node_of, filled = slot_nodes(targets_pair, nodes_pair, myself, capacity_pair)
    gather_rows = (
        (node_of[:, None] == jnp.arange(coarse_local)[None, :]) & (filled[:, None] > 0)
    ).astype(jnp.bfloat16)
    replies = jnp.dot(gather_rows, node_values, preferred_element_type=jnp.float32).astype(
        jnp.bfloat16
    )
    answers = lax.all_to_all(
        replies.reshape(col_count, capacity_pair, feature),
        "col",
        split_axis=0,
        concat_axis=0,
        tiled=True,
    )
    my_targets = lax.dynamic_index_in_dim(targets_pair, myself, 0, keepdims=False)
    slot_pair = my_targets * capacity_pair + rank_slots(my_targets, col_count)
    chooser_fine = (slot_pair[:, None] == jnp.arange(col_count * capacity_pair)[None, :]).astype(
        jnp.bfloat16
    )
    fetched = jnp.dot(
        chooser_fine, answers.reshape(-1, feature), preferred_element_type=jnp.float32
    )
    fetched_small = fetched.reshape(coarse_local, 2, feature).transpose(1, 2, 0)
    spread = halves.T
    first_value = jnp.dot(
        fetched_small[0].reshape(feature * (coarse_local // 2), 2),
        spread,
        precision=lax.Precision.HIGHEST,
    ).reshape(feature, fine_local)
    second_value = jnp.dot(
        fetched_small[1].reshape(feature * (coarse_local // 2), 2),
        spread,
        precision=lax.Precision.HIGHEST,
    ).reshape(feature, fine_local)
    interp = first_value * interp_weight[0][None, :] + second_value * interp_weight[1][None, :]
    member_terms = ensemble.reshape(feature, fine_local).astype(jnp.float32) * interp
    local_sum = jnp.sum(member_terms.reshape(members_here, levels, fine_local), axis=0)
    members_all = members_here * lax.axis_size("mem")
    ensemble_sum = lax.psum(local_sum, "mem")
    return climate * state + ensemble_sum / (members_all - 1)


def per_device(
    increment,
    ensemble,
    climate,
    restrict_dest,
    restrict_local,
    restrict_weight,
    conv_blocks,
    neighbours,
    interp_dest,
    interp_local,
    interp_weight,
):
    once_applied = apply_once(
        increment,
        ensemble,
        climate,
        restrict_dest,
        restrict_local,
        restrict_weight,
        conv_blocks,
        neighbours,
        interp_dest,
        interp_local,
        interp_weight,
    )
    twice_applied = apply_once(
        once_applied,
        ensemble,
        climate,
        restrict_dest,
        restrict_local,
        restrict_weight,
        conv_blocks,
        neighbours,
        interp_dest,
        interp_local,
        interp_weight,
    )
    return (once_applied, twice_applied)


def solution(mesh):
    in_specs = (
        P(None, "col"),
        P("mem", None, "col"),
        P(None, "col"),
        P(),
        P(),
        P("col"),
        P("col", None, None, None),
        P("col", None),
        P(),
        P(),
        P(None, "col"),
    )
    out_specs = (P(None, "col"), P(None, "col"))
    return jax.shard_map(
        per_device, mesh=mesh, in_specs=in_specs, out_specs=out_specs, check_vma=False
    )
```

profile of v0, /device:TPU:0, one launch (start us, length us, event | category | flops | bytes accessed | tf_op | source)
XLA Modules:
  0.0 371.7 jit_solution(13545520503073181821)
XLA Ops:
  7.2 0.5 broadcast.257
  7.7 1.4 reduce.15
  9.1 0.6 reduce-window.36
  10.1 1.1 broadcast_multiply_fusion.1
  11.2 6.3 %convert_multiply_fusion.3 = f32[16,8,16384]{2,1,0:T(8,128)} fusion(bf16[16,8,16384]{2,1,0:T(8,128)(2,1)} %param.12, f32[8,16384]{1,0:T(8,128)S(1)} %broadcast_multiply_fusion.1), kind=kLoop, calls=%fused_computation.3 | loop fusion | flops 4194304 | bytes 13107200 | tf_op jit(solution)/shard_map/mul | solution.py:72
  17.5 9.3 %reshape.316 = f32[16384,128]{1,0:T(8,128)} reshape(f32[16,8,16384]{2,1,0:T(8,128)} %convert_multiply_fusion.3) | data formatting | bytes 16777216 | tf_op jit(solution)/shard_map/reshape | solution.py:73
  26.8 8.3 %fusion.50 = f32[16384,2]{1,0:T(8,128)} fusion(f32[16384,128]{1,0:T(8,128)} %reshape.316, s32[128]{0:T(128)S(1)} %and_select_fusion), kind=kOutput, calls=%fused_computation.70 | convolution fusion | flops 50331904 | bytes 8520192 | tf_op jit(solution)/shard_map/dot_general | solution.py:74
  35.1 7.0 %reshape.334 = f32[128,256,1]{1,0,2:T(8,128)S(1)} reshape(f32[16384,2]{1,0:T(8,128)} %fusion.50) | data formatting | bytes 262144 | tf_op jit(solution)/shard_map/reshape | solution.py:75
  42.1 1.1 convolution_convert_fusion.5
  43.2 6.4 %all-to-all-start = ((bf16[8,64,128]{2,1,0:T(8,128)(2,1)}), bf16[8,64,128]{2,1,0:T(8,128)(2,1)S(1)}, u32[]{:S(2)}, u32[]{:S(2)}) async-start(bf16[8,64,128]{2,1,0:T(8,128)(2,1)} %convolution_convert_fusion.5), calls=%async_computation | async-start | bytes 262144 | tf_op jit(solution)/shard_map/all_to_all | solution.py:84
  50.0 0.6 reduce-window.34
  51.8 0.5 reshape.332
  52.4 1.1 reduce-window.30
  55.2 2.3 select_reduce_fusion
  57.9 3.6 collective-permute-start.1
  61.5 1.9 collective-permute-done.1
  63.4 3.6 collective-permute-done
  67.5 1.2 convolution_convert_fusion.2
  68.7 3.4 all-to-all-start.1
  72.4 1.1 reduce-window.26
  74.3 7.5 %all-to-all-done.1 = bf16[8,128,128]{2,1,0:T(8,128)(2,1)S(1)} async-done(((bf16[8,128,128]{2,1,0:T(8,128)(2,1)}), bf16[8,128,128]{2,1,0:T(8,128)(2,1)S(1)}, u32[]{:S(2)}, u32[]{:S(2)}) %all-to-all-start.1) | async-done | bytes 262176 | tf_op jit(solution)/shard_map/all_to_all | solution.py:117
  82.5 9.7 %reshape_squeeze.18 = f32[16384,2]{1,0:T(8,128)} reshape(f32[1,128,256]{2,1,0:T(8,128)S(1)} %copy.36) | data formatting | bytes 262144 | tf_op jit(solution)/shard_map/reshape;squeeze | solution.py:140
  92.2 8.5 %fusion.48 = f32[16384,128]{1,0:T(8,128)} fusion(f32[16384,2]{1,0:T(8,128)} %reshape_squeeze.18, s32[128]{0:T(128)S(1)} %and_select_fusion), kind=kOutput, calls=%fused_computation.68 | convolution fusion | flops 50331904 | bytes 8520192 | tf_op jit(solution)/shard_map/dot_general | solution.py:139
  100.8 9.4 %reshape.323 = f32[16,8,16384]{2,1,0:T(8,128)} reshape(f32[16384,128]{1,0:T(8,128)} %fusion.48) | data formatting | bytes 16777216 | tf_op jit(solution)/shard_map/reshape | solution.py:143
  110.1 9.7 %reshape_squeeze.17 = f32[16384,2]{1,0:T(8,128)} reshape(f32[1,128,256]{2,1,0:T(8,128)S(1)} %copy.35) | data formatting | bytes 262144 | tf_op jit(solution)/shard_map/reshape;squeeze | solution.py:135
  119.9 8.5 %fusion.49 = f32[16384,128]{1,0:T(8,128)} fusion(f32[16384,2]{1,0:T(8,128)} %reshape_squeeze.17, s32[128]{0:T(128)S(1)} %and_select_fusion), kind=kOutput, calls=%fused_computation.69 | convolution fusion | flops 50331904 | bytes 8520192 | tf_op jit(solution)/shard_map/dot_general | solution.py:134
  128.4 9.4 %reshape.322 = f32[16,8,16384]{2,1,0:T(8,128)} reshape(f32[16384,128]{1,0:T(8,128)} %fusion.49) | data formatting | bytes 16777216 | tf_op jit(solution)/shard_map/reshape | solution.py:138
  137.8 8.9 %fusion = f32[8,16384]{1,0:T(8,128)} fusion(bf16[16,8,16384]{2,1,0:T(8,128)(2,1)} %param.12, f32[16,8,16384]{2,1,0:T(8,128)} %reshape.323, f32[16,8,16384]{2,1,0:T(8,128)} %reshape.322, f32[16384]{0:T(1024)S(1)} %bitcast.105, f32[16384]{0:T(1024)S(1)} %bitcast.103), kind=kLoop, calls=%fused_computation.4 | loop fusion | flops 12451840 | bytes 21626880 | tf_op jit(solution)/shard_map/reduce_sum | solution.py:146
  147.0 44.2 %all-reduce.3.cloned.1.call-done = f32[8,16384]{1,0:T(8,128)} async-done(((f32[8,16384]{1,0:T(8,128)}), f32[8,16384]{1,0:T(8,128)}) %all-reduce.3.cloned.1.call-update) | async-done | bytes 524304 | tf_op jit(solution)/shard_map/psum | solution.py:148
  191.2 1.2 broadcast_multiply_fusion
  192.3 6.5 %convert_multiply_fusion.1 = f32[16,8,16384]{2,1,0:T(8,128)} fusion(bf16[16,8,16384]{2,1,0:T(8,128)(2,1)} %param.12, f32[8,16384]{1,0:T(8,128)S(1)} %get-tuple-element.6), kind=kLoop, calls=%fused_computation.1 | loop fusion | flops 4194304 | bytes 13107200 | tf_op jit(solution)/shard_map/mul | solution.py:72
  198.9 9.3 %reshape.324 = f32[16384,128]{1,0:T(8,128)} reshape(f32[16,8,16384]{2,1,0:T(8,128)} %convert_multiply_fusion.1) | data formatting | bytes 16777216 | tf_op jit(solution)/shard_map/reshape | solution.py:73
  208.1 8.3 %fusion.47 = f32[16384,2]{1,0:T(8,128)} fusion(f32[16384,128]{1,0:T(8,128)} %reshape.324, s32[128]{0:T(128)S(1)} %and_select_fusion), kind=kOutput, calls=%fused_computation.67 | convolution fusion | flops 50331904 | bytes 8520192 | tf_op jit(solution)/shard_map/dot_general | solution.py:74
  216.4 6.9 %reshape.339 = f32[128,256,1]{1,0,2:T(8,128)S(1)} reshape(f32[16384,2]{1,0:T(8,128)} %fusion.47) | data formatting | bytes 262144 | tf_op jit(solution)/shard_map/reshape | solution.py:75
  223.8 11.1 %all_to_all.20 = bf16[8,64,128]{2,1,0:T(8,128)(2,1)S(1)} all-to-all(bf16[8,64,128]{2,1,0:T(8,128)(2,1)S(1)} %convolution_convert_fusion.4), channel_id=1, replica_groups=mesh['mem'=4,'col'=8] {'col'}, dimensions={0} | all-to-all | bytes 262144 | tf_op jit(solution)/shard_map/all_to_all | solution.py:84
  235.2 0.7 collective-permute-start.3
  235.9 2.4 collective-permute-done.3
  238.3 3.1 collective-permute-done.2
  242.4 12.1 %all_to_all.21 = bf16[8,128,128]{2,1,0:T(8,128)(2,1)S(1)} all-to-all(bf16[8,128,128]{2,1,0:T(8,128)(2,1)S(1)} %bitcast.108), channel_id=1, replica_groups=mesh['mem'=4,'col'=8] {'col'}, dimensions={0} | all-to-all | bytes 524288 | tf_op jit(solution)/shard_map/all_to_all | solution.py:117
  255.2 9.7 %reshape_squeeze.20 = f32[16384,2]{1,0:T(8,128)} reshape(f32[1,128,256]{2,1,0:T(8,128)S(1)} %copy.41) | data formatting | bytes 262144 | tf_op jit(solution)/shard_map/reshape;squeeze | solution.py:140
  265.0 8.5 %fusion.45 = f32[16384,128]{1,0:T(8,128)} fusion(f32[16384,2]{1,0:T(8,128)} %reshape_squeeze.20, s32[128]{0:T(128)S(1)} %and_select_fusion), kind=kOutput, calls=%fused_computation.65 | convolution fusion | flops 50331904 | bytes 8520192 | tf_op jit(solution)/shard_map/dot_general | solution.py:139
  273.5 9.4 %reshape.331 = f32[16,8,16384]{2,1,0:T(8,128)} reshape(f32[16384,128]{1,0:T(8,128)} %fusion.45) | data formatting | bytes 16777216 | tf_op jit(solution)/shard_map/reshape | solution.py:143
  282.9 9.7 %reshape_squeeze.19 = f32[16384,2]{1,0:T(8,128)} reshape(f32[1,128,256]{2,1,0:T(8,128)S(1)} %copy.40) | data formatting | bytes 262144 | tf_op jit(solution)/shard_map/reshape;squeeze | solution.py:135
  292.6 8.5 %fusion.46 = f32[16384,128]{1,0:T(8,128)} fusion(f32[16384,2]{1,0:T(8,128)} %reshape_squeeze.19, s32[128]{0:T(128)S(1)} %and_select_fusion), kind=kOutput, calls=%fused_computation.66 | convolution fusion | flops 50331904 | bytes 8520192 | tf_op jit(solution)/shard_map/dot_general | solution.py:134
  301.2 9.4 %reshape.330 = f32[16,8,16384]{2,1,0:T(8,128)} reshape(f32[16384,128]{1,0:T(8,128)} %fusion.46) | data formatting | bytes 16777216 | tf_op jit(solution)/shard_map/reshape | solution.py:138
  310.6 8.8 %fusion.1 = f32[8,16384]{1,0:T(8,128)} fusion(bf16[16,8,16384]{2,1,0:T(8,128)(2,1)} %param.12, f32[16,8,16384]{2,1,0:T(8,128)} %reshape.331, f32[16,8,16384]{2,1,0:T(8,128)} %reshape.330, f32[16384]{0:T(1024)S(1)} %bitcast.106, f32[16384]{0:T(1024)S(1)} %bitcast.104), kind=kLoop, calls=%fused_computation.5 | loop fusion | flops 12451840 | bytes 21626880 | tf_op jit(solution)/shard_map/reduce_sum | solution.py:146
  319.4 43.5 %all-reduce.5.cloned.1.call-done = f32[8,16384]{1,0:T(8,128)} async-done(((f32[8,16384]{1,0:T(8,128)}), f32[8,16384]{1,0:T(8,128)}) %all-reduce.5.cloned.1.call-update) | async-done | bytes 524304 | tf_op jit(solution)/shard_map/psum | solution.py:148
  362.9 1.9 multiply_add_fusion
  (92 shorter events, 8.9 us)
Async XLA Ops:
  7.2 60.1 %copy-start = (bf16[2,4,128,128]{3,2,1,0:T(8,128)(2,1)S(1)}, bf16[2,4,128,128]{3,2,1,0:T(8,128)(2,1)}, u32[]{:S(2)}) copy-start(bf16[2,4,128,128]{3,2,1,0:T(8,128)(2,1)} %param.17) | copy-start | bytes 786436
  35.1 14.5 %copy-start.7 = (s32[2048,1]{0,1:T(1,128)S(1)}, s32[2048,1]{0,1:T(1,128)}, u32[]{:S(2)}) copy-start(s32[2048,1]{0,1:T(1,128)} %param.14) | copy-start | bytes 24580
  35.1 14.5 %copy-start.6 = (s32[2048,2]{0,1:T(2,128)S(1)}, s32[2048,2]{0,1:T(2,128)}, u32[]{:S(2)}) copy-start(s32[2048,2]{0,1:T(2,128)} %param.19) | copy-start | bytes 49156
  35.1 14.9 %copy-start.9 = (s32[2048]{0:T(1024)S(1)}, s32[2048]{0:T(1024)}, u32[]{:S(2)}) copy-start(s32[2048]{0:T(1024)} %param.15) | copy-start | bytes 24580
  35.1 16.3 %copy-start.5 = (f32[2,16384]{1,0:T(2,128)S(1)}, f32[2,16384]{1,0:T(2,128)}, u32[]{:S(2)}) copy-start(f32[2,16384]{1,0:T(2,128)} %param.21) | copy-start | bytes 393220
  35.1 18.7 %copy-start.8 = (s32[2048,2]{0,1:T(2,128)S(1)}, s32[2048,2]{0,1:T(2,128)}, u32[]{:S(2)}) copy-start(s32[2048,2]{0,1:T(2,128)} %param.20) | copy-start | bytes 49156
  35.1 26.4 %copy-start.10 = (s32[2,4]{1,0:T(2,128)S(1)}, s32[2,4]{1,0:T(2,128)}, u32[]{:S(2)}) copy-start(s32[2,4]{1,0:T(2,128)} %param.18) | copy-start | bytes 100
  43.2 14.4 %all-to-all-start = ((bf16[8,64,128]{2,1,0:T(8,128)(2,1)}), bf16[8,64,128]{2,1,0:T(8,128)(2,1)S(1)}, u32[]{:S(2)}, u32[]{:S(2)}) async-start(bf16[8,64,128]{2,1,0:T(8,128)(2,1)} %convolution_convert_fusion.5), calls=%async_computation | async-start | bytes 262144 | tf_op jit(solution)/shard_map/all_to_all | solution.py:84
  57.9 5.5 %collective-permute-start.1 = (bf16[256,128]{1,0:T(8,128)(2,1)S(1)}, bf16[256,128]{1,0:T(8,128)(2,1)S(1)}, u32[]{:S(2)}, u32[]{:S(2)}) collective-permute-start(bf16[256,128]{1,0:T(8,128)(2,1)S(1)} %convolution_convert_fusion.7), channel_id=1, source_target_pairs={{1,0},{2,1},{3,2},{4,3},{5,4},{6,5},{7,6},{0,7},{9,8},{10,9},{11,1... | collective-permute-start | bytes 196616 | tf_op jit(solution)/shard_map/ppermute | solution.py:17
  61.5 5.5 %collective-permute-start = (bf16[256,128]{1,0:T(8,128)(2,1)S(1)}, bf16[256,128]{1,0:T(8,128)(2,1)S(1)}, u32[]{:S(2)}, u32[]{:S(2)}) collective-permute-start(bf16[256,128]{1,0:T(8,128)(2,1)S(1)} %convolution_convert_fusion.7), channel_id=1, source_target_pairs={{0,1},{1,2},{2,3},{3,4},{4,5},{5,6},{6,7},{7,0},{8,9},{9,10},{10,1... | collective-permute-start | bytes 196616 | tf_op jit(solution)/shard_map/ppermute | solution.py:16
  68.7 13.1 %all-to-all-start.1 = ((bf16[8,128,128]{2,1,0:T(8,128)(2,1)}), bf16[8,128,128]{2,1,0:T(8,128)(2,1)S(1)}, u32[]{:S(2)}, u32[]{:S(2)}) async-start(bf16[8,128,128]{2,1,0:T(8,128)(2,1)} %bitcast.25), calls=%async_computation.1 | async-start | bytes 524288 | tf_op jit(solution)/shard_map/all_to_all | solution.py:117
  72.1 119.1 %all-reduce.3.cloned.1.call-start = ((), (), s32[]{:S(2)}) async-start(), calls=%async_computation.4 | async-start | bytes 1048576 | tf_op jit(solution)/shard_map/psum | solution.py:148
  137.8 53.4 %copy-start.1 = (f32[8,16384]{1,0:T(8,128)S(1)}, f32[8,16384]{1,0:T(8,128)}, u32[]{:S(2)}) copy-start(f32[8,16384]{1,0:T(8,128)} %param.11) | copy-start | bytes 1572868
  137.8 53.4 %copy-start.2 = (f32[8,16384]{1,0:T(8,128)S(1)}, f32[8,16384]{1,0:T(8,128)}, u32[]{:S(2)}) copy-start(f32[8,16384]{1,0:T(8,128)} %param.13) | copy-start | bytes 1572868
  137.8 53.4 %copy-start.4 = (f32[16384]{0:T(1024)S(1)}, f32[16384]{0:T(1024)}, u32[]{:S(2)}) copy-start(f32[16384]{0:T(1024)} %param.16) | copy-start | bytes 196612
  146.7 216.2 %all-reduce.5.cloned.1.call-start = ((), (), s32[]{:S(2)}) async-start(), calls=%async_computation.5 | async-start | bytes 1048576 | tf_op jit(solution)/shard_map/psum | solution.py:148
  192.3 170.6 %copy-start.3 = (f32[8,16384]{1,0:T(8,128)}, f32[8,16384]{1,0:T(8,128)S(1)}, u32[]{:S(2)}) copy-start(f32[8,16384]{1,0:T(8,128)S(1)} %get-tuple-element.7) | copy-start | bytes 1572868
  235.2 3.1 collective-permute-start.3
  235.9 5.5 %collective-permute-start.2 = (bf16[256,128]{1,0:T(8,128)(2,1)S(1)}, bf16[256,128]{1,0:T(8,128)(2,1)S(1)}, u32[]{:S(2)}, u32[]{:S(2)}) collective-permute-start(bf16[256,128]{1,0:T(8,128)(2,1)S(1)} %convolution_convert_fusion.6), channel_id=1, source_target_pairs={{0,1},{1,2},{2,3},{3,4},{4,5},{5,6},{6,7},{7,0},{8,9},{9,10},{10,1... | collective-permute-start | bytes 196616 | tf_op jit(solution)/shard_map/ppermute | solution.py:16
Sparse Core Ops, SparseCore 0:
  146.8 44.2 all-reduce.2
  319.5 43.3 all-reduce.4
where the time goes:
time: 374 us; the launch traced here: 372 us
  local copies, waits for them, and re-layouts  114 us (30%)
  waiting for transfers between devices  106 us (28%)
  matrix products  56.3 us (15%)
  other arithmetic  42.9 us (11%)
  blocking collectives  23.3 us (6%)
  starting transfers between devices  14.6 us (4%)
  between operations  14.5 us (4%)
    psum x2, waiting for transfers between devices, apply_once(): ensemble_sum = lax.psum(local_sum, 'mem')  87.7 us
    another operation x2, local copies, waits for them, and re-layouts, apply_once(): fetched_small[1].reshape(feature * (coarse_local // 2), 2)  19.5 us
    another operation x2, local copies, waits for them, and re-layouts, apply_once(): fetched_small[0].reshape(feature * (coarse_local // 2), 2)  19.4 us
    reshape x2, local copies, waits for them, and re-layouts, apply_once(): second_value = jnp.dot(fetched_small[1].reshape(feature * (coarse_local /...  18.8 us
    reshape x2, local copies, waits for them, and re-layouts, apply_once(): first_value = jnp.dot(fetched_small[0].reshape(feature * (coarse_local //...  18.8 us
    reshape x2, local copies, waits for them, and re-layouts, apply_once(): paired = product.reshape(feature * (coarse_local // 2), 2 * TILE)  18.6 us
    reduce_sum x2, other arithmetic, apply_once(): jnp.sum(member_terms.reshape(members_here, levels, fine_local), axis=0)  17.7 us
    dot_general x2, matrix products, apply_once(): jnp.dot(fetched_small[0].reshape(feature * (coarse_local // 2), 2), sprea...  17.1 us
  transfers between devices with their start and end apart: 8, of which 7 were waited for; matrix products, arithmetic and copies ran while one was open for 3% of the time, Pallas kernels for 0%

commit v1 on v0

v1 whole, which is shorter than its diff:
```python
import functools

import jax
import jax.numpy as jnp
from jax import lax
from jax.experimental import pallas as pl
from jax.experimental.pallas import tpu as pltpu
from jax.sharding import PartitionSpec as P

TILE = 64
LANES = 128
ROWS16 = 16
VMEM_BYTES = 48 * 1024 * 1024
HALF = jnp.bfloat16
FULL = jnp.float32


def swap(array, axis, mask):
    size = lax.axis_size(axis)
    return lax.ppermute(array, axis, [(i, i ^ mask) for i in range(size)])


def gather_slots(array):
    size = lax.axis_size("col")
    myself = lax.axis_index("col")
    if size == 8:
        same_core = [array] + [swap(array, "col", mask) for mask in (6, 4, 2)]
        other_core = [swap(piece, "col", 1) for piece in same_core]
        masks = jnp.array([0, 6, 4, 2, 1, 7, 5, 3], jnp.int32)
        return same_core + other_core, masks ^ myself
    stacked = lax.all_gather(array, "col")
    return [stacked[i] for i in range(size)], jnp.arange(size, dtype=jnp.int32)


def tile_indicator(tiles, columns):
    tile = lax.broadcasted_iota(jnp.int32, (tiles, columns), 0)
    column = lax.broadcasted_iota(jnp.int32, (tiles, columns), 1)
    return (column >= tile * TILE) & (column < tile * TILE + TILE)


def tile_sums(state, weight, ensemble_ref, partial_ref):
    members, levels, width = ensemble_ref.shape
    tiles = width // TILE
    weighted = state * weight
    product = ensemble_ref[...].astype(FULL) * weighted[None]
    product = product.reshape(members * levels, width).astype(HALF)
    indicator = jnp.where(tile_indicator(tiles, width), 1.0, 0.0).astype(HALF)
    partial_ref[...] = lax.dot_general(
        indicator, product, (((1,), (1,)), ((), ())), preferred_element_type=FULL
    ).astype(HALF)


def first_kernel(state_ref, weight_ref, ensemble_ref, partial_ref):
    tile_sums(state_ref[...], weight_ref[...], ensemble_ref, partial_ref)


def second_kernel(
    scale, state_ref, climate_ref, mine_ref, theirs_ref, weight_ref, ensemble_ref, state_out, partial_ref
):
    total = mine_ref[...].astype(FULL) + theirs_ref[...].astype(FULL)
    state = climate_ref[...] * state_ref[...] + total * scale
    state_out[...] = state
    tile_sums(state, weight_ref[...], ensemble_ref, partial_ref)


def params():
    return pltpu.CompilerParams(vmem_limit_bytes=VMEM_BYTES)


def column_sizes(ensemble):
    members, levels, fine = ensemble.shape
    width = min(fine, LANES // 4 * TILE)
    return members, levels, fine, width, fine // width


def run_first(state, weight, ensemble):
    members, levels, fine, width, steps = column_sizes(ensemble)
    tiles = width // TILE
    return pl.pallas_call(
        first_kernel,
        grid=(steps,),
        in_specs=[
            pl.BlockSpec((levels, width), lambda i: (0, i)),
            pl.BlockSpec((1, width), lambda i: (0, i)),
            pl.BlockSpec((members, levels, width), lambda i: (0, 0, i)),
        ],
        out_specs=pl.BlockSpec((tiles, members * levels), lambda i: (i, 0)),
        out_shape=jax.ShapeDtypeStruct((fine // TILE, members * levels), HALF),
        compiler_params=params(),
        name="tile_sums_first",
    )(state, weight, ensemble)


def run_second(scale, state, climate, mine, theirs, weight, ensemble):
    members, levels, fine, width, steps = column_sizes(ensemble)
    tiles = width // TILE
    row = pl.BlockSpec((levels, width), lambda i: (0, i))
    return pl.pallas_call(
        functools.partial(second_kernel, scale),
        grid=(steps,),
        in_specs=[
            row,
            row,
            row,
            row,
            pl.BlockSpec((1, width), lambda i: (0, i)),
            pl.BlockSpec((members, levels, width), lambda i: (0, 0, i)),
        ],
        out_specs=[row, pl.BlockSpec((tiles, members * levels), lambda i: (i, 0))],
        out_shape=[
            jax.ShapeDtypeStruct((levels, fine), FULL),
            jax.ShapeDtypeStruct((fine // TILE, members * levels), HALF),
        ],
        compiler_params=params(),
        name="tile_sums_second",
    )(state, climate, mine, theirs, weight, ensemble)


def matrix_kernel(slots, blocks, neigh, target_ref, tile_row_ref, tile_block_ref, *refs):
    conv_refs, matrix_ref = refs[:slots], refs[slots]
    pairs = target_ref.shape[0]
    size = LANES
    nodes = blocks * size
    target = target_ref[...]
    chosen = jnp.zeros((pairs, neigh * size), FULL)
    for s in range(slots):
        node = lax.broadcasted_iota(jnp.int32, (pairs, nodes), 1) + s * nodes
        pick = jnp.where(node == target, 1.0, 0.0).astype(HALF)
        rows = [
            jnp.concatenate(
                [conv_refs[s][pl.ds((b * neigh + k) * size, size), :] for k in range(neigh)], axis=1
            )
            for b in range(blocks)
        ]
        chosen = chosen + jnp.dot(pick, jnp.concatenate(rows, axis=0), preferred_element_type=FULL)
    chosen = chosen.astype(HALF)
    table = jnp.concatenate(
        [ref[pl.ds(blocks * neigh * size, ROWS16), :] for ref in conv_refs], axis=0
    )
    slot_of = target // nodes
    block_of = slot_of * ROWS16 + (target - slot_of * nodes) // size
    entry = lax.broadcasted_iota(jnp.int32, (pairs, slots * ROWS16), 1)
    near = jnp.dot(
        jnp.where(entry == block_of, 1.0, 0.0).astype(HALF), table, preferred_element_type=FULL
    )
    for s in range(slots):
        span = pl.ds(s * nodes, nodes)
        row = lax.broadcasted_iota(jnp.int32, (size, nodes), 0)
        place = jnp.where(row == tile_row_ref[:, span], 1.0, 0.0).astype(HALF)
        block = tile_block_ref[:, span].astype(FULL)
        value = jnp.zeros((pairs, nodes), FULL)
        for k in range(neigh):
            moved = jnp.dot(chosen[:, k * size : (k + 1) * size], place, preferred_element_type=FULL)
            value = jnp.where(near[:, k : k + 1] == block, moved, value)
        matrix_ref[:, span] = value.astype(HALF)


def run_matrix(target, tile_row, tile_block, conv_all, blocks, neigh):
    slots = len(conv_all)
    return pl.pallas_call(
        functools.partial(matrix_kernel, slots, blocks, neigh),
        in_specs=[pl.BlockSpec(memory_space=pltpu.VMEM)] * (3 + slots),
        out_specs=pl.BlockSpec(memory_space=pltpu.VMEM),
        out_shape=jax.ShapeDtypeStruct((target.shape[0], tile_row.shape[1]), HALF),
        compiler_params=params(),
        name="pair_matrix",
    )(target, tile_row, tile_block, *conv_all)


def spread_kernel(slots, matrix_ref, ensemble_ref, weight_ref, *refs):
    partial_refs, out_ref, values_ref = refs[:slots], refs[slots], refs[slots + 1]
    members, levels, width = ensemble_ref.shape
    tiles = width // TILE
    feature = members * levels

    @pl.when(pl.program_id(0) == 0)
    def _():
        span = partial_refs[0].shape[0]
        pairs = matrix_ref.shape[0]
        values = jnp.zeros((pairs, feature), FULL)
        for s in range(slots):
            values = values + jnp.dot(
                matrix_ref[:, s * span : (s + 1) * span],
                partial_refs[s][...],
                preferred_element_type=FULL,
            )
        values = values.T
        half = 2 * tiles
        lane = lax.broadcasted_iota(jnp.int32, (feature, 2 * half), 1)
        for i in range(pairs // half):
            two = values[:, i // 2 * 2 * half : (i // 2 + 1) * 2 * half]
            turned = pltpu.roll(two, half, 1)
            keep = (lane < half) if i % 2 == 0 else (lane >= half)
            values_ref[i] = jnp.where(keep, two, turned).astype(HALF)

    inside = tile_indicator(tiles, width)
    high = weight_ref[...].astype(HALF).astype(FULL)
    low = weight_ref[...] - high
    weights = jnp.concatenate(
        [
            jnp.where(inside, part[k : k + 1, :], 0.0).astype(HALF)
            for part in (high, low)
            for k in range(2)
        ],
        axis=0,
    )
    left = values_ref[pl.program_id(0)]
    piece = 4 * LANES
    for c in range(0, width, piece):
        field = jnp.dot(left, weights[:, c : c + piece], preferred_element_type=FULL)
        field = field.reshape(members, levels, piece)
        terms = ensemble_ref[:, :, c : c + piece].astype(FULL) * field
        out_ref[:, c : c + piece] = jnp.sum(terms, axis=0).astype(HALF)


def run_spread(matrix, ensemble, interp_weight, partial_all):
    members, levels, fine, width, steps = column_sizes(ensemble)
    slots = len(partial_all)
    feature = members * levels
    whole = pl.BlockSpec(memory_space=pltpu.VMEM)
    return pl.pallas_call(
        functools.partial(spread_kernel, slots),
        grid=(steps,),
        in_specs=[
            whole,
            pl.BlockSpec((members, levels, width), lambda i: (0, 0, i)),
            pl.BlockSpec((2, width), lambda i: (0, i)),
        ]
        + [whole] * slots,
        out_specs=pl.BlockSpec((levels, width), lambda i: (0, i)),
        out_shape=jax.ShapeDtypeStruct((levels, fine), HALF),
        scratch_shapes=[pltpu.VMEM((steps, feature, LANES), HALF)],
        compiler_params=params(),
        name="spread",
    )(matrix, ensemble, interp_weight, *partial_all)


def add_half(one, two):
    return (one.astype(FULL) + two.astype(FULL)).astype(HALF)


def member_sum(local):
    size = lax.axis_size("mem")
    masks = [1 << i for i in range(size.bit_length() - 1)]
    middle = local.shape[1] // 2
    halves = [local[:, :middle], local[:, middle:]]
    orders = [masks, masks[::-1]]
    for step in range(len(masks) - 1):
        moved = [swap(part, "mem", order[step]) for part, order in zip(halves, orders)]
        halves = [add_half(part, other) for part, other in zip(halves, moved)]
    moved = [swap(part, "mem", order[-1]) for part, order in zip(halves, orders)]
    return jnp.concatenate(halves, axis=1), jnp.concatenate(moved, axis=1)


def per_device(
    increment,
    ensemble,
    climate,
    restrict_dest,
    restrict_local,
    restrict_weight,
    conv_blocks,
    neighbours,
    interp_dest,
    interp_local,
    interp_weight,
):
    col_count = lax.axis_size("col")
    myself = lax.axis_index("col")
    members, levels, fine, width, steps = column_sizes(ensemble)
    coarse_local = fine // TILE
    blocks, neigh = neighbours.shape
    node_block = coarse_local // blocks
    scale = 1.0 / (members * lax.axis_size("mem") - 1)
    weight = restrict_weight[None, :]

    near = jnp.pad(
        neighbours.astype(HALF), ((0, ROWS16 - blocks), (0, node_block - neigh))
    )
    rows = conv_blocks.reshape(blocks * neigh * node_block, node_block)
    conv_all, sources = gather_slots(jnp.concatenate([rows, near], axis=0))

    owner = lax.dynamic_slice_in_dim(interp_dest, myself * coarse_local, coarse_local, 0)
    local = lax.dynamic_slice_in_dim(interp_local, myself * coarse_local, coarse_local, 0)
    slot = jnp.sum(
        jnp.where(owner[:, :, None] == sources[None, None, :], jnp.arange(col_count)[None, None, :], 0),
        axis=2,
    )
    target = slot * coarse_local + local
    target = target.reshape(steps, width // TILE, 2).transpose(0, 2, 1).reshape(-1, 1)
    owner_all = restrict_dest[:, 0].reshape(col_count, coarse_local)[sources].reshape(1, -1)
    local_all = restrict_local.reshape(col_count, coarse_local)[sources].reshape(1, -1)
    tile_row = local_all % node_block
    tile_block = owner_all * blocks + local_all // node_block

    partial = run_first(increment, weight, ensemble)
    partial_all, _ = gather_slots(partial)
    matrix = run_matrix(target, tile_row, tile_block, conv_all, blocks, neigh)
    mine, theirs = member_sum(run_spread(matrix, ensemble, interp_weight, partial_all))
    once_applied, partial = run_second(scale, increment, climate, mine, theirs, weight, ensemble)
    partial_all, _ = gather_slots(partial)
    mine, theirs = member_sum(run_spread(matrix, ensemble, interp_weight, partial_all))
    total = mine.astype(FULL) + theirs.astype(FULL)
    return once_applied, climate * once_applied + total * scale


def solution(mesh):
    in_specs = (
        P(None, "col"),
        P("mem", None, "col"),
        P(None, "col"),
        P(),
        P(),
        P("col"),
        P("col", None, None, None),
        P("col", None),
        P(),
        P(),
        P(None, "col"),
    )
    out_specs = (P(None, "col"), P(None, "col"))
    return jax.shard_map(
        per_device, mesh=mesh, in_specs=in_specs, out_specs=out_specs, check_vma=False
    )
```

time: 374 us -> 102 us (0.27)
  local copies, waits for them, and re-layouts: 114 us -> 6.18 us
  waiting for transfers between devices: 106 us -> 40.1 us
  matrix products: 56.3 us -> 0 us
  other arithmetic: 42.9 us -> 4.25 us
  Pallas kernels: 0 us -> 23.9 us
  blocking collectives: 23.3 us -> 0 us
  between operations: 14.5 us -> 0.95 us
  starting transfers between devices: 14.6 us -> 26.4 us
    psum x2 -> x0, waiting for transfers between devices: 87.7 us -> none  [apply_once(): ensemble_sum = lax.psum(local_sum, 'mem')]
    reshape x9 -> x4, local copies, waits for them, and re-layouts: 70.5 us -> 0.35 us  [the longest x3 0.35 us: per_device(): target.reshape(steps, width // TILE, 2).transpose(0, 2, 1).reshape(-1, 1)]
    dot_general x18 -> x0, matrix products: 56.3 us -> none  [the longest x2 17.1 us: apply_once(): jnp.dot(fetched_small[0].reshape(feature * (coarse_local // 2), 2), sprea...]
    another operation x12 -> x1, local copies, waits for them, and re-layouts: 39.6 us -> 0.01 us  [per_device(): restrict_dest[:, 0].reshape(col_count, coarse_local)[sources].reshape(1, -1)]
    ppermute x4 -> x29, waiting for transfers between devices: 11 us -> 40.1 us  [swap(): return lax.ppermute(array, axis, [(i, i ^ mask) for i in range(size)])]
    pallas_call x0 -> x5, Pallas kernels: none -> 23.9 us  [the longest x2 13.9 us: run_spread(): pl.pallas_call(functools.partial(spread_kernel, slots), grid=(steps,), in...]
    all_to_all x2 -> x0, blocking collectives: 23.3 us -> none  [the longest x1 12.1 us: apply_once(): lax.all_to_all(replies.reshape(col_count, capacity_pair, feature), 'col',...]
    ppermute x4 -> x29, starting transfers between devices: 4.34 us -> 26.4 us  [swap(): return lax.ppermute(array, axis, [(i, i ^ mask) for i in range(size)])]
  transfers between devices with their start and end apart: 8 -> 29, of which waited for: 7 -> 15; matrix products, arithmetic and copies ran while one was open for 3% -> 3% of each run, Pallas kernels for 0% -> 6%
where the time goes in v1:
time: 102 us
  waiting for transfers between devices  40.1 us (39%)
  starting transfers between devices  26.4 us (26%)
  Pallas kernels  23.9 us (23%)
  local copies, waits for them, and re-layouts  6.18 us (6%)
  other arithmetic  4.25 us (4%)
    ppermute x29, waiting for transfers between devices, swap(): return lax.ppermute(array, axis, [(i, i ^ mask) for i in range(size)])  40.1 us
    ppermute x29, starting transfers between devices, swap(): return lax.ppermute(array, axis, [(i, i ^ mask) for i in range(size)])  26.4 us
    pallas_call x2, Pallas kernels, run_spread(): pl.pallas_call(functools.partial(spread_kernel, slots), grid=(steps,), in...  13.9 us
    unnamed x29, local copies, waits for them, and re-layouts  4.66 us
    pallas_call x1, Pallas kernels, run_matrix(): pl.pallas_call(functools.partial(matrix_kernel, slots, blocks, neigh), in...  3.8 us
    pallas_call x1, Pallas kernels, run_second(): pl.pallas_call(functools.partial(second_kernel, scale), grid=(steps,), in...  3.59 us
    pallas_call x1, Pallas kernels, run_first(): pl.pallas_call(first_kernel, grid=(steps,), in_specs=[pl.BlockSpec((level...  2.63 us
  transfers between devices with their start and end apart: 29, of which 15 were waited for; matrix products, arithmetic and copies ran while one was open for 3% of the time, Pallas kernels for 6%

profile of v1, /device:TPU:0, one launch (start us, length us, event | category | flops | bytes accessed | tf_op | source)
XLA Modules:
  0.0 101.7 jit_solution(1780626656347585291)
XLA Ops:
  0.7 0.7 convert_element_type.47
  1.4 1.0 fusion.1.refs_0_
  2.4 5.1 %collective-permute-start = (bf16[1040,128]{1,0:T(8,128)(2,1)S(1)}, bf16[1040,128]{1,0:T(8,128)(2,1)S(1)}, u32[]{:S(2)}, u32[]{:S(2)}) collective-permute-start(bf16[1040,128]{1,0:T(8,128)(2,1)S(1)} %fusion.1.refs_0_), channel_id=1, source_target_pairs={{0,6},{1,7},{2,4},{3,5},{4,2},{5,3},{6,0},{7,1},{8,14},{9,15},{10,... | collective-permute-start | bytes 798728 | tf_op jit(solution)/shard_map/ppermute | solution.py:20
  7.5 0.6 collective-permute-start.2
  8.1 2.2 %copy-done.1 = bf16[16,8,16384]{2,1,0:T(8,128)(2,1)S(1)} copy-done((bf16[16,8,16384]{2,1,0:T(8,128)(2,1)S(1)}, bf16[16,8,16384]{2,1,0:T(8,128)(2,1)}, u32[]{:S(2)}) %copy-start.1) | copy-done | bytes 4194328
  10.3 1.0 %copy-done.3 = f32[8,16384]{1,0:T(8,128)S(1)} copy-done((f32[8,16384]{1,0:T(8,128)S(1)}, f32[8,16384]{1,0:T(8,128)}, u32[]{:S(2)}) %copy-start.3) | copy-done | bytes 524312
  11.4 0.8 copy-done.7
  12.2 2.6 %tile_sums_first.1.refs_0_ = bf16[256,128]{1,0:T(8,128)(2,1)S(1)} custom-call(f32[8,16384]{1,0:T(8,128)S(1)} %copy-done.3, f32[1,16384]{1,0:T(1,128)S(1)} %bitcast.15, bf16[16,8,16384]{2,1,0:T(8,128)(2,1)S(1)} %copy-done.1), custom_call_target="tpu_custom_call" | custom-call | tf_op jit(solution)/shard_map/tile_sums_first/pallas_call | solution.py:79
  14.8 3.8 %collective-permute-start.7 = (bf16[256,128]{1,0:T(8,128)(2,1)S(1)}, bf16[256,128]{1,0:T(8,128)(2,1)S(1)}, u32[]{:S(2)}, u32[]{:S(2)}) collective-permute-start(bf16[256,128]{1,0:T(8,128)(2,1)S(1)} %tile_sums_first.1.refs_0_), channel_id=1, source_target_pairs={{0,6},{1,7},{2,4},{3,5},{4,2},{5,3},{6,0},{7,1},{8,14},{9,15},{10,... | collective-permute-start | bytes 196616 | tf_op jit(solution)/shard_map/ppermute | solution.py:20
  18.6 0.5 broadcast.143
  19.1 0.7 reduce.3
  19.8 0.6 gather_fusion.1
  20.4 0.6 gather_fusion
  21.0 0.3 collective-permute-start.4
  21.3 10.9 %collective-permute-done.1.refs_2_ = bf16[1040,128]{1,0:T(8,128)(2,1)S(1)} collective-permute-done((bf16[1040,128]{1,0:T(8,128)(2,1)S(1)}, bf16[1040,128]{1,0:T(8,128)(2,1)S(1)}, u32[]{:S(2)}, u32[]{:S(2)}) %collective-permute-start.1) | collective-permute-done | bytes 266272 | tf_op jit(solution)/shard_map/ppermute | solution.py:20
  32.3 2.2 %collective-permute-start.8 = (bf16[256,128]{1,0:T(8,128)(2,1)S(1)}, bf16[256,128]{1,0:T(8,128)(2,1)S(1)}, u32[]{:S(2)}, u32[]{:S(2)}) collective-permute-start(bf16[256,128]{1,0:T(8,128)(2,1)S(1)} %tile_sums_first.1.refs_0_), channel_id=1, source_target_pairs={{0,4},{1,5},{2,6},{3,7},{4,0},{5,1},{6,2},{7,3},{8,12},{9,13},{10,... | collective-permute-start | bytes 196616 | tf_op jit(solution)/shard_map/ppermute | solution.py:20
  34.5 4.5 %collective-permute-done.8.refs_2_ = bf16[256,128]{1,0:T(8,128)(2,1)S(1)} collective-permute-done((bf16[256,128]{1,0:T(8,128)(2,1)S(1)}, bf16[256,128]{1,0:T(8,128)(2,1)S(1)}, u32[]{:S(2)}, u32[]{:S(2)}) %collective-permute-start.8) | collective-permute-done | bytes 65568 | tf_op jit(solution)/shard_map/ppermute | solution.py:20
  39.2 4.1 %collective-permute-done.9.refs_3_ = bf16[256,128]{1,0:T(8,128)(2,1)S(1)} collective-permute-done((bf16[256,128]{1,0:T(8,128)(2,1)S(1)}, bf16[256,128]{1,0:T(8,128)(2,1)S(1)}, u32[]{:S(2)}, u32[]{:S(2)}) %collective-permute-start.9) | collective-permute-done | bytes 65568 | tf_op jit(solution)/shard_map/ppermute | solution.py:20
  43.3 0.5 collective-permute-start.11
  43.9 0.4 collective-permute-start.13
  44.4 0.7 dynamic-slice_add_fusion
  45.1 0.3 reshape.203.target_ref
  45.4 3.8 %pair_matrix.1.matrix_ref = bf16[512,2048]{1,0:T(8,128)(2,1)S(1)} custom-call(s32[512,1]{1,0:T(8,128)S(1)} %reshape.203.target_ref, s32[1,2048]{1,0:T(1,128)S(1)} %get-tuple-element.15.tile_row_ref, s32[1,2048]{1,0:T(1,128)S(1)} %get-tuple-element.14.tile_block_ref, bf16[1040,128]{1,0:T(8,128)(2,1)S(1)} %fusion.1.refs_0_, ...), custom_call_target="tpu_custom_call" | custom-call | tf_op jit(solution)/shard_map/pair_matrix/pallas_call | solution.py:160
  49.3 7.0 %spread.2 = bf16[8,16384]{1,0:T(8,128)(2,1)S(1)} custom-call(bf16[512,2048]{1,0:T(8,128)(2,1)S(1)} %pair_matrix.1.matrix_ref, bf16[16,8,16384]{2,1,0:T(8,128)(2,1)} %ensemble_ref.7, f32[2,16384]{1,0:T(2,128)S(1)} %copy-done.6, bf16[256,128]{1,0:T(8,128)(2,1)S(1)} %tile_sums_first.1.refs_0_, bf16[256,128]{1,0:T(8,128)(2,1)S(1)} %collective-permute-done.7.refs_1_, ...), custom_call_target="tpu_custom_call" | custom-call | tf_op jit(solution)/shard_map/spread/pallas_call | solution.py:221
  56.4 1.6 %collective-permute-start.14 = (bf16[8,8192]{1,0:T(8,128)(2,1)S(1)}, bf16[8,8192]{1,0:T(8,128)(2,1)S(1)}, u32[]{:S(2)}, u32[]{:S(2)}) collective-permute-start(bf16[8,8192]{1,0:T(8,128)(2,1)S(1)} %get-tuple-element.12), channel_id=1, source_target_pairs={{0,8},{8,0},{16,24},{24,16},{1,9},{9,1},{17,25},{25,17},{2,10},{10... | collective-permute-start | bytes 393224 | tf_op jit(solution)/shard_map/ppermute | solution.py:20
  57.9 1.5 %collective-permute-start.15 = (bf16[8,8192]{1,0:T(8,128)(2,1)S(1)}, bf16[8,8192]{1,0:T(8,128)(2,1)S(1)}, u32[]{:S(2)}, u32[]{:S(2)}) collective-permute-start(bf16[8,8192]{1,0:T(8,128)(2,1)S(1)} %get-tuple-element.13), channel_id=1, source_target_pairs={{0,16},{8,24},{16,0},{24,8},{1,17},{9,25},{17,1},{25,9},{2,18},{10... | collective-permute-start | bytes 393224 | tf_op jit(solution)/shard_map/ppermute | solution.py:20
  59.4 2.5 %collective-permute-done.14 = bf16[8,8192]{1,0:T(8,128)(2,1)S(1)} collective-permute-done((bf16[8,8192]{1,0:T(8,128)(2,1)S(1)}, bf16[8,8192]{1,0:T(8,128)(2,1)S(1)}, u32[]{:S(2)}, u32[]{:S(2)}) %collective-permute-start.14) | collective-permute-done | bytes 131104 | tf_op jit(solution)/shard_map/ppermute | solution.py:20
  61.9 1.2 %collective-permute-done.15 = bf16[8,8192]{1,0:T(8,128)(2,1)S(1)} collective-permute-done((bf16[8,8192]{1,0:T(8,128)(2,1)S(1)}, bf16[8,8192]{1,0:T(8,128)(2,1)S(1)}, u32[]{:S(2)}, u32[]{:S(2)}) %collective-permute-start.15) | collective-permute-done | bytes 131104 | tf_op jit(solution)/shard_map/ppermute | solution.py:20
  63.2 1.6 %collective-permute-start.16 = (bf16[8,8192]{1,0:T(8,128)(2,1)S(1)}, bf16[8,8192]{1,0:T(8,128)(2,1)S(1)}, u32[]{:S(2)}, u32[]{:S(2)}) collective-permute-start(bf16[8,8192]{1,0:T(8,128)(2,1)S(1)} %get-tuple-element.10), channel_id=1, source_target_pairs={{0,16},{8,24},{16,0},{24,8},{1,17},{9,25},{17,1},{25,9},{2,18},{10... | collective-permute-start | bytes 393224 | tf_op jit(solution)/shard_map/ppermute | solution.py:20
  64.8 0.5 collective-permute-start.17
  65.3 2.9 %collective-permute-done.16 = bf16[8,8192]{1,0:T(8,128)(2,1)S(1)} collective-permute-done((bf16[8,8192]{1,0:T(8,128)(2,1)S(1)}, bf16[8,8192]{1,0:T(8,128)(2,1)S(1)}, u32[]{:S(2)}, u32[]{:S(2)}) %collective-permute-start.16) | collective-permute-done | bytes 131104 | tf_op jit(solution)/shard_map/ppermute | solution.py:20
  68.2 1.5 %collective-permute-done.17 = bf16[8,8192]{1,0:T(8,128)(2,1)S(1)} collective-permute-done((bf16[8,8192]{1,0:T(8,128)(2,1)S(1)}, bf16[8,8192]{1,0:T(8,128)(2,1)S(1)}, u32[]{:S(2)}, u32[]{:S(2)}) %collective-permute-start.17) | collective-permute-done | bytes 131104 | tf_op jit(solution)/shard_map/ppermute | solution.py:20
  69.8 3.6 %tile_sums_second.1 = (f32[8,16384]{1,0:T(8,128)}, bf16[256,128]{1,0:T(8,128)(2,1)S(1)}) custom-call(f32[8,16384]{1,0:T(8,128)S(1)} %copy-done.4, f32[8,16384]{1,0:T(8,128)S(1)} %copy-done.5, bf16[8,16384]{1,0:T(8,128)(2,1)S(1)} %pad_maximum_fusion.mine_ref, bf16[8,16384]{1,0:T(8,128)(2,1)S(1)} %pad_maximum_fusion.1.theirs_ref, f32[1,16384]{1,0:T(1,128)S(1)} %bitcast.16, ...), custom_call_target="tpu_custom_call" | custom-call | tf_op jit(solution)/shard_map/tile_sums_second/pallas_call | solution.py:98
  73.4 1.9 %collective-permute-start.18 = (bf16[256,128]{1,0:T(8,128)(2,1)S(1)}, bf16[256,128]{1,0:T(8,128)(2,1)S(1)}, u32[]{:S(2)}, u32[]{:S(2)}) collective-permute-start(bf16[256,128]{1,0:T(8,128)(2,1)S(1)} %get-tuple-element.5.refs_0_), channel_id=1, source_target_pairs={{0,6},{1,7},{2,4},{3,5},{4,2},{5,3},{6,0},{7,1},{8,14},{9,15},{10,... | collective-permute-start | bytes 196616 | tf_op jit(solution)/shard_map/ppermute | solution.py:20
  75.3 2.5 %collective-permute-start.20 = (bf16[256,128]{1,0:T(8,128)(2,1)S(1)}, bf16[256,128]{1,0:T(8,128)(2,1)S(1)}, u32[]{:S(2)}, u32[]{:S(2)}) collective-permute-start(bf16[256,128]{1,0:T(8,128)(2,1)S(1)} %get-tuple-element.5.refs_0_), channel_id=1, source_target_pairs={{0,2},{1,3},{2,0},{3,1},{4,6},{5,7},{6,4},{7,5},{8,10},{9,11},{10,... | collective-permute-start | bytes 196616 | tf_op jit(solution)/shard_map/ppermute | solution.py:20
  77.8 1.7 %collective-permute-done.18.refs_1_ = bf16[256,128]{1,0:T(8,128)(2,1)S(1)} collective-permute-done((bf16[256,128]{1,0:T(8,128)(2,1)S(1)}, bf16[256,128]{1,0:T(8,128)(2,1)S(1)}, u32[]{:S(2)}, u32[]{:S(2)}) %collective-permute-start.18) | collective-permute-done | bytes 65568 | tf_op jit(solution)/shard_map/ppermute | solution.py:20
  79.5 1.4 %collective-permute-done.19.refs_2_ = bf16[256,128]{1,0:T(8,128)(2,1)S(1)} collective-permute-done((bf16[256,128]{1,0:T(8,128)(2,1)S(1)}, bf16[256,128]{1,0:T(8,128)(2,1)S(1)}, u32[]{:S(2)}, u32[]{:S(2)}) %collective-permute-start.19) | collective-permute-done | bytes 65568 | tf_op jit(solution)/shard_map/ppermute | solution.py:20
  80.9 0.5 collective-permute-start.24
  81.4 0.7 collective-permute-done.23.refs_6_
  82.3 6.9 %spread.3 = bf16[8,16384]{1,0:T(8,128)(2,1)S(1)} custom-call(bf16[512,2048]{1,0:T(8,128)(2,1)S(1)} %pair_matrix.1.matrix_ref, bf16[16,8,16384]{2,1,0:T(8,128)(2,1)} %ensemble_ref.7, f32[2,16384]{1,0:T(2,128)S(1)} %copy-done.6, bf16[256,128]{1,0:T(8,128)(2,1)S(1)} %get-tuple-element.5.refs_0_, bf16[256,128]{1,0:T(8,128)(2,1)S(1)} %collective-permute-done.18.refs_1_, ...), custom_call_target="tpu_custom_call" | custom-call | tf_op jit(solution)/shard_map/spread/pallas_call | solution.py:221
  89.2 0.6 collective-permute-start.25
  89.8 0.5 collective-permute-start.26
  90.3 4.7 %collective-permute-done.25 = bf16[8,8192]{1,0:T(8,128)(2,1)S(1)} collective-permute-done((bf16[8,8192]{1,0:T(8,128)(2,1)S(1)}, bf16[8,8192]{1,0:T(8,128)(2,1)S(1)}, u32[]{:S(2)}, u32[]{:S(2)}) %collective-permute-start.25) | collective-permute-done | bytes 131104 | tf_op jit(solution)/shard_map/ppermute | solution.py:20
  95.3 0.6 collective-permute-start.27
  95.9 1.5 %collective-permute-start.28 = (bf16[8,8192]{1,0:T(8,128)(2,1)S(1)}, bf16[8,8192]{1,0:T(8,128)(2,1)S(1)}, u32[]{:S(2)}, u32[]{:S(2)}) collective-permute-start(bf16[8,8192]{1,0:T(8,128)(2,1)S(1)} %get-tuple-element.7), channel_id=1, source_target_pairs={{0,8},{8,0},{16,24},{24,16},{1,9},{9,1},{17,25},{25,17},{2,10},{10... | collective-permute-start | bytes 393224 | tf_op jit(solution)/shard_map/ppermute | solution.py:20
  97.4 3.0 %collective-permute-done.27 = bf16[8,8192]{1,0:T(8,128)(2,1)S(1)} collective-permute-done((bf16[8,8192]{1,0:T(8,128)(2,1)S(1)}, bf16[8,8192]{1,0:T(8,128)(2,1)S(1)}, u32[]{:S(2)}, u32[]{:S(2)}) %collective-permute-start.27) | collective-permute-done | bytes 131104 | tf_op jit(solution)/shard_map/ppermute | solution.py:20
  100.3 0.5 collective-permute-done.28
  100.8 0.9 multiply_add_fusion
  (68 shorter events, 1.2 us)
Async XLA Ops:
  0.6 33.9 %copy-start = (s32[2048,2]{0,1:T(2,128)S(1)}, s32[2048,2]{0,1:T(2,128)}, u32[]{:S(2)}) copy-start(s32[2048,2]{0,1:T(2,128)} %param.20) | copy-start | bytes 49156
  0.6 18.0 %copy-start.12 = (s32[8]{0:T(128)S(1)}, s32[8]{0:T(128)}, u32[]{:S(2)}) copy-start(s32[8]{0:T(128)} %constant.49.clone) | copy-start | bytes 100
  0.7 18.5 %copy-start.10 = (s32[2048,1]{0,1:T(1,128)S(1)}, s32[2048,1]{0,1:T(1,128)}, u32[]{:S(2)}) copy-start(s32[2048,1]{0,1:T(1,128)} %param.15) | copy-start | bytes 24580
  0.7 19.7 %copy-start.11 = (s32[2048]{0:T(1024)S(1)}, s32[2048]{0:T(1024)}, u32[]{:S(2)}) copy-start(s32[2048]{0:T(1024)} %param.16) | copy-start | bytes 24580
  2.4 18.7 %collective-permute-start = (bf16[1040,128]{1,0:T(8,128)(2,1)S(1)}, bf16[1040,128]{1,0:T(8,128)(2,1)S(1)}, u32[]{:S(2)}, u32[]{:S(2)}) collective-permute-start(bf16[1040,128]{1,0:T(8,128)(2,1)S(1)} %fusion.1.refs_0_), channel_id=1, source_target_pairs={{0,6},{1,7},{2,4},{3,5},{4,2},{5,3},{6,0},{7,1},{8,14},{9,15},{10,... | collective-permute-start | bytes 798728 | tf_op jit(solution)/shard_map/ppermute | solution.py:20
  7.5 24.8 %collective-permute-start.1 = (bf16[1040,128]{1,0:T(8,128)(2,1)S(1)}, bf16[1040,128]{1,0:T(8,128)(2,1)S(1)}, u32[]{:S(2)}, u32[]{:S(2)}) collective-permute-start(bf16[1040,128]{1,0:T(8,128)(2,1)S(1)} %fusion.1.refs_0_), channel_id=1, source_target_pairs={{0,4},{1,5},{2,6},{3,7},{4,0},{5,1},{6,2},{7,3},{8,12},{9,13},{10,... | collective-permute-start | bytes 798728 | tf_op jit(solution)/shard_map/ppermute | solution.py:20
  7.5 31.6 %collective-permute-start.2 = (bf16[1040,128]{1,0:T(8,128)(2,1)S(1)}, bf16[1040,128]{1,0:T(8,128)(2,1)S(1)}, u32[]{:S(2)}, u32[]{:S(2)}) collective-permute-start(bf16[1040,128]{1,0:T(8,128)(2,1)S(1)} %fusion.1.refs_0_), channel_id=1, source_target_pairs={{0,2},{1,3},{2,0},{3,1},{4,6},{5,7},{6,4},{7,5},{8,10},{9,11},{10,... | collective-permute-start | bytes 798728 | tf_op jit(solution)/shard_map/ppermute | solution.py:20
  8.1 35.2 %collective-permute-start.3 = (bf16[1040,128]{1,0:T(8,128)(2,1)S(1)}, bf16[1040,128]{1,0:T(8,128)(2,1)S(1)}, u32[]{:S(2)}, u32[]{:S(2)}) collective-permute-start(bf16[1040,128]{1,0:T(8,128)(2,1)S(1)} %fusion.1.refs_0_), channel_id=1, source_target_pairs={{0,1},{1,0},{2,3},{3,2},{4,5},{5,4},{6,7},{7,6},{8,9},{9,8},{10,11... | collective-permute-start | bytes 798728 | tf_op jit(solution)/shard_map/ppermute | solution.py:20
  8.1 2.2 %copy-start.1 = (bf16[16,8,16384]{2,1,0:T(8,128)(2,1)S(1)}, bf16[16,8,16384]{2,1,0:T(8,128)(2,1)}, u32[]{:S(2)}) copy-start(bf16[16,8,16384]{2,1,0:T(8,128)(2,1)} %ensemble_ref.7) | copy-start | bytes 12582916
  10.3 1.0 %copy-start.3 = (f32[8,16384]{1,0:T(8,128)S(1)}, f32[8,16384]{1,0:T(8,128)}, u32[]{:S(2)}) copy-start(f32[8,16384]{1,0:T(8,128)} %state_ref.3) | copy-start | bytes 1572868
  11.4 0.8 copy-start.7
  12.2 37.1 %copy-start.6 = (f32[2,16384]{1,0:T(2,128)S(1)}, f32[2,16384]{1,0:T(2,128)}, u32[]{:S(2)}) copy-start(f32[2,16384]{1,0:T(2,128)} %weight_ref.3) | copy-start | bytes 393220
  14.8 17.5 %collective-permute-start.7 = (bf16[256,128]{1,0:T(8,128)(2,1)S(1)}, bf16[256,128]{1,0:T(8,128)(2,1)S(1)}, u32[]{:S(2)}, u32[]{:S(2)}) collective-permute-start(bf16[256,128]{1,0:T(8,128)(2,1)S(1)} %tile_sums_first.1.refs_0_), channel_id=1, source_target_pairs={{0,6},{1,7},{2,4},{3,5},{4,2},{5,3},{6,0},{7,1},{8,14},{9,15},{10,... | collective-permute-start | bytes 196616 | tf_op jit(solution)/shard_map/ppermute | solution.py:20
  21.0 22.8 %collective-permute-start.4 = (bf16[1040,128]{1,0:T(8,128)(2,1)S(1)}, bf16[1040,128]{1,0:T(8,128)(2,1)S(1)}, u32[]{:S(2)}, u32[]{:S(2)}) collective-permute-start(bf16[1040,128]{1,0:T(8,128)(2,1)S(1)} %collective-permute-done.refs_1_), channel_id=1, source_target_pairs={{0,1},{1,0},{2,3},{3,2},{4,5},{5,4},{6,7},{7,6},{8,9},{9,8},{10,11... | collective-permute-start | bytes 798728 | tf_op jit(solution)/shard_map/ppermute | solution.py:20
  32.3 11.6 %collective-permute-start.5 = (bf16[1040,128]{1,0:T(8,128)(2,1)S(1)}, bf16[1040,128]{1,0:T(8,128)(2,1)S(1)}, u32[]{:S(2)}, u32[]{:S(2)}) collective-permute-start(bf16[1040,128]{1,0:T(8,128)(2,1)S(1)} %collective-permute-done.1.refs_2_), channel_id=1, source_target_pairs={{0,1},{1,0},{2,3},{3,2},{4,5},{5,4},{6,7},{7,6},{8,9},{9,8},{10,11... | collective-permute-start | bytes 798728 | tf_op jit(solution)/shard_map/ppermute | solution.py:20
  32.3 6.7 %collective-permute-start.8 = (bf16[256,128]{1,0:T(8,128)(2,1)S(1)}, bf16[256,128]{1,0:T(8,128)(2,1)S(1)}, u32[]{:S(2)}, u32[]{:S(2)}) collective-permute-start(bf16[256,128]{1,0:T(8,128)(2,1)S(1)} %tile_sums_first.1.refs_0_), channel_id=1, source_target_pairs={{0,4},{1,5},{2,6},{3,7},{4,0},{5,1},{6,2},{7,3},{8,12},{9,13},{10,... | collective-permute-start | bytes 196616 | tf_op jit(solution)/shard_map/ppermute | solution.py:20
  39.1 4.3 %collective-permute-start.9 = (bf16[256,128]{1,0:T(8,128)(2,1)S(1)}, bf16[256,128]{1,0:T(8,128)(2,1)S(1)}, u32[]{:S(2)}, u32[]{:S(2)}) collective-permute-start(bf16[256,128]{1,0:T(8,128)(2,1)S(1)} %tile_sums_first.1.refs_0_), channel_id=1, source_target_pairs={{0,2},{1,3},{2,0},{3,1},{4,6},{5,7},{6,4},{7,5},{8,10},{9,11},{10,... | collective-permute-start | bytes 196616 | tf_op jit(solution)/shard_map/ppermute | solution.py:20
  39.1 6.3 %collective-permute-start.6 = (bf16[1040,128]{1,0:T(8,128)(2,1)S(1)}, bf16[1040,128]{1,0:T(8,128)(2,1)S(1)}, u32[]{:S(2)}, u32[]{:S(2)}) collective-permute-start(bf16[1040,128]{1,0:T(8,128)(2,1)S(1)} %collective-permute-done.2.refs_3_), channel_id=1, source_target_pairs={{0,1},{1,0},{2,3},{3,2},{4,5},{5,4},{6,7},{7,6},{8,9},{9,8},{10,11... | collective-permute-start | bytes 798728 | tf_op jit(solution)/shard_map/ppermute | solution.py:20
  43.3 5.9 %collective-permute-start.10 = (bf16[256,128]{1,0:T(8,128)(2,1)S(1)}, bf16[256,128]{1,0:T(8,128)(2,1)S(1)}, u32[]{:S(2)}, u32[]{:S(2)}) collective-permute-start(bf16[256,128]{1,0:T(8,128)(2,1)S(1)} %tile_sums_first.1.refs_0_), channel_id=1, source_target_pairs={{0,1},{1,0},{2,3},{3,2},{4,5},{5,4},{6,7},{7,6},{8,9},{9,8},{10,11... | collective-permute-start | bytes 196616 | tf_op jit(solution)/shard_map/ppermute | solution.py:20
  43.3 5.9 %collective-permute-start.11 = (bf16[256,128]{1,0:T(8,128)(2,1)S(1)}, bf16[256,128]{1,0:T(8,128)(2,1)S(1)}, u32[]{:S(2)}, u32[]{:S(2)}) collective-permute-start(bf16[256,128]{1,0:T(8,128)(2,1)S(1)} %collective-permute-done.7.refs_1_), channel_id=1, source_target_pairs={{0,1},{1,0},{2,3},{3,2},{4,5},{5,4},{6,7},{7,6},{8,9},{9,8},{10,11... | collective-permute-start | bytes 196616 | tf_op jit(solution)/shard_map/ppermute | solution.py:20
  43.8 5.4 %collective-permute-start.12 = (bf16[256,128]{1,0:T(8,128)(2,1)S(1)}, bf16[256,128]{1,0:T(8,128)(2,1)S(1)}, u32[]{:S(2)}, u32[]{:S(2)}) collective-permute-start(bf16[256,128]{1,0:T(8,128)(2,1)S(1)} %collective-permute-done.8.refs_2_), channel_id=1, source_target_pairs={{0,1},{1,0},{2,3},{3,2},{4,5},{5,4},{6,7},{7,6},{8,9},{9,8},{10,11... | collective-permute-start | bytes 196616 | tf_op jit(solution)/shard_map/ppermute | solution.py:20
  43.9 5.4 %collective-permute-start.13 = (bf16[256,128]{1,0:T(8,128)(2,1)S(1)}, bf16[256,128]{1,0:T(8,128)(2,1)S(1)}, u32[]{:S(2)}, u32[]{:S(2)}) collective-permute-start(bf16[256,128]{1,0:T(8,128)(2,1)S(1)} %collective-permute-done.9.refs_3_), channel_id=1, source_target_pairs={{0,1},{1,0},{2,3},{3,2},{4,5},{5,4},{6,7},{7,6},{8,9},{9,8},{10,11... | collective-permute-start | bytes 196616 | tf_op jit(solution)/shard_map/ppermute | solution.py:20
  49.2 20.5 %copy-start.2 = (bf16[16,8,16384]{2,1,0:T(8,128)(2,1)S(1)}, bf16[16,8,16384]{2,1,0:T(8,128)(2,1)}, u32[]{:S(2)}) copy-start(bf16[16,8,16384]{2,1,0:T(8,128)(2,1)} %ensemble_ref.7) | copy-start | bytes 12582916
  49.2 20.5 %copy-start.4 = (f32[8,16384]{1,0:T(8,128)S(1)}, f32[8,16384]{1,0:T(8,128)}, u32[]{:S(2)}) copy-start(f32[8,16384]{1,0:T(8,128)} %state_ref.3) | copy-start | bytes 1572868
  49.2 20.5 %copy-start.5 = (f32[8,16384]{1,0:T(8,128)S(1)}, f32[8,16384]{1,0:T(8,128)}, u32[]{:S(2)}) copy-start(f32[8,16384]{1,0:T(8,128)} %climate_ref.1) | copy-start | bytes 1572868
  49.2 20.5 %copy-start.8 = (f32[16384]{0:T(1024)S(1)}, f32[16384]{0:T(1024)}, u32[]{:S(2)}) copy-start(f32[16384]{0:T(1024)} %param.17) | copy-start | bytes 196612
  56.4 5.5 %collective-permute-start.14 = (bf16[8,8192]{1,0:T(8,128)(2,1)S(1)}, bf16[8,8192]{1,0:T(8,128)(2,1)S(1)}, u32[]{:S(2)}, u32[]{:S(2)}) collective-permute-start(bf16[8,8192]{1,0:T(8,128)(2,1)S(1)} %get-tuple-element.12), channel_id=1, source_target_pairs={{0,8},{8,0},{16,24},{24,16},{1,9},{9,1},{17,25},{25,17},{2,10},{10... | collective-permute-start | bytes 393224 | tf_op jit(solution)/shard_map/ppermute | solution.py:20
  57.9 5.2 %collective-permute-start.15 = (bf16[8,8192]{1,0:T(8,128)(2,1)S(1)}, bf16[8,8192]{1,0:T(8,128)(2,1)S(1)}, u32[]{:S(2)}, u32[]{:S(2)}) collective-permute-start(bf16[8,8192]{1,0:T(8,128)(2,1)S(1)} %get-tuple-element.13), channel_id=1, source_target_pairs={{0,16},{8,24},{16,0},{24,8},{1,17},{9,25},{17,1},{25,9},{2,18},{10... | collective-permute-start | bytes 393224 | tf_op jit(solution)/shard_map/ppermute | solution.py:20
  63.2 5.0 %collective-permute-start.16 = (bf16[8,8192]{1,0:T(8,128)(2,1)S(1)}, bf16[8,8192]{1,0:T(8,128)(2,1)S(1)}, u32[]{:S(2)}, u32[]{:S(2)}) collective-permute-start(bf16[8,8192]{1,0:T(8,128)(2,1)S(1)} %get-tuple-element.10), channel_id=1, source_target_pairs={{0,16},{8,24},{16,0},{24,8},{1,17},{9,25},{17,1},{25,9},{2,18},{10... | collective-permute-start | bytes 393224 | tf_op jit(solution)/shard_map/ppermute | solution.py:20
  64.8 5.0 %collective-permute-start.17 = (bf16[8,8192]{1,0:T(8,128)(2,1)S(1)}, bf16[8,8192]{1,0:T(8,128)(2,1)S(1)}, u32[]{:S(2)}, u32[]{:S(2)}) collective-permute-start(bf16[8,8192]{1,0:T(8,128)(2,1)S(1)} %get-tuple-element.11), channel_id=1, source_target_pairs={{0,8},{8,0},{16,24},{24,16},{1,9},{9,1},{17,25},{25,17},{2,10},{10... | collective-permute-start | bytes 393224 | tf_op jit(solution)/shard_map/ppermute | solution.py:20
  73.4 27.5 %copy-start.9 = (f32[8,16384]{1,0:T(8,128)S(1)}, f32[8,16384]{1,0:T(8,128)}, u32[]{:S(2)}) copy-start(f32[8,16384]{1,0:T(8,128)} %get-tuple-element.2) | copy-start | bytes 1572868
  73.4 6.1 %collective-permute-start.18 = (bf16[256,128]{1,0:T(8,128)(2,1)S(1)}, bf16[256,128]{1,0:T(8,128)(2,1)S(1)}, u32[]{:S(2)}, u32[]{:S(2)}) collective-permute-start(bf16[256,128]{1,0:T(8,128)(2,1)S(1)} %get-tuple-element.5.refs_0_), channel_id=1, source_target_pairs={{0,6},{1,7},{2,4},{3,5},{4,2},{5,3},{6,0},{7,1},{8,14},{9,15},{10,... | collective-permute-start | bytes 196616 | tf_op jit(solution)/shard_map/ppermute | solution.py:20
  75.3 5.5 %collective-permute-start.19 = (bf16[256,128]{1,0:T(8,128)(2,1)S(1)}, bf16[256,128]{1,0:T(8,128)(2,1)S(1)}, u32[]{:S(2)}, u32[]{:S(2)}) collective-permute-start(bf16[256,128]{1,0:T(8,128)(2,1)S(1)} %get-tuple-element.5.refs_0_), channel_id=1, source_target_pairs={{0,4},{1,5},{2,6},{3,7},{4,0},{5,1},{6,2},{7,3},{8,12},{9,13},{10,... | collective-permute-start | bytes 196616 | tf_op jit(solution)/shard_map/ppermute | solution.py:20
  75.3 5.5 %collective-permute-start.20 = (bf16[256,128]{1,0:T(8,128)(2,1)S(1)}, bf16[256,128]{1,0:T(8,128)(2,1)S(1)}, u32[]{:S(2)}, u32[]{:S(2)}) collective-permute-start(bf16[256,128]{1,0:T(8,128)(2,1)S(1)} %get-tuple-element.5.refs_0_), channel_id=1, source_target_pairs={{0,2},{1,3},{2,0},{3,1},{4,6},{5,7},{6,4},{7,5},{8,10},{9,11},{10,... | collective-permute-start | bytes 196616 | tf_op jit(solution)/shard_map/ppermute | solution.py:20
  77.8 3.6 %collective-permute-start.21 = (bf16[256,128]{1,0:T(8,128)(2,1)S(1)}, bf16[256,128]{1,0:T(8,128)(2,1)S(1)}, u32[]{:S(2)}, u32[]{:S(2)}) collective-permute-start(bf16[256,128]{1,0:T(8,128)(2,1)S(1)} %get-tuple-element.5.refs_0_), channel_id=1, source_target_pairs={{0,1},{1,0},{2,3},{3,2},{4,5},{5,4},{6,7},{7,6},{8,9},{9,8},{10,11... | collective-permute-start | bytes 196616 | tf_op jit(solution)/shard_map/ppermute | solution.py:20
  79.5 1.9 %collective-permute-start.22 = (bf16[256,128]{1,0:T(8,128)(2,1)S(1)}, bf16[256,128]{1,0:T(8,128)(2,1)S(1)}, u32[]{:S(2)}, u32[]{:S(2)}) collective-permute-start(bf16[256,128]{1,0:T(8,128)(2,1)S(1)} %collective-permute-done.18.refs_1_), channel_id=1, source_target_pairs={{0,1},{1,0},{2,3},{3,2},{4,5},{5,4},{6,7},{7,6},{8,9},{9,8},{10,11... | collective-permute-start | bytes 196616 | tf_op jit(solution)/shard_map/ppermute | solution.py:20
  80.9 1.3 %collective-permute-start.23 = (bf16[256,128]{1,0:T(8,128)(2,1)S(1)}, bf16[256,128]{1,0:T(8,128)(2,1)S(1)}, u32[]{:S(2)}, u32[]{:S(2)}) collective-permute-start(bf16[256,128]{1,0:T(8,128)(2,1)S(1)} %collective-permute-done.19.refs_2_), channel_id=1, source_target_pairs={{0,1},{1,0},{2,3},{3,2},{4,5},{5,4},{6,7},{7,6},{8,9},{9,8},{10,11... | collective-permute-start | bytes 196616 | tf_op jit(solution)/shard_map/ppermute | solution.py:20
  80.9 1.4 %collective-permute-start.24 = (bf16[256,128]{1,0:T(8,128)(2,1)S(1)}, bf16[256,128]{1,0:T(8,128)(2,1)S(1)}, u32[]{:S(2)}, u32[]{:S(2)}) collective-permute-start(bf16[256,128]{1,0:T(8,128)(2,1)S(1)} %collective-permute-done.20.refs_3_), channel_id=1, source_target_pairs={{0,1},{1,0},{2,3},{3,2},{4,5},{5,4},{6,7},{7,6},{8,9},{9,8},{10,11... | collective-permute-start | bytes 196616 | tf_op jit(solution)/shard_map/ppermute | solution.py:20
  89.2 5.8 %collective-permute-start.25 = (bf16[8,8192]{1,0:T(8,128)(2,1)S(1)}, bf16[8,8192]{1,0:T(8,128)(2,1)S(1)}, u32[]{:S(2)}, u32[]{:S(2)}) collective-permute-start(bf16[8,8192]{1,0:T(8,128)(2,1)S(1)} %get-tuple-element.8), channel_id=1, source_target_pairs={{0,8},{8,0},{16,24},{24,16},{1,9},{9,1},{17,25},{25,17},{2,10},{10... | collective-permute-start | bytes 393224 | tf_op jit(solution)/shard_map/ppermute | solution.py:20
  89.8 5.5 %collective-permute-start.26 = (bf16[8,8192]{1,0:T(8,128)(2,1)S(1)}, bf16[8,8192]{1,0:T(8,128)(2,1)S(1)}, u32[]{:S(2)}, u32[]{:S(2)}) collective-permute-start(bf16[8,8192]{1,0:T(8,128)(2,1)S(1)} %get-tuple-element.9), channel_id=1, source_target_pairs={{0,16},{8,24},{16,0},{24,8},{1,17},{9,25},{17,1},{25,9},{2,18},{10... | collective-permute-start | bytes 393224 | tf_op jit(solution)/shard_map/ppermute | solution.py:20
  95.3 5.0 %collective-permute-start.27 = (bf16[8,8192]{1,0:T(8,128)(2,1)S(1)}, bf16[8,8192]{1,0:T(8,128)(2,1)S(1)}, u32[]{:S(2)}, u32[]{:S(2)}) collective-permute-start(bf16[8,8192]{1,0:T(8,128)(2,1)S(1)} %get-tuple-element.6), channel_id=1, source_target_pairs={{0,16},{8,24},{16,0},{24,8},{1,17},{9,25},{17,1},{25,9},{2,18},{10... | collective-permute-start | bytes 393224 | tf_op jit(solution)/shard_map/ppermute | solution.py:20
  95.9 5.0 %collective-permute-start.28 = (bf16[8,8192]{1,0:T(8,128)(2,1)S(1)}, bf16[8,8192]{1,0:T(8,128)(2,1)S(1)}, u32[]{:S(2)}, u32[]{:S(2)}) collective-permute-start(bf16[8,8192]{1,0:T(8,128)(2,1)S(1)} %get-tuple-element.7), channel_id=1, source_target_pairs={{0,8},{8,0},{16,24},{24,16},{1,9},{9,1},{17,25},{25,17},{2,10},{10... | collective-permute-start | bytes 393224 | tf_op jit(solution)/shard_map/ppermute | solution.py:20

commit v2 on v1

v2 whole, which is shorter than its diff:
```python
import functools

import jax
import jax.numpy as jnp
from jax import lax
from jax.experimental import pallas as pl
from jax.experimental.pallas import tpu as pltpu
from jax.sharding import PartitionSpec as P

TILE = 64
LANES = 128
VMEM_BYTES = 16 * 1024 * 1024
HALF = jnp.bfloat16
FULL = jnp.float32


def swap(array, axis, mask):
    size = lax.axis_size(axis)
    return lax.ppermute(array, axis, [(i, i ^ mask) for i in range(size)])


def gather_slots(array):
    size = lax.axis_size("col")
    myself = lax.axis_index("col")
    if size == 8:
        same_core = [array] + [swap(array, "col", mask) for mask in (6, 4, 2)]
        other_core = [swap(piece, "col", 1) for piece in same_core]
        masks = jnp.array([0, 6, 4, 2, 1, 7, 5, 3], jnp.int32)
        return same_core + other_core, masks ^ myself
    stacked = lax.all_gather(array, "col")
    return [stacked[i] for i in range(size)], jnp.arange(size, dtype=jnp.int32)


def tile_indicator(tiles, columns):
    tile = lax.broadcasted_iota(jnp.int32, (tiles, columns), 0)
    column = lax.broadcasted_iota(jnp.int32, (tiles, columns), 1)
    return (column >= tile * TILE) & (column < tile * TILE + TILE)


def ones_where(mask):
    return jnp.where(mask, 1.0, 0.0).astype(HALF)


def tile_sums(weighted, ensemble):
    members, levels, width = ensemble.shape
    product = ensemble.astype(FULL) * weighted[None]
    product = product.reshape(members * levels, width).astype(HALF)
    return lax.dot_general(
        ones_where(tile_indicator(width // TILE, width)),
        product,
        (((1,), (1,)), ((), ())),
        preferred_element_type=FULL,
    ).astype(HALF)


def whole(count):
    return [pl.BlockSpec(memory_space=pltpu.VMEM)] * count


def params():
    return pltpu.CompilerParams(vmem_limit_bytes=VMEM_BYTES)


def column_sizes(ensemble):
    members, levels, fine = ensemble.shape
    width = min(fine, LANES // 4 * TILE)
    return members, levels, fine, width, fine // width


def first_kernel(
    width, state_hbm, weight_hbm, ensemble_hbm, ensemble_ref, partial_ref, state_ref, weight_ref, sems
):
    fine = state_hbm.shape[1]
    tiles = width // TILE
    steps = fine // width
    copies = []
    for i in range(steps):
        span = pl.ds(i * width, width)
        copies.append(
            [
                pltpu.make_async_copy(source.at[:, span], target.at[:, span], sems.at[i, j])
                for j, (source, target) in enumerate(
                    [(state_hbm, state_ref), (weight_hbm, weight_ref)]
                )
            ]
            + [
                pltpu.make_async_copy(
                    ensemble_hbm.at[:, :, span], ensemble_ref.at[:, :, span], sems.at[i, 2]
                )
            ]
        )
    for group in copies:
        for copy in group:
            copy.start()
    for i, group in enumerate(copies):
        for copy in group:
            copy.wait()
        span = pl.ds(i * width, width)
        weighted = state_ref[:, span] * weight_ref[:, span]
        partial_ref[pl.ds(i * tiles, tiles), :] = tile_sums(weighted, ensemble_ref[:, :, span])


def run_first(state, weight, ensemble):
    members, levels, fine, width, steps = column_sizes(ensemble)
    return pl.pallas_call(
        functools.partial(first_kernel, width),
        in_specs=[pl.BlockSpec(memory_space=pltpu.HBM)] * 3,
        out_specs=whole(2),
        out_shape=[
            jax.ShapeDtypeStruct(ensemble.shape, ensemble.dtype),
            jax.ShapeDtypeStruct((fine // TILE, members * levels), HALF),
        ],
        scratch_shapes=[
            pltpu.VMEM((levels, fine), FULL),
            pltpu.VMEM((1, fine), FULL),
            pltpu.SemaphoreType.DMA((steps, 3)),
        ],
        compiler_params=params(),
        name="tile_sums_first",
    )(state, weight, ensemble)


def second_kernel(
    width,
    scale,
    state_ref,
    climate_ref,
    mine_ref,
    theirs_ref,
    weight_ref,
    ensemble_ref,
    state_out,
    partial_ref,
):
    tiles = width // TILE

    def step(i, carry):
        span = pl.ds(pl.multiple_of(i * width, width), width)
        total = mine_ref[:, span].astype(FULL) + theirs_ref[:, span].astype(FULL)
        state = climate_ref[:, span] * state_ref[:, span] + total * scale
        state_out[:, span] = state
        rows = pl.ds(pl.multiple_of(i * tiles, tiles), tiles)
        partial_ref[rows, :] = tile_sums(state * weight_ref[:, span], ensemble_ref[:, :, span])
        return carry

    lax.fori_loop(0, state_ref.shape[1] // width, step, 0)


def run_second(scale, state, climate, mine, theirs, weight, ensemble):
    members, levels, fine, width, steps = column_sizes(ensemble)
    return pl.pallas_call(
        functools.partial(second_kernel, width, scale),
        in_specs=whole(6),
        out_specs=whole(2),
        out_shape=[
            jax.ShapeDtypeStruct((levels, fine), FULL),
            jax.ShapeDtypeStruct((fine // TILE, members * levels), HALF),
        ],
        compiler_params=params(),
        name="tile_sums_second",
    )(state, climate, mine, theirs, weight, ensemble)


def tables_kernel(tile_node_ref, near_node_ref, target_ref, conv_ref, matrix_ref, select_ref):
    blocks, neigh, size, _ = conv_ref.shape
    nodes = blocks * size
    rows = [
        jnp.concatenate([conv_ref[b, k] for k in range(neigh)], axis=1) for b in range(blocks)
    ]

    def step(s, carry):
        span = pl.ds(pl.multiple_of(s * nodes, nodes), nodes)
        tile_node = tile_node_ref[:, span]
        for b in range(blocks):
            place = ones_where(near_node_ref[b] == tile_node)
            matrix_ref[pl.ds(b * size, size), span] = jnp.dot(
                rows[b], place, preferred_element_type=FULL
            ).astype(HALF)
        node = lax.broadcasted_iota(jnp.int32, (target_ref.shape[0], nodes), 1) + s * nodes
        select_ref[:, span] = ones_where(node == target_ref[...])
        return carry

    lax.fori_loop(0, tile_node_ref.shape[1] // nodes, step, 0)


def run_tables(tile_node, near_node, target, conv_blocks):
    blocks, neigh, size, _ = conv_blocks.shape
    total = tile_node.shape[1]
    return pl.pallas_call(
        tables_kernel,
        in_specs=whole(4),
        out_specs=whole(2),
        out_shape=[
            jax.ShapeDtypeStruct((blocks * size, total), HALF),
            jax.ShapeDtypeStruct((target.shape[0], total), HALF),
        ],
        compiler_params=params(),
        name="tables",
    )(tile_node, near_node, target, conv_blocks)


def slot_product(matrix_ref, piece_refs):
    span = piece_refs[0].shape[0]
    total = jnp.zeros((matrix_ref.shape[0], piece_refs[0].shape[1]), FULL)
    for s, piece in enumerate(piece_refs):
        total = total + jnp.dot(
            matrix_ref[:, s * span : (s + 1) * span], piece[...], preferred_element_type=FULL
        )
    return total


def nodes_kernel(matrix_ref, *refs):
    refs[-1][...] = slot_product(matrix_ref, refs[:-1]).astype(HALF)


def run_nodes(matrix, partial_all):
    return pl.pallas_call(
        nodes_kernel,
        in_specs=whole(1 + len(partial_all)),
        out_specs=whole(1)[0],
        out_shape=jax.ShapeDtypeStruct((matrix.shape[0], partial_all[0].shape[1]), HALF),
        compiler_params=params(),
        name="nodes",
    )(matrix, *partial_all)


def spread_kernel(width, slots, select_ref, ensemble_ref, weight_ref, *refs):
    node_refs, out_ref, values_ref = refs[:slots], refs[slots], refs[slots + 1]
    members, levels, fine = ensemble_ref.shape
    tiles = width // TILE
    feature = members * levels
    pairs = select_ref.shape[0]
    values = slot_product(select_ref, node_refs).T
    half = 2 * tiles
    lane = lax.broadcasted_iota(jnp.int32, (feature, 2 * half), 1)
    for i in range(pairs // half):
        two = values[:, i // 2 * 2 * half : (i // 2 + 1) * 2 * half]
        turned = pltpu.roll(two, half, 1)
        keep = (lane < half) if i % 2 == 0 else (lane >= half)
        values_ref[i] = jnp.where(keep, two, turned).astype(HALF)
    piece = 2 * LANES

    def step(i, carry):
        start = pl.multiple_of(i * width, width)
        inside = tile_indicator(tiles, width)
        weight = weight_ref[:, pl.ds(start, width)]
        high = weight.astype(HALF).astype(FULL)
        low = weight - high
        weights = jnp.concatenate(
            [
                jnp.where(inside, part[k : k + 1, :], 0.0).astype(HALF)
                for part in (high, low)
                for k in range(2)
            ],
            axis=0,
        )
        left = values_ref[i]
        for c in range(0, width, piece):
            field = jnp.dot(left, weights[:, c : c + piece], preferred_element_type=FULL)
            field = field.reshape(members, levels, piece)
            span = pl.ds(pl.multiple_of(start + c, piece), piece)
            terms = ensemble_ref[:, :, span].astype(FULL) * field
            out_ref[:, span] = jnp.sum(terms, axis=0).astype(HALF)
        return carry

    lax.fori_loop(0, fine // width, step, 0)


def run_spread(select, ensemble, interp_weight, nodes_all):
    members, levels, fine, width, steps = column_sizes(ensemble)
    slots = len(nodes_all)
    return pl.pallas_call(
        functools.partial(spread_kernel, width, slots),
        in_specs=whole(3 + slots),
        out_specs=whole(1)[0],
        out_shape=jax.ShapeDtypeStruct((levels, fine), HALF),
        scratch_shapes=[pltpu.VMEM((steps, members * levels, LANES), HALF)],
        compiler_params=params(),
        name="spread",
    )(select, ensemble, interp_weight, *nodes_all)


def add_half(one, two):
    return (one.astype(FULL) + two.astype(FULL)).astype(HALF)


def member_sum(local):
    size = lax.axis_size("mem")
    masks = [1 << i for i in range(size.bit_length() - 1)]
    middle = local.shape[1] // 2
    halves = [local[:, :middle], local[:, middle:]]
    orders = [masks, masks[::-1]]
    for step in range(len(masks) - 1):
        moved = [swap(part, "mem", order[step]) for part, order in zip(halves, orders)]
        halves = [add_half(part, other) for part, other in zip(halves, moved)]
    moved = [swap(part, "mem", order[-1]) for part, order in zip(halves, orders)]
    return jnp.concatenate(halves, axis=1), jnp.concatenate(moved, axis=1)


def per_device(
    increment,
    ensemble,
    climate,
    restrict_dest,
    restrict_local,
    restrict_weight,
    conv_blocks,
    neighbours,
    interp_dest,
    interp_local,
    interp_weight,
):
    col_count = lax.axis_size("col")
    myself = lax.axis_index("col")
    members, levels, fine, width, steps = column_sizes(ensemble)
    coarse_local = fine // TILE
    blocks, neigh = neighbours.shape
    node_block = coarse_local // blocks
    scale = 1.0 / (members * lax.axis_size("mem") - 1)
    weight = restrict_weight[None, :]

    ensemble, partial = run_first(increment, weight, ensemble)
    partial_all, sources = gather_slots(partial)

    owner = lax.dynamic_slice_in_dim(interp_dest, myself * coarse_local, coarse_local, 0)
    local = lax.dynamic_slice_in_dim(interp_local, myself * coarse_local, coarse_local, 0)
    slot = jnp.sum(
        jnp.where(owner[:, :, None] == sources[None, None, :], jnp.arange(col_count)[None, None, :], 0),
        axis=2,
    )
    target = slot * coarse_local + local
    target = target.reshape(steps, width // TILE, 2).transpose(0, 2, 1).reshape(-1, 1)
    node_all = restrict_dest[:, 0] * coarse_local + restrict_local
    tile_node = node_all.reshape(col_count, coarse_local)[sources].reshape(1, -1)
    near_node = neighbours[:, :, None] * node_block + jnp.arange(node_block, dtype=jnp.int32)
    near_node = near_node.reshape(blocks, neigh * node_block, 1)
    matrix, select = run_tables(tile_node, near_node, target, conv_blocks)

    nodes_all, _ = gather_slots(run_nodes(matrix, partial_all))
    mine, theirs = member_sum(run_spread(select, ensemble, interp_weight, nodes_all))
    once_applied, partial = run_second(scale, increment, climate, mine, theirs, weight, ensemble)
    partial_all, _ = gather_slots(partial)
    nodes_all, _ = gather_slots(run_nodes(matrix, partial_all))
    mine, theirs = member_sum(run_spread(select, ensemble, interp_weight, nodes_all))
    total = mine.astype(FULL) + theirs.astype(FULL)
    return once_applied, climate * once_applied + total * scale


def solution(mesh):
    in_specs = (
        P(None, "col"),
        P("mem", None, "col"),
        P(None, "col"),
        P(),
        P(),
        P("col"),
        P("col", None, None, None),
        P("col", None),
        P(),
        P(),
        P(None, "col"),
    )
    out_specs = (P(None, "col"), P(None, "col"))
    return jax.shard_map(
        per_device, mesh=mesh, in_specs=in_specs, out_specs=out_specs, check_vma=False
    )
```

time: 102 us -> 97.5 us (0.956)
  Pallas kernels: 23.9 us -> 17.8 us
  local copies, waits for them, and re-layouts: 6.18 us -> 9.7 us
  starting transfers between devices: 26.4 us -> 29.3 us
  waiting for transfers between devices: 40.1 us -> 37.4 us
  other arithmetic: 4.25 us -> 1.99 us
    pallas_call x5 -> x7, Pallas kernels: 23.9 us -> 17.8 us  [the longest x2 6.82 us: run_spread(): pl.pallas_call(functools.partial(spread_kernel, width, slots), in_specs=w...]
    unnamed x29 -> x35, local copies, waits for them, and re-layouts: 4.66 us -> 8.31 us
    ppermute x29 -> x36, starting transfers between devices: 26.4 us -> 29.3 us  [swap(): return lax.ppermute(array, axis, [(i, i ^ mask) for i in range(size)])]
    ppermute x29 -> x36, waiting for transfers between devices: 40.1 us -> 37.4 us  [swap(): return lax.ppermute(array, axis, [(i, i ^ mask) for i in range(size)])]
  transfers between devices with their start and end apart: 29 -> 36, of which waited for: 15 -> 21; matrix products, arithmetic and copies ran while one was open for 3% -> 2% of each run, Pallas kernels for 6% -> 3%
where the time goes in v2:
time: 97.5 us; the launch traced here: 97.2 us
  waiting for transfers between devices  37.4 us (38%)
  starting transfers between devices  29.3 us (30%)
  Pallas kernels  17.8 us (18%)
  local copies, waits for them, and re-layouts  9.7 us (10%)
  other arithmetic  1.99 us (2%)
  between operations  1.02 us (1%)
    ppermute x36, waiting for transfers between devices, swap(): return lax.ppermute(array, axis, [(i, i ^ mask) for i in range(size)])  37.4 us
    ppermute x36, starting transfers between devices, swap(): return lax.ppermute(array, axis, [(i, i ^ mask) for i in range(size)])  29.3 us
    unnamed x35, local copies, waits for them, and re-layouts  8.31 us
    pallas_call x2, Pallas kernels, run_spread(): pl.pallas_call(functools.partial(spread_kernel, width, slots), in_specs=w...  6.82 us
    pallas_call x1, Pallas kernels, run_first(): pl.pallas_call(functools.partial(first_kernel, width), in_specs=[pl.Block...  4.46 us
    pallas_call x1, Pallas kernels, run_tables(): pl.pallas_call(tables_kernel, in_specs=whole(4), out_specs=whole(2), out_...  2.85 us
    pallas_call x1, Pallas kernels, run_second(): pl.pallas_call(functools.partial(second_kernel, width, scale), in_specs=w...  2.81 us
  transfers between devices with their start and end apart: 36, of which 21 were waited for; matrix products, arithmetic and copies ran while one was open for 2% of the time, Pallas kernels for 3%

profile of v2, /device:TPU:0, one launch (start us, length us, event | category | flops | bytes accessed | tf_op | source)
XLA Modules:
  0.0 97.2 jit_solution(2568473480690769270)
XLA Ops:
  0.7 2.2 %copy-done.4 = bf16[16,8,16384]{2,1,0:T(8,128)(2,1)S(1)} copy-done((bf16[16,8,16384]{2,1,0:T(8,128)(2,1)S(1)}, bf16[16,8,16384]{2,1,0:T(8,128)(2,1)}, u32[]{:S(2)}) %copy-start.4) | copy-done | bytes 4194328
  2.9 1.0 %copy-done.5 = f32[8,16384]{1,0:T(8,128)S(1)} copy-done((f32[8,16384]{1,0:T(8,128)S(1)}, f32[8,16384]{1,0:T(8,128)}, u32[]{:S(2)}) %copy-start.5) | copy-done | bytes 524312
  3.9 0.8 copy-done.9
  4.8 4.5 %tile_sums_first.1 = (bf16[16,8,16384]{2,1,0:T(8,128)(2,1)S(1)}, bf16[256,128]{1,0:T(8,128)(2,1)S(1)}) custom-call(f32[8,16384]{1,0:T(8,128)S(1)} %copy-done.5, f32[1,16384]{1,0:T(1,128)S(1)} %bitcast.12, bf16[16,8,16384]{2,1,0:T(8,128)(2,1)S(1)} %copy-done.4), custom_call_target="tpu_custom_call" | custom-call | tf_op jit(solution)/shard_map/tile_sums_first/pallas_call | solution.py:105
  9.2 2.0 %copy-done.1 = bf16[16,8,16384]{2,1,0:T(8,128)(2,1)} copy-done((bf16[16,8,16384]{2,1,0:T(8,128)(2,1)}, bf16[16,8,16384]{2,1,0:T(8,128)(2,1)S(1)}, u32[]{:S(2)}) %copy-start.1) | copy-done | bytes 4194328
  11.7 2.6 %collective-permute-start.2 = (bf16[256,128]{1,0:T(8,128)(2,1)S(1)}, bf16[256,128]{1,0:T(8,128)(2,1)S(1)}, u32[]{:S(2)}, u32[]{:S(2)}) collective-permute-start(bf16[256,128]{1,0:T(8,128)(2,1)S(1)} %get-tuple-element.11.refs_0_), channel_id=1, source_target_pairs={{0,2},{1,3},{2,0},{3,1},{4,6},{5,7},{6,4},{7,5},{8,10},{9,11},{10,... | collective-permute-start | bytes 196616 | tf_op jit(solution)/shard_map/ppermute | solution.py:19
  14.3 2.6 %collective-permute-start.1 = (bf16[256,128]{1,0:T(8,128)(2,1)S(1)}, bf16[256,128]{1,0:T(8,128)(2,1)S(1)}, u32[]{:S(2)}, u32[]{:S(2)}) collective-permute-start(bf16[256,128]{1,0:T(8,128)(2,1)S(1)} %get-tuple-element.11.refs_0_), channel_id=1, source_target_pairs={{0,4},{1,5},{2,6},{3,7},{4,0},{5,1},{6,2},{7,3},{8,12},{9,13},{10,... | collective-permute-start | bytes 196616 | tf_op jit(solution)/shard_map/ppermute | solution.py:19
  17.6 0.7 dynamic-slice_add_fusion
  18.5 2.8 %collective-permute-done.1.refs_2_ = bf16[256,128]{1,0:T(8,128)(2,1)S(1)} collective-permute-done((bf16[256,128]{1,0:T(8,128)(2,1)S(1)}, bf16[256,128]{1,0:T(8,128)(2,1)S(1)}, u32[]{:S(2)}, u32[]{:S(2)}) %collective-permute-start.1) | collective-permute-done | bytes 65568 | tf_op jit(solution)/shard_map/ppermute | solution.py:19
  21.3 1.7 %collective-permute-done.refs_1_ = bf16[256,128]{1,0:T(8,128)(2,1)S(1)} collective-permute-done((bf16[256,128]{1,0:T(8,128)(2,1)S(1)}, bf16[256,128]{1,0:T(8,128)(2,1)S(1)}, u32[]{:S(2)}, u32[]{:S(2)}) %collective-permute-start) | collective-permute-done | bytes 65568 | tf_op jit(solution)/shard_map/ppermute | solution.py:19
  22.9 0.6 gather_fusion
  23.8 2.8 %tables.1 = (bf16[256,2048]{1,0:T(8,128)(2,1)S(1)}, bf16[512,2048]{1,0:T(8,128)(2,1)S(1)}) custom-call(s32[1,2048]{1,0:T(1,128)S(1)} %bitcast.14, s32[2,512,1]{2,1,0:T(8,128)S(1)} %broadcast_add_fusion.near_node_ref, s32[512,1]{1,0:T(8,128)S(1)} %reshape.70.target_ref, bf16[2,4,128,128]{3,2,1,0:T(8,128)(2,1)S(1)} %copy-done.11), custom_call_target="tpu_custom_call" | custom-call | tf_op jit(solution)/shard_map/tables/pallas_call | solution.py:189
  27.1 1.4 %collective-permute-start.9 = (bf16[256,128]{1,0:T(8,128)(2,1)S(1)}, bf16[256,128]{1,0:T(8,128)(2,1)S(1)}, u32[]{:S(2)}, u32[]{:S(2)}) collective-permute-start(bf16[256,128]{1,0:T(8,128)(2,1)S(1)} %nodes.2.refs_0_), channel_id=1, source_target_pairs={{0,2},{1,3},{2,0},{3,1},{4,6},{5,7},{6,4},{7,5},{8,10},{9,11},{10,... | collective-permute-start | bytes 196616 | tf_op jit(solution)/shard_map/ppermute | solution.py:19
  28.5 2.2 %collective-permute-start.8 = (bf16[256,128]{1,0:T(8,128)(2,1)S(1)}, bf16[256,128]{1,0:T(8,128)(2,1)S(1)}, u32[]{:S(2)}, u32[]{:S(2)}) collective-permute-start(bf16[256,128]{1,0:T(8,128)(2,1)S(1)} %nodes.2.refs_0_), channel_id=1, source_target_pairs={{0,4},{1,5},{2,6},{3,7},{4,0},{5,1},{6,2},{7,3},{8,12},{9,13},{10,... | collective-permute-start | bytes 196616 | tf_op jit(solution)/shard_map/ppermute | solution.py:19
  30.7 0.9 collective-permute-start.7
  32.1 4.8 %collective-permute-done.8.refs_2_ = bf16[256,128]{1,0:T(8,128)(2,1)S(1)} collective-permute-done((bf16[256,128]{1,0:T(8,128)(2,1)S(1)}, bf16[256,128]{1,0:T(8,128)(2,1)S(1)}, u32[]{:S(2)}, u32[]{:S(2)}) %collective-permute-start.8) | collective-permute-done | bytes 65568 | tf_op jit(solution)/shard_map/ppermute | solution.py:19
  37.4 0.7 collective-permute-done.12.refs_6_
  38.3 2.2 %copy-done.2 = bf16[16,8,16384]{2,1,0:T(8,128)(2,1)S(1)} copy-done((bf16[16,8,16384]{2,1,0:T(8,128)(2,1)S(1)}, bf16[16,8,16384]{2,1,0:T(8,128)(2,1)}, u32[]{:S(2)}) %copy-start.2) | copy-done | bytes 4194328
  40.5 3.4 %spread.2 = bf16[8,16384]{1,0:T(8,128)(2,1)S(1)} custom-call(bf16[512,2048]{1,0:T(8,128)(2,1)S(1)} %get-tuple-element.8.select_ref, bf16[16,8,16384]{2,1,0:T(8,128)(2,1)S(1)} %copy-done.2, f32[2,16384]{1,0:T(2,128)S(1)} %copy-done.8, bf16[256,128]{1,0:T(8,128)(2,1)S(1)} %nodes.2.refs_0_, bf16[256,128]{1,0:T(8,128)(2,1)S(1)} %collective-permute-done.7.refs_1_, ...), custom_call_target="tpu_custom_call" | custom-call | tf_op jit(solution)/shard_map/spread/pallas_call | solution.py:272
  44.0 1.6 %collective-permute-start.14 = (bf16[8,8192]{1,0:T(8,128)(2,1)S(1)}, bf16[8,8192]{1,0:T(8,128)(2,1)S(1)}, u32[]{:S(2)}, u32[]{:S(2)}) collective-permute-start(bf16[8,8192]{1,0:T(8,128)(2,1)S(1)} %get-tuple-element.20), channel_id=1, source_target_pairs={{0,8},{8,0},{16,24},{24,16},{1,9},{9,1},{17,25},{25,17},{2,10},{10... | collective-permute-start | bytes 393224 | tf_op jit(solution)/shard_map/ppermute | solution.py:19
  45.5 1.5 %collective-permute-start.15 = (bf16[8,8192]{1,0:T(8,128)(2,1)S(1)}, bf16[8,8192]{1,0:T(8,128)(2,1)S(1)}, u32[]{:S(2)}, u32[]{:S(2)}) collective-permute-start(bf16[8,8192]{1,0:T(8,128)(2,1)S(1)} %get-tuple-element.21), channel_id=1, source_target_pairs={{0,16},{8,24},{16,0},{24,8},{1,17},{9,25},{17,1},{25,9},{2,18},{10... | collective-permute-start | bytes 393224 | tf_op jit(solution)/shard_map/ppermute | solution.py:19
  47.0 2.7 %collective-permute-done.14 = bf16[8,8192]{1,0:T(8,128)(2,1)S(1)} collective-permute-done((bf16[8,8192]{1,0:T(8,128)(2,1)S(1)}, bf16[8,8192]{1,0:T(8,128)(2,1)S(1)}, u32[]{:S(2)}, u32[]{:S(2)}) %collective-permute-start.14) | collective-permute-done | bytes 131104 | tf_op jit(solution)/shard_map/ppermute | solution.py:19
  49.8 1.2 %collective-permute-done.15 = bf16[8,8192]{1,0:T(8,128)(2,1)S(1)} collective-permute-done((bf16[8,8192]{1,0:T(8,128)(2,1)S(1)}, bf16[8,8192]{1,0:T(8,128)(2,1)S(1)}, u32[]{:S(2)}, u32[]{:S(2)}) %collective-permute-start.15) | collective-permute-done | bytes 131104 | tf_op jit(solution)/shard_map/ppermute | solution.py:19
  51.1 1.6 %collective-permute-start.16 = (bf16[8,8192]{1,0:T(8,128)(2,1)S(1)}, bf16[8,8192]{1,0:T(8,128)(2,1)S(1)}, u32[]{:S(2)}, u32[]{:S(2)}) collective-permute-start(bf16[8,8192]{1,0:T(8,128)(2,1)S(1)} %get-tuple-element.18), channel_id=1, source_target_pairs={{0,16},{8,24},{16,0},{24,8},{1,17},{9,25},{17,1},{25,9},{2,18},{10... | collective-permute-start | bytes 393224 | tf_op jit(solution)/shard_map/ppermute | solution.py:19
  52.6 0.5 collective-permute-start.17
  53.2 2.9 %collective-permute-done.16 = bf16[8,8192]{1,0:T(8,128)(2,1)S(1)} collective-permute-done((bf16[8,8192]{1,0:T(8,128)(2,1)S(1)}, bf16[8,8192]{1,0:T(8,128)(2,1)S(1)}, u32[]{:S(2)}, u32[]{:S(2)}) %collective-permute-start.16) | collective-permute-done | bytes 131104 | tf_op jit(solution)/shard_map/ppermute | solution.py:19
  56.1 1.5 %collective-permute-done.17 = bf16[8,8192]{1,0:T(8,128)(2,1)S(1)} collective-permute-done((bf16[8,8192]{1,0:T(8,128)(2,1)S(1)}, bf16[8,8192]{1,0:T(8,128)(2,1)S(1)}, u32[]{:S(2)}, u32[]{:S(2)}) %collective-permute-start.17) | collective-permute-done | bytes 131104 | tf_op jit(solution)/shard_map/ppermute | solution.py:19
  57.7 2.8 %tile_sums_second.1 = (f32[8,16384]{1,0:T(8,128)}, bf16[256,128]{1,0:T(8,128)(2,1)S(1)}) custom-call(f32[8,16384]{1,0:T(8,128)S(1)} %copy-done.6, f32[8,16384]{1,0:T(8,128)S(1)} %copy-done.7, bf16[8,16384]{1,0:T(8,128)(2,1)S(1)} %pad_maximum_fusion.mine_ref, bf16[8,16384]{1,0:T(8,128)(2,1)S(1)} %pad_maximum_fusion.1.theirs_ref, f32[1,16384]{1,0:T(1,128)S(1)} %bitcast.13, ...), custom_call_target="tpu_custom_call" | custom-call | tf_op jit(solution)/shard_map/tile_sums_second/pallas_call | solution.py:151
  60.5 1.2 %collective-permute-start.20 = (bf16[256,128]{1,0:T(8,128)(2,1)S(1)}, bf16[256,128]{1,0:T(8,128)(2,1)S(1)}, u32[]{:S(2)}, u32[]{:S(2)}) collective-permute-start(bf16[256,128]{1,0:T(8,128)(2,1)S(1)} %get-tuple-element.13.refs_0_), channel_id=1, source_target_pairs={{0,2},{1,3},{2,0},{3,1},{4,6},{5,7},{6,4},{7,5},{8,10},{9,11},{10,... | collective-permute-start | bytes 196616 | tf_op jit(solution)/shard_map/ppermute | solution.py:19
  61.6 1.7 %collective-permute-start.19 = (bf16[256,128]{1,0:T(8,128)(2,1)S(1)}, bf16[256,128]{1,0:T(8,128)(2,1)S(1)}, u32[]{:S(2)}, u32[]{:S(2)}) collective-permute-start(bf16[256,128]{1,0:T(8,128)(2,1)S(1)} %get-tuple-element.13.refs_0_), channel_id=1, source_target_pairs={{0,4},{1,5},{2,6},{3,7},{4,0},{5,1},{6,2},{7,3},{8,12},{9,13},{10,... | collective-permute-start | bytes 196616 | tf_op jit(solution)/shard_map/ppermute | solution.py:19
  63.3 1.6 %collective-permute-start.18 = (bf16[256,128]{1,0:T(8,128)(2,1)S(1)}, bf16[256,128]{1,0:T(8,128)(2,1)S(1)}, u32[]{:S(2)}, u32[]{:S(2)}) collective-permute-start(bf16[256,128]{1,0:T(8,128)(2,1)S(1)} %get-tuple-element.13.refs_0_), channel_id=1, source_target_pairs={{0,6},{1,7},{2,4},{3,5},{4,2},{5,3},{6,0},{7,1},{8,14},{9,15},{10,... | collective-permute-start | bytes 196616 | tf_op jit(solution)/shard_map/ppermute | solution.py:19
  65.4 2.2 %collective-permute-done.19.refs_2_ = bf16[256,128]{1,0:T(8,128)(2,1)S(1)} collective-permute-done((bf16[256,128]{1,0:T(8,128)(2,1)S(1)}, bf16[256,128]{1,0:T(8,128)(2,1)S(1)}, u32[]{:S(2)}, u32[]{:S(2)}) %collective-permute-start.19) | collective-permute-done | bytes 65568 | tf_op jit(solution)/shard_map/ppermute | solution.py:19
  67.6 1.8 %collective-permute-done.18.refs_1_ = bf16[256,128]{1,0:T(8,128)(2,1)S(1)} collective-permute-done((bf16[256,128]{1,0:T(8,128)(2,1)S(1)}, bf16[256,128]{1,0:T(8,128)(2,1)S(1)}, u32[]{:S(2)}, u32[]{:S(2)}) %collective-permute-start.18) | collective-permute-done | bytes 65568 | tf_op jit(solution)/shard_map/ppermute | solution.py:19
  69.4 1.2 %collective-permute-done.22.refs_5_ = bf16[256,128]{1,0:T(8,128)(2,1)S(1)} collective-permute-done((bf16[256,128]{1,0:T(8,128)(2,1)S(1)}, bf16[256,128]{1,0:T(8,128)(2,1)S(1)}, u32[]{:S(2)}, u32[]{:S(2)}) %collective-permute-start.22) | collective-permute-done | bytes 65568 | tf_op jit(solution)/shard_map/ppermute | solution.py:19
  71.1 2.2 %collective-permute-start.26 = (bf16[256,128]{1,0:T(8,128)(2,1)S(1)}, bf16[256,128]{1,0:T(8,128)(2,1)S(1)}, u32[]{:S(2)}, u32[]{:S(2)}) collective-permute-start(bf16[256,128]{1,0:T(8,128)(2,1)S(1)} %nodes.3.refs_0_), channel_id=1, source_target_pairs={{0,4},{1,5},{2,6},{3,7},{4,0},{5,1},{6,2},{7,3},{8,12},{9,13},{10,... | collective-permute-start | bytes 196616 | tf_op jit(solution)/shard_map/ppermute | solution.py:19
  73.4 2.2 %collective-permute-start.25 = (bf16[256,128]{1,0:T(8,128)(2,1)S(1)}, bf16[256,128]{1,0:T(8,128)(2,1)S(1)}, u32[]{:S(2)}, u32[]{:S(2)}) collective-permute-start(bf16[256,128]{1,0:T(8,128)(2,1)S(1)} %nodes.3.refs_0_), channel_id=1, source_target_pairs={{0,6},{1,7},{2,4},{3,5},{4,2},{5,3},{6,0},{7,1},{8,14},{9,15},{10,... | collective-permute-start | bytes 196616 | tf_op jit(solution)/shard_map/ppermute | solution.py:19
  75.5 0.9 collective-permute-done.27.refs_3_
  76.4 3.3 %collective-permute-done.26.refs_2_ = bf16[256,128]{1,0:T(8,128)(2,1)S(1)} collective-permute-done((bf16[256,128]{1,0:T(8,128)(2,1)S(1)}, bf16[256,128]{1,0:T(8,128)(2,1)S(1)}, u32[]{:S(2)}, u32[]{:S(2)}) %collective-permute-start.26) | collective-permute-done | bytes 65568 | tf_op jit(solution)/shard_map/ppermute | solution.py:19
  80.2 0.7 collective-permute-done.30.refs_6_
  81.1 3.4 %spread.3 = bf16[8,16384]{1,0:T(8,128)(2,1)S(1)} custom-call(bf16[512,2048]{1,0:T(8,128)(2,1)S(1)} %get-tuple-element.8.select_ref, bf16[16,8,16384]{2,1,0:T(8,128)(2,1)S(1)} %copy-done.3, f32[2,16384]{1,0:T(2,128)S(1)} %copy-done.8, bf16[256,128]{1,0:T(8,128)(2,1)S(1)} %nodes.3.refs_0_, bf16[256,128]{1,0:T(8,128)(2,1)S(1)} %collective-permute-done.25.refs_1_, ...), custom_call_target="tpu_custom_call" | custom-call | tf_op jit(solution)/shard_map/spread/pallas_call | solution.py:272
  84.6 0.6 collective-permute-start.32
  85.2 0.5 collective-permute-start.33
  85.7 4.7 %collective-permute-done.32 = bf16[8,8192]{1,0:T(8,128)(2,1)S(1)} collective-permute-done((bf16[8,8192]{1,0:T(8,128)(2,1)S(1)}, bf16[8,8192]{1,0:T(8,128)(2,1)S(1)}, u32[]{:S(2)}, u32[]{:S(2)}) %collective-permute-start.32) | collective-permute-done | bytes 131104 | tf_op jit(solution)/shard_map/ppermute | solution.py:19
  90.7 0.6 collective-permute-start.34
  91.3 1.5 %collective-permute-start.35 = (bf16[8,8192]{1,0:T(8,128)(2,1)S(1)}, bf16[8,8192]{1,0:T(8,128)(2,1)S(1)}, u32[]{:S(2)}, u32[]{:S(2)}) collective-permute-start(bf16[8,8192]{1,0:T(8,128)(2,1)S(1)} %get-tuple-element.15), channel_id=1, source_target_pairs={{0,8},{8,0},{16,24},{24,16},{1,9},{9,1},{17,25},{25,17},{2,10},{10... | collective-permute-start | bytes 393224 | tf_op jit(solution)/shard_map/ppermute | solution.py:19
  92.8 3.0 %collective-permute-done.34 = bf16[8,8192]{1,0:T(8,128)(2,1)S(1)} collective-permute-done((bf16[8,8192]{1,0:T(8,128)(2,1)S(1)}, bf16[8,8192]{1,0:T(8,128)(2,1)S(1)}, u32[]{:S(2)}, u32[]{:S(2)}) %collective-permute-start.34) | collective-permute-done | bytes 131104 | tf_op jit(solution)/shard_map/ppermute | solution.py:19
  95.8 0.5 collective-permute-done.35
  96.3 0.9 multiply_add_fusion
  (90 shorter events, 5.5 us)
Async XLA Ops:
  0.6 16.7 %copy-start = (s32[2048,2]{0,1:T(2,128)S(1)}, s32[2048,2]{0,1:T(2,128)}, u32[]{:S(2)}) copy-start(s32[2048,2]{0,1:T(2,128)} %param.20) | copy-start | bytes 49156
  0.6 16.2 %copy-start.16 = (s32[8]{0:T(128)S(1)}, s32[8]{0:T(128)}, u32[]{:S(2)}) copy-start(s32[8]{0:T(128)} %constant.5.clone) | copy-start | bytes 100
  0.7 16.2 %copy-start.15 = (s32[2,4]{1,0:T(2,128)S(1)}, s32[2,4]{1,0:T(2,128)}, u32[]{:S(2)}) copy-start(s32[2,4]{1,0:T(2,128)} %param.19) | copy-start | bytes 100
  4.8 12.2 %copy-start.14 = (s32[2048,1]{0,1:T(1,128)S(1)}, s32[2048,1]{0,1:T(1,128)}, u32[]{:S(2)}) copy-start(s32[2048,1]{0,1:T(1,128)} %param.15) | copy-start | bytes 24580
  4.8 13.6 %copy-start.13 = (s32[2048]{0:T(1024)S(1)}, s32[2048]{0:T(1024)}, u32[]{:S(2)}) copy-start(s32[2048]{0:T(1024)} %param.16) | copy-start | bytes 24580
  4.8 19.0 %copy-start.11 = (bf16[2,4,128,128]{3,2,1,0:T(8,128)(2,1)S(1)}, bf16[2,4,128,128]{3,2,1,0:T(8,128)(2,1)}, u32[]{:S(2)}) copy-start(bf16[2,4,128,128]{3,2,1,0:T(8,128)(2,1)} %conv_ref.1) | copy-start | bytes 786436
  4.8 33.6 %copy-start.8 = (f32[2,16384]{1,0:T(2,128)S(1)}, f32[2,16384]{1,0:T(2,128)}, u32[]{:S(2)}) copy-start(f32[2,16384]{1,0:T(2,128)} %weight_ref.3) | copy-start | bytes 393220
  11.2 15.4 %collective-permute-start.3 = (bf16[256,128]{1,0:T(8,128)(2,1)S(1)}, bf16[256,128]{1,0:T(8,128)(2,1)S(1)}, u32[]{:S(2)}, u32[]{:S(2)}) collective-permute-start(bf16[256,128]{1,0:T(8,128)(2,1)S(1)} %get-tuple-element.11.refs_0_), channel_id=1, source_target_pairs={{0,1},{1,0},{2,3},{3,2},{4,5},{5,4},{6,7},{7,6},{8,9},{9,8},{10,11... | collective-permute-start | bytes 196616 | tf_op jit(solution)/shard_map/ppermute | solution.py:19
  11.7 6.7 %collective-permute-start.2 = (bf16[256,128]{1,0:T(8,128)(2,1)S(1)}, bf16[256,128]{1,0:T(8,128)(2,1)S(1)}, u32[]{:S(2)}, u32[]{:S(2)}) collective-permute-start(bf16[256,128]{1,0:T(8,128)(2,1)S(1)} %get-tuple-element.11.refs_0_), channel_id=1, source_target_pairs={{0,2},{1,3},{2,0},{3,1},{4,6},{5,7},{6,4},{7,5},{8,10},{9,11},{10,... | collective-permute-start | bytes 196616 | tf_op jit(solution)/shard_map/ppermute | solution.py:19
  14.3 7.0 %collective-permute-start.1 = (bf16[256,128]{1,0:T(8,128)(2,1)S(1)}, bf16[256,128]{1,0:T(8,128)(2,1)S(1)}, u32[]{:S(2)}, u32[]{:S(2)}) collective-permute-start(bf16[256,128]{1,0:T(8,128)(2,1)S(1)} %get-tuple-element.11.refs_0_), channel_id=1, source_target_pairs={{0,4},{1,5},{2,6},{3,7},{4,0},{5,1},{6,2},{7,3},{8,12},{9,13},{10,... | collective-permute-start | bytes 196616 | tf_op jit(solution)/shard_map/ppermute | solution.py:19
  16.9 6.1 %collective-permute-start = (bf16[256,128]{1,0:T(8,128)(2,1)S(1)}, bf16[256,128]{1,0:T(8,128)(2,1)S(1)}, u32[]{:S(2)}, u32[]{:S(2)}) collective-permute-start(bf16[256,128]{1,0:T(8,128)(2,1)S(1)} %get-tuple-element.11.refs_0_), channel_id=1, source_target_pairs={{0,6},{1,7},{2,4},{3,5},{4,2},{5,3},{6,0},{7,1},{8,14},{9,15},{10,... | collective-permute-start | bytes 196616 | tf_op jit(solution)/shard_map/ppermute | solution.py:19
  18.4 8.2 %collective-permute-start.6 = (bf16[256,128]{1,0:T(8,128)(2,1)S(1)}, bf16[256,128]{1,0:T(8,128)(2,1)S(1)}, u32[]{:S(2)}, u32[]{:S(2)}) collective-permute-start(bf16[256,128]{1,0:T(8,128)(2,1)S(1)} %collective-permute-done.2.refs_3_), channel_id=1, source_target_pairs={{0,1},{1,0},{2,3},{3,2},{4,5},{5,4},{6,7},{7,6},{8,9},{9,8},{10,11... | collective-permute-start | bytes 196616 | tf_op jit(solution)/shard_map/ppermute | solution.py:19
  21.3 5.4 %collective-permute-start.5 = (bf16[256,128]{1,0:T(8,128)(2,1)S(1)}, bf16[256,128]{1,0:T(8,128)(2,1)S(1)}, u32[]{:S(2)}, u32[]{:S(2)}) collective-permute-start(bf16[256,128]{1,0:T(8,128)(2,1)S(1)} %collective-permute-done.1.refs_2_), channel_id=1, source_target_pairs={{0,1},{1,0},{2,3},{3,2},{4,5},{5,4},{6,7},{7,6},{8,9},{9,8},{10,11... | collective-permute-start | bytes 196616 | tf_op jit(solution)/shard_map/ppermute | solution.py:19
  22.9 3.8 %collective-permute-start.4 = (bf16[256,128]{1,0:T(8,128)(2,1)S(1)}, bf16[256,128]{1,0:T(8,128)(2,1)S(1)}, u32[]{:S(2)}, u32[]{:S(2)}) collective-permute-start(bf16[256,128]{1,0:T(8,128)(2,1)S(1)} %collective-permute-done.refs_1_), channel_id=1, source_target_pairs={{0,1},{1,0},{2,3},{3,2},{4,5},{5,4},{6,7},{7,6},{8,9},{9,8},{10,11... | collective-permute-start | bytes 196616 | tf_op jit(solution)/shard_map/ppermute | solution.py:19
  27.1 4.6 %collective-permute-start.9 = (bf16[256,128]{1,0:T(8,128)(2,1)S(1)}, bf16[256,128]{1,0:T(8,128)(2,1)S(1)}, u32[]{:S(2)}, u32[]{:S(2)}) collective-permute-start(bf16[256,128]{1,0:T(8,128)(2,1)S(1)} %nodes.2.refs_0_), channel_id=1, source_target_pairs={{0,2},{1,3},{2,0},{3,1},{4,6},{5,7},{6,4},{7,5},{8,10},{9,11},{10,... | collective-permute-start | bytes 196616 | tf_op jit(solution)/shard_map/ppermute | solution.py:19
  28.5 8.4 %collective-permute-start.8 = (bf16[256,128]{1,0:T(8,128)(2,1)S(1)}, bf16[256,128]{1,0:T(8,128)(2,1)S(1)}, u32[]{:S(2)}, u32[]{:S(2)}) collective-permute-start(bf16[256,128]{1,0:T(8,128)(2,1)S(1)} %nodes.2.refs_0_), channel_id=1, source_target_pairs={{0,4},{1,5},{2,6},{3,7},{4,0},{5,1},{6,2},{7,3},{8,12},{9,13},{10,... | collective-permute-start | bytes 196616 | tf_op jit(solution)/shard_map/ppermute | solution.py:19
  30.7 6.2 %collective-permute-start.7 = (bf16[256,128]{1,0:T(8,128)(2,1)S(1)}, bf16[256,128]{1,0:T(8,128)(2,1)S(1)}, u32[]{:S(2)}, u32[]{:S(2)}) collective-permute-start(bf16[256,128]{1,0:T(8,128)(2,1)S(1)} %nodes.2.refs_0_), channel_id=1, source_target_pairs={{0,6},{1,7},{2,4},{3,5},{4,2},{5,3},{6,0},{7,1},{8,14},{9,15},{10,... | collective-permute-start | bytes 196616 | tf_op jit(solution)/shard_map/ppermute | solution.py:19
  31.6 5.8 %collective-permute-start.10 = (bf16[256,128]{1,0:T(8,128)(2,1)S(1)}, bf16[256,128]{1,0:T(8,128)(2,1)S(1)}, u32[]{:S(2)}, u32[]{:S(2)}) collective-permute-start(bf16[256,128]{1,0:T(8,128)(2,1)S(1)} %nodes.2.refs_0_), channel_id=1, source_target_pairs={{0,1},{1,0},{2,3},{3,2},{4,5},{5,4},{6,7},{7,6},{8,9},{9,8},{10,11... | collective-permute-start | bytes 196616 | tf_op jit(solution)/shard_map/ppermute | solution.py:19
  31.7 5.7 %collective-permute-start.13 = (bf16[256,128]{1,0:T(8,128)(2,1)S(1)}, bf16[256,128]{1,0:T(8,128)(2,1)S(1)}, u32[]{:S(2)}, u32[]{:S(2)}) collective-permute-start(bf16[256,128]{1,0:T(8,128)(2,1)S(1)} %collective-permute-done.9.refs_3_), channel_id=1, source_target_pairs={{0,1},{1,0},{2,3},{3,2},{4,5},{5,4},{6,7},{7,6},{8,9},{9,8},{10,11... | collective-permute-start | bytes 196616 | tf_op jit(solution)/shard_map/ppermute | solution.py:19
  36.9 1.3 %collective-permute-start.12 = (bf16[256,128]{1,0:T(8,128)(2,1)S(1)}, bf16[256,128]{1,0:T(8,128)(2,1)S(1)}, u32[]{:S(2)}, u32[]{:S(2)}) collective-permute-start(bf16[256,128]{1,0:T(8,128)(2,1)S(1)} %collective-permute-done.8.refs_2_), channel_id=1, source_target_pairs={{0,1},{1,0},{2,3},{3,2},{4,5},{5,4},{6,7},{7,6},{8,9},{9,8},{10,11... | collective-permute-start | bytes 196616 | tf_op jit(solution)/shard_map/ppermute | solution.py:19
  36.9 1.4 %collective-permute-start.11 = (bf16[256,128]{1,0:T(8,128)(2,1)S(1)}, bf16[256,128]{1,0:T(8,128)(2,1)S(1)}, u32[]{:S(2)}, u32[]{:S(2)}) collective-permute-start(bf16[256,128]{1,0:T(8,128)(2,1)S(1)} %collective-permute-done.7.refs_1_), channel_id=1, source_target_pairs={{0,1},{1,0},{2,3},{3,2},{4,5},{5,4},{6,7},{7,6},{8,9},{9,8},{10,11... | collective-permute-start | bytes 196616 | tf_op jit(solution)/shard_map/ppermute | solution.py:19
  40.5 17.1 %copy-start.3 = (bf16[16,8,16384]{2,1,0:T(8,128)(2,1)S(1)}, bf16[16,8,16384]{2,1,0:T(8,128)(2,1)}, u32[]{:S(2)}) copy-start(bf16[16,8,16384]{2,1,0:T(8,128)(2,1)} %copy-done.1) | copy-start | bytes 12582916
  40.5 17.1 %copy-start.6 = (f32[8,16384]{1,0:T(8,128)S(1)}, f32[8,16384]{1,0:T(8,128)}, u32[]{:S(2)}) copy-start(f32[8,16384]{1,0:T(8,128)} %state_ref.1) | copy-start | bytes 1572868
  40.5 17.1 %copy-start.7 = (f32[8,16384]{1,0:T(8,128)S(1)}, f32[8,16384]{1,0:T(8,128)}, u32[]{:S(2)}) copy-start(f32[8,16384]{1,0:T(8,128)} %climate_ref.1) | copy-start | bytes 1572868
  40.5 17.2 %copy-start.10 = (f32[16384]{0:T(1024)S(1)}, f32[16384]{0:T(1024)}, u32[]{:S(2)}) copy-start(f32[16384]{0:T(1024)} %param.17) | copy-start | bytes 196612
  44.0 5.8 %collective-permute-start.14 = (bf16[8,8192]{1,0:T(8,128)(2,1)S(1)}, bf16[8,8192]{1,0:T(8,128)(2,1)S(1)}, u32[]{:S(2)}, u32[]{:S(2)}) collective-permute-start(bf16[8,8192]{1,0:T(8,128)(2,1)S(1)} %get-tuple-element.20), channel_id=1, source_target_pairs={{0,8},{8,0},{16,24},{24,16},{1,9},{9,1},{17,25},{25,17},{2,10},{10... | collective-permute-start | bytes 393224 | tf_op jit(solution)/shard_map/ppermute | solution.py:19
  45.5 5.5 %collective-permute-start.15 = (bf16[8,8192]{1,0:T(8,128)(2,1)S(1)}, bf16[8,8192]{1,0:T(8,128)(2,1)S(1)}, u32[]{:S(2)}, u32[]{:S(2)}) collective-permute-start(bf16[8,8192]{1,0:T(8,128)(2,1)S(1)} %get-tuple-element.21), channel_id=1, source_target_pairs={{0,16},{8,24},{16,0},{24,8},{1,17},{9,25},{17,1},{25,9},{2,18},{10... | collective-permute-start | bytes 393224 | tf_op jit(solution)/shard_map/ppermute | solution.py:19
  51.1 5.0 %collective-permute-start.16 = (bf16[8,8192]{1,0:T(8,128)(2,1)S(1)}, bf16[8,8192]{1,0:T(8,128)(2,1)S(1)}, u32[]{:S(2)}, u32[]{:S(2)}) collective-permute-start(bf16[8,8192]{1,0:T(8,128)(2,1)S(1)} %get-tuple-element.18), channel_id=1, source_target_pairs={{0,16},{8,24},{16,0},{24,8},{1,17},{9,25},{17,1},{25,9},{2,18},{10... | collective-permute-start | bytes 393224 | tf_op jit(solution)/shard_map/ppermute | solution.py:19
  52.6 5.0 %collective-permute-start.17 = (bf16[8,8192]{1,0:T(8,128)(2,1)S(1)}, bf16[8,8192]{1,0:T(8,128)(2,1)S(1)}, u32[]{:S(2)}, u32[]{:S(2)}) collective-permute-start(bf16[8,8192]{1,0:T(8,128)(2,1)S(1)} %get-tuple-element.19), channel_id=1, source_target_pairs={{0,8},{8,0},{16,24},{24,16},{1,9},{9,1},{17,25},{25,17},{2,10},{10... | collective-permute-start | bytes 393224 | tf_op jit(solution)/shard_map/ppermute | solution.py:19
  60.5 4.4 %collective-permute-start.20 = (bf16[256,128]{1,0:T(8,128)(2,1)S(1)}, bf16[256,128]{1,0:T(8,128)(2,1)S(1)}, u32[]{:S(2)}, u32[]{:S(2)}) collective-permute-start(bf16[256,128]{1,0:T(8,128)(2,1)S(1)} %get-tuple-element.13.refs_0_), channel_id=1, source_target_pairs={{0,2},{1,3},{2,0},{3,1},{4,6},{5,7},{6,4},{7,5},{8,10},{9,11},{10,... | collective-permute-start | bytes 196616 | tf_op jit(solution)/shard_map/ppermute | solution.py:19
  61.6 5.9 %collective-permute-start.19 = (bf16[256,128]{1,0:T(8,128)(2,1)S(1)}, bf16[256,128]{1,0:T(8,128)(2,1)S(1)}, u32[]{:S(2)}, u32[]{:S(2)}) collective-permute-start(bf16[256,128]{1,0:T(8,128)(2,1)S(1)} %get-tuple-element.13.refs_0_), channel_id=1, source_target_pairs={{0,4},{1,5},{2,6},{3,7},{4,0},{5,1},{6,2},{7,3},{8,12},{9,13},{10,... | collective-permute-start | bytes 196616 | tf_op jit(solution)/shard_map/ppermute | solution.py:19
  63.3 6.1 %collective-permute-start.18 = (bf16[256,128]{1,0:T(8,128)(2,1)S(1)}, bf16[256,128]{1,0:T(8,128)(2,1)S(1)}, u32[]{:S(2)}, u32[]{:S(2)}) collective-permute-start(bf16[256,128]{1,0:T(8,128)(2,1)S(1)} %get-tuple-element.13.refs_0_), channel_id=1, source_target_pairs={{0,6},{1,7},{2,4},{3,5},{4,2},{5,3},{6,0},{7,1},{8,14},{9,15},{10,... | collective-permute-start | bytes 196616 | tf_op jit(solution)/shard_map/ppermute | solution.py:19
  64.9 4.5 %collective-permute-start.21 = (bf16[256,128]{1,0:T(8,128)(2,1)S(1)}, bf16[256,128]{1,0:T(8,128)(2,1)S(1)}, u32[]{:S(2)}, u32[]{:S(2)}) collective-permute-start(bf16[256,128]{1,0:T(8,128)(2,1)S(1)} %get-tuple-element.13.refs_0_), channel_id=1, source_target_pairs={{0,1},{1,0},{2,3},{3,2},{4,5},{5,4},{6,7},{7,6},{8,9},{9,8},{10,11... | collective-permute-start | bytes 196616 | tf_op jit(solution)/shard_map/ppermute | solution.py:19
  64.9 4.5 %collective-permute-start.24 = (bf16[256,128]{1,0:T(8,128)(2,1)S(1)}, bf16[256,128]{1,0:T(8,128)(2,1)S(1)}, u32[]{:S(2)}, u32[]{:S(2)}) collective-permute-start(bf16[256,128]{1,0:T(8,128)(2,1)S(1)} %collective-permute-done.20.refs_3_), channel_id=1, source_target_pairs={{0,1},{1,0},{2,3},{3,2},{4,5},{5,4},{6,7},{7,6},{8,9},{9,8},{10,11... | collective-permute-start | bytes 196616 | tf_op jit(solution)/shard_map/ppermute | solution.py:19
  67.6 1.8 %collective-permute-start.23 = (bf16[256,128]{1,0:T(8,128)(2,1)S(1)}, bf16[256,128]{1,0:T(8,128)(2,1)S(1)}, u32[]{:S(2)}, u32[]{:S(2)}) collective-permute-start(bf16[256,128]{1,0:T(8,128)(2,1)S(1)} %collective-permute-done.19.refs_2_), channel_id=1, source_target_pairs={{0,1},{1,0},{2,3},{3,2},{4,5},{5,4},{6,7},{7,6},{8,9},{9,8},{10,11... | collective-permute-start | bytes 196616 | tf_op jit(solution)/shard_map/ppermute | solution.py:19
  69.4 1.3 %collective-permute-start.22 = (bf16[256,128]{1,0:T(8,128)(2,1)S(1)}, bf16[256,128]{1,0:T(8,128)(2,1)S(1)}, u32[]{:S(2)}, u32[]{:S(2)}) collective-permute-start(bf16[256,128]{1,0:T(8,128)(2,1)S(1)} %collective-permute-done.18.refs_1_), channel_id=1, source_target_pairs={{0,1},{1,0},{2,3},{3,2},{4,5},{5,4},{6,7},{7,6},{8,9},{9,8},{10,11... | collective-permute-start | bytes 196616 | tf_op jit(solution)/shard_map/ppermute | solution.py:19
  71.1 25.2 %copy-start.12 = (f32[8,16384]{1,0:T(8,128)S(1)}, f32[8,16384]{1,0:T(8,128)}, u32[]{:S(2)}) copy-start(f32[8,16384]{1,0:T(8,128)} %get-tuple-element.6) | copy-start | bytes 1572868
  71.1 5.3 %collective-permute-start.27 = (bf16[256,128]{1,0:T(8,128)(2,1)S(1)}, bf16[256,128]{1,0:T(8,128)(2,1)S(1)}, u32[]{:S(2)}, u32[]{:S(2)}) collective-permute-start(bf16[256,128]{1,0:T(8,128)(2,1)S(1)} %nodes.3.refs_0_), channel_id=1, source_target_pairs={{0,2},{1,3},{2,0},{3,1},{4,6},{5,7},{6,4},{7,5},{8,10},{9,11},{10,... | collective-permute-start | bytes 196616 | tf_op jit(solution)/shard_map/ppermute | solution.py:19
  71.1 8.6 %collective-permute-start.26 = (bf16[256,128]{1,0:T(8,128)(2,1)S(1)}, bf16[256,128]{1,0:T(8,128)(2,1)S(1)}, u32[]{:S(2)}, u32[]{:S(2)}) collective-permute-start(bf16[256,128]{1,0:T(8,128)(2,1)S(1)} %nodes.3.refs_0_), channel_id=1, source_target_pairs={{0,4},{1,5},{2,6},{3,7},{4,0},{5,1},{6,2},{7,3},{8,12},{9,13},{10,... | collective-permute-start | bytes 196616 | tf_op jit(solution)/shard_map/ppermute | solution.py:19
  73.4 6.4 %collective-permute-start.25 = (bf16[256,128]{1,0:T(8,128)(2,1)S(1)}, bf16[256,128]{1,0:T(8,128)(2,1)S(1)}, u32[]{:S(2)}, u32[]{:S(2)}) collective-permute-start(bf16[256,128]{1,0:T(8,128)(2,1)S(1)} %nodes.3.refs_0_), channel_id=1, source_target_pairs={{0,6},{1,7},{2,4},{3,5},{4,2},{5,3},{6,0},{7,1},{8,14},{9,15},{10,... | collective-permute-start | bytes 196616 | tf_op jit(solution)/shard_map/ppermute | solution.py:19
  75.5 4.7 %collective-permute-start.28 = (bf16[256,128]{1,0:T(8,128)(2,1)S(1)}, bf16[256,128]{1,0:T(8,128)(2,1)S(1)}, u32[]{:S(2)}, u32[]{:S(2)}) collective-permute-start(bf16[256,128]{1,0:T(8,128)(2,1)S(1)} %nodes.3.refs_0_), channel_id=1, source_target_pairs={{0,1},{1,0},{2,3},{3,2},{4,5},{5,4},{6,7},{7,6},{8,9},{9,8},{10,11... | collective-permute-start | bytes 196616 | tf_op jit(solution)/shard_map/ppermute | solution.py:19
  76.4 3.9 %collective-permute-start.31 = (bf16[256,128]{1,0:T(8,128)(2,1)S(1)}, bf16[256,128]{1,0:T(8,128)(2,1)S(1)}, u32[]{:S(2)}, u32[]{:S(2)}) collective-permute-start(bf16[256,128]{1,0:T(8,128)(2,1)S(1)} %collective-permute-done.27.refs_3_), channel_id=1, source_target_pairs={{0,1},{1,0},{2,3},{3,2},{4,5},{5,4},{6,7},{7,6},{8,9},{9,8},{10,11... | collective-permute-start | bytes 196616 | tf_op jit(solution)/shard_map/ppermute | solution.py:19
  79.7 1.3 %collective-permute-start.30 = (bf16[256,128]{1,0:T(8,128)(2,1)S(1)}, bf16[256,128]{1,0:T(8,128)(2,1)S(1)}, u32[]{:S(2)}, u32[]{:S(2)}) collective-permute-start(bf16[256,128]{1,0:T(8,128)(2,1)S(1)} %collective-permute-done.26.refs_2_), channel_id=1, source_target_pairs={{0,1},{1,0},{2,3},{3,2},{4,5},{5,4},{6,7},{7,6},{8,9},{9,8},{10,11... | collective-permute-start | bytes 196616 | tf_op jit(solution)/shard_map/ppermute | solution.py:19
  79.7 1.4 %collective-permute-start.29 = (bf16[256,128]{1,0:T(8,128)(2,1)S(1)}, bf16[256,128]{1,0:T(8,128)(2,1)S(1)}, u32[]{:S(2)}, u32[]{:S(2)}) collective-permute-start(bf16[256,128]{1,0:T(8,128)(2,1)S(1)} %collective-permute-done.25.refs_1_), channel_id=1, source_target_pairs={{0,1},{1,0},{2,3},{3,2},{4,5},{5,4},{6,7},{7,6},{8,9},{9,8},{10,11... | collective-permute-start | bytes 196616 | tf_op jit(solution)/shard_map/ppermute | solution.py:19
  84.6 5.8 %collective-permute-start.32 = (bf16[8,8192]{1,0:T(8,128)(2,1)S(1)}, bf16[8,8192]{1,0:T(8,128)(2,1)S(1)}, u32[]{:S(2)}, u32[]{:S(2)}) collective-permute-start(bf16[8,8192]{1,0:T(8,128)(2,1)S(1)} %get-tuple-element.16), channel_id=1, source_target_pairs={{0,8},{8,0},{16,24},{24,16},{1,9},{9,1},{17,25},{25,17},{2,10},{10... | collective-permute-start | bytes 393224 | tf_op jit(solution)/shard_map/ppermute | solution.py:19
  85.2 5.5 %collective-permute-start.33 = (bf16[8,8192]{1,0:T(8,128)(2,1)S(1)}, bf16[8,8192]{1,0:T(8,128)(2,1)S(1)}, u32[]{:S(2)}, u32[]{:S(2)}) collective-permute-start(bf16[8,8192]{1,0:T(8,128)(2,1)S(1)} %get-tuple-element.17), channel_id=1, source_target_pairs={{0,16},{8,24},{16,0},{24,8},{1,17},{9,25},{17,1},{25,9},{2,18},{10... | collective-permute-start | bytes 393224 | tf_op jit(solution)/shard_map/ppermute | solution.py:19
  90.7 5.0 %collective-permute-start.34 = (bf16[8,8192]{1,0:T(8,128)(2,1)S(1)}, bf16[8,8192]{1,0:T(8,128)(2,1)S(1)}, u32[]{:S(2)}, u32[]{:S(2)}) collective-permute-start(bf16[8,8192]{1,0:T(8,128)(2,1)S(1)} %get-tuple-element.14), channel_id=1, source_target_pairs={{0,16},{8,24},{16,0},{24,8},{1,17},{9,25},{17,1},{25,9},{2,18},{10... | collective-permute-start | bytes 393224 | tf_op jit(solution)/shard_map/ppermute | solution.py:19
  91.3 5.0 %collective-permute-start.35 = (bf16[8,8192]{1,0:T(8,128)(2,1)S(1)}, bf16[8,8192]{1,0:T(8,128)(2,1)S(1)}, u32[]{:S(2)}, u32[]{:S(2)}) collective-permute-start(bf16[8,8192]{1,0:T(8,128)(2,1)S(1)} %get-tuple-element.15), channel_id=1, source_target_pairs={{0,8},{8,0},{16,24},{24,16},{1,9},{9,1},{17,25},{25,17},{2,10},{10... | collective-permute-start | bytes 393224 | tf_op jit(solution)/shard_map/ppermute | solution.py:19
  (5 other events, 8.3 us)

commit v3 on v2

v3 whole, which is shorter than its diff:
```python
import functools

import jax
import jax.numpy as jnp
from jax import lax
from jax.experimental import pallas as pl
from jax.experimental.pallas import tpu as pltpu
from jax.sharding import PartitionSpec as P

TILE = 64
LANES = 128
FIRST_BYTES = 107 * 512 * 1024
VMEM_BYTES = 40 * 1024 * 1024
TABLE_BYTES = 32 * 1024 * 1024
HALF = jnp.bfloat16
FULL = jnp.float32


def swap(array, axis, mask):
    size = lax.axis_size(axis)
    return lax.ppermute(array, axis, [(i, i ^ mask) for i in range(size)])


def slot_masks():
    return (0, 2, 4, 6, 1, 3, 5, 7) if lax.axis_size("col") == 8 else None


def slot_source(masks, myself, slot):
    return slot if masks is None else myself ^ masks[slot]


def gather_slots(array):
    if slot_masks() is not None:
        same_core = [array] + [swap(array, "col", mask) for mask in (2, 4, 6)]
        return same_core + [swap(piece, "col", 1) for piece in same_core]
    stacked = lax.all_gather(array, "col")
    return [stacked[i] for i in range(lax.axis_size("col"))]


def tile_indicator(tiles, columns):
    tile = lax.broadcasted_iota(jnp.int32, (tiles, columns), 0)
    column = lax.broadcasted_iota(jnp.int32, (tiles, columns), 1)
    return (column >= tile * TILE) & (column < tile * TILE + TILE)


def ones_where(mask):
    return jnp.where(mask, 1.0, 0.0).astype(HALF)


def tile_sums(weighted, ensemble):
    members, levels, width = ensemble.shape
    product = ensemble.astype(FULL) * weighted[None]
    product = product.reshape(members * levels, width).astype(HALF)
    return lax.dot_general(
        ones_where(tile_indicator(width // TILE, width)),
        product,
        (((1,), (1,)), ((), ())),
        preferred_element_type=FULL,
    ).astype(HALF)


def whole(count):
    return [pl.BlockSpec(memory_space=pltpu.VMEM)] * count


def params(limit):
    return pltpu.CompilerParams(vmem_limit_bytes=limit)


def column_sizes(ensemble):
    members, levels, fine = ensemble.shape
    width = min(fine, LANES // 4 * TILE)
    return members, levels, fine, width, fine // width


def chunk_copy(source, target, sems, index, width, i):
    lead = (slice(None),) * (len(source.shape) - 1)
    span = pl.ds(pl.multiple_of(i * width, width), width)
    return pltpu.make_async_copy(
        source.at[lead + (span,)], target.at[lead + (span,)], sems.at[index, i]
    )


def first_kernel(
    width, state_hbm, weight_hbm, ensemble_hbm, partial_ref, state_ref, weight_ref, ensemble_ref, sems
):
    steps = state_hbm.shape[1] // width
    tiles = width // TILE
    pairs = [(state_hbm, state_ref), (weight_hbm, weight_ref), (ensemble_hbm, ensemble_ref)]

    def copies(i):
        return [
            chunk_copy(source, target, sems, j, width, i)
            for j, (source, target) in enumerate(pairs)
        ]

    for i in range(steps):
        for copy in copies(i):
            copy.start()

    def step(i, carry):
        for copy in copies(i):
            copy.wait()
        span = pl.ds(pl.multiple_of(i * width, width), width)
        weighted = state_ref[:, span] * weight_ref[:, span]
        rows = pl.ds(pl.multiple_of(i * tiles, tiles), tiles)
        partial_ref[rows, :] = tile_sums(weighted, ensemble_ref[:, :, span])
        return carry

    lax.fori_loop(0, steps, step, 0)


def run_first(state, weight, ensemble):
    members, levels, fine, width, steps = column_sizes(ensemble)
    return pl.pallas_call(
        functools.partial(first_kernel, width),
        in_specs=[pl.BlockSpec(memory_space=pltpu.HBM)] * 3,
        out_specs=whole(1)[0],
        out_shape=jax.ShapeDtypeStruct((fine // TILE, members * levels), HALF),
        scratch_shapes=[
            pltpu.VMEM((levels, fine), FULL),
            pltpu.VMEM((1, fine), FULL),
            pltpu.VMEM((members, levels, fine), HALF),
            pltpu.SemaphoreType.DMA((3, steps)),
        ],
        compiler_params=params(FIRST_BYTES),
        name="tile_sums_first",
    )(state, weight, ensemble)


def second_kernel(width, scale, ensemble_ref, state_ref, climate_ref, weight_ref, *refs):
    sum_refs, (state_out, partial_ref) = refs[:4], refs[4:]
    tiles = width // TILE
    half = sum_refs[0].shape[1] // width

    for part in range(2):
        mine_ref, theirs_ref = sum_refs[2 * part : 2 * part + 2]

        def step(j, carry):
            i = j + part * half
            span = pl.ds(pl.multiple_of(i * width, width), width)
            near = pl.ds(pl.multiple_of(j * width, width), width)
            total = mine_ref[:, near].astype(FULL) + theirs_ref[:, near].astype(FULL)
            state = climate_ref[:, span] * state_ref[:, span] + total * scale
            state_out[:, span] = state
            rows = pl.ds(pl.multiple_of(i * tiles, tiles), tiles)
            partial_ref[rows, :] = tile_sums(state * weight_ref[:, span], ensemble_ref[:, :, span])
            return carry

        lax.fori_loop(0, half, step, 0)


def run_second(scale, state, climate, sums, weight, ensemble):
    members, levels, fine, width, steps = column_sizes(ensemble)
    return pl.pallas_call(
        functools.partial(second_kernel, width, scale),
        in_specs=whole(8),
        out_specs=whole(2),
        out_shape=[
            jax.ShapeDtypeStruct((levels, fine), FULL),
            jax.ShapeDtypeStruct((fine // TILE, members * levels), HALF),
        ],
        compiler_params=params(VMEM_BYTES),
        name="tile_sums_second",
    )(ensemble, state, climate, weight, *sums)


def matrix_kernel(masks, myself_ref, near_ref, dest_ref, local_ref, conv_ref, matrix_ref):
    blocks, neigh, size, _ = conv_ref.shape
    nodes = blocks * size
    rows = [
        jnp.concatenate([conv_ref[b, k] for k in range(neigh)], axis=1) for b in range(blocks)
    ]
    row = lax.broadcasted_iota(jnp.int32, (size, nodes), 0)
    for s in range(dest_ref.shape[1] // nodes):
        source = slot_source(masks, myself_ref[0], s)
        span = pl.ds(pl.multiple_of(source * nodes, nodes), nodes)
        tile_node = dest_ref[:, span] * nodes + local_ref[:, span]
        for b in range(blocks):
            place = jnp.concatenate(
                [ones_where(row == tile_node - near_ref[b, k] * size) for k in range(neigh)], axis=0
            )
            matrix_ref[b * size : (b + 1) * size, s * nodes : (s + 1) * nodes] = jnp.dot(
                rows[b], place, preferred_element_type=FULL
            ).astype(HALF)


def run_matrix(myself, neighbours, dest, local, conv_blocks):
    blocks, neigh, size, _ = conv_blocks.shape
    scalars = pl.BlockSpec(memory_space=pltpu.SMEM)
    return pl.pallas_call(
        functools.partial(matrix_kernel, slot_masks()),
        in_specs=[scalars, scalars] + whole(3),
        out_specs=whole(1)[0],
        out_shape=jax.ShapeDtypeStruct((blocks * size, dest.shape[1]), HALF),
        compiler_params=params(TABLE_BYTES),
        name="node_matrix",
    )(myself, neighbours, dest, local, conv_blocks)


def select_kernel(masks, nodes, myself_ref, dest_ref, local_ref, select_ref):
    span = pl.ds(pl.multiple_of(myself_ref[0] * nodes, nodes), nodes)
    dest, local = (
        jnp.concatenate([ref[k : k + 1, span] for k in range(2)], axis=1)
        for ref in (dest_ref, local_ref)
    )
    row = lax.broadcasted_iota(jnp.int32, (nodes, 2 * nodes), 0)
    for s in range(dest_ref.shape[1] // nodes):
        source = slot_source(masks, myself_ref[0], s)
        select_ref[s * nodes : (s + 1) * nodes, :] = ones_where(
            row == jnp.where(dest == source, local, -1)
        )


def run_select(myself, dest, local, nodes):
    return pl.pallas_call(
        functools.partial(select_kernel, slot_masks(), nodes),
        in_specs=[pl.BlockSpec(memory_space=pltpu.SMEM)] + whole(2),
        out_specs=whole(1)[0],
        out_shape=jax.ShapeDtypeStruct((dest.shape[1], 2 * nodes), HALF),
        compiler_params=params(TABLE_BYTES),
        name="selection",
    )(myself, dest, local)


def nodes_kernel(matrix_ref, *refs):
    span = refs[0].shape[0]
    total = jnp.zeros(refs[-1].shape, FULL)
    for s, piece in enumerate(refs[:-1]):
        total = total + jnp.dot(
            matrix_ref[:, s * span : (s + 1) * span], piece[...], preferred_element_type=FULL
        )
    refs[-1][...] = total.astype(HALF)


def run_nodes(matrix, partial_all):
    return pl.pallas_call(
        nodes_kernel,
        in_specs=whole(1 + len(partial_all)),
        out_specs=whole(1)[0],
        out_shape=jax.ShapeDtypeStruct((matrix.shape[0], partial_all[0].shape[1]), HALF),
        compiler_params=params(TABLE_BYTES),
        name="nodes",
    )(matrix, *partial_all)


def spread_kernel(width, slots, ensemble_ref, select_ref, weight_ref, *refs):
    node_refs, out_refs, values_ref = refs[:slots], refs[slots : slots + 2], refs[slots + 2]
    members, levels, fine = ensemble_ref.shape
    tiles = width // TILE
    steps = fine // width
    feature = members * levels
    nodes = node_refs[0].shape[0]
    pairs = select_ref.shape[1]
    values = jnp.zeros((feature, pairs), FULL)
    for s, piece in enumerate(node_refs):
        values = values + lax.dot_general(
            piece[...],
            select_ref[s * nodes : (s + 1) * nodes, :],
            (((0,), (0,)), ((), ())),
            preferred_element_type=FULL,
        )
    lane = lax.broadcasted_iota(jnp.int32, (feature, LANES), 1)
    group = LANES // tiles
    for i in range(steps):
        first = i // group * LANES
        ends = [values[:, k * pairs // 2 + first : k * pairs // 2 + first + LANES] for k in range(2)]
        left = ends[0]
        for place in range(group):
            shift = (place - i % group) * tiles % LANES
            moved = ends[place % 2] if shift == 0 else pltpu.roll(ends[place % 2], shift, 1)
            left = moved if place == 0 else jnp.where(lane < place * tiles, left, moved)
        values_ref[i] = left.astype(HALF)
    piece = 2 * LANES

    for part in range(2):
        out_ref = out_refs[part]

        def step(j, carry):
            i = j + part * (steps // 2)
            inside = tile_indicator(tiles, width)
            weight = weight_ref[:, pl.ds(pl.multiple_of(i * width, width), width)]
            high = weight.astype(HALF).astype(FULL)
            low = weight - high
            weights = jnp.concatenate(
                [
                    jnp.where(inside, source[k : k + 1, :], 0.0).astype(HALF)
                    for source in (high, low)
                    for k in range(2)
                ],
                axis=0,
            )
            left = values_ref[i]
            for c in range(0, width, piece):
                field = jnp.dot(left, weights[:, c : c + piece], preferred_element_type=FULL)
                field = field.reshape(members, levels, piece)
                span = pl.ds(pl.multiple_of(i * width + c, piece), piece)
                terms = ensemble_ref[:, :, span].astype(FULL) * field
                near = pl.ds(pl.multiple_of(j * width + c, piece), piece)
                out_ref[:, near] = jnp.sum(terms, axis=0).astype(HALF)
            return carry

        lax.fori_loop(0, steps // 2, step, 0)


def run_spread(select, ensemble, interp_weight, nodes_all):
    members, levels, fine, width, steps = column_sizes(ensemble)
    slots = len(nodes_all)
    return pl.pallas_call(
        functools.partial(spread_kernel, width, slots),
        in_specs=whole(3 + slots),
        out_specs=whole(2),
        out_shape=[jax.ShapeDtypeStruct((levels, fine // 2), HALF)] * 2,
        scratch_shapes=[pltpu.VMEM((steps, members * levels, LANES), HALF)],
        compiler_params=params(VMEM_BYTES),
        name="spread",
    )(ensemble, select, interp_weight, *nodes_all)


def add_half(one, two):
    return (one.astype(FULL) + two.astype(FULL)).astype(HALF)


def member_sum(halves):
    size = lax.axis_size("mem")
    masks = [1 << i for i in range(size.bit_length() - 1)]
    orders = [masks, masks[::-1]]
    for step in range(len(masks) - 1):
        moved = [swap(part, "mem", order[step]) for part, order in zip(halves, orders)]
        halves = [add_half(part, other) for part, other in zip(halves, moved)]
    moved = [swap(part, "mem", order[-1]) for part, order in zip(halves, orders)]
    return halves[0], moved[0], halves[1], moved[1]


def per_device(
    increment,
    ensemble,
    climate,
    restrict_dest,
    restrict_local,
    restrict_weight,
    conv_blocks,
    neighbours,
    interp_dest,
    interp_local,
    interp_weight,
):
    myself = lax.axis_index("col")[None]
    members = ensemble.shape[0]
    nodes = ensemble.shape[2] // TILE
    scale = 1.0 / (members * lax.axis_size("mem") - 1)
    weight = restrict_weight[None, :]

    partial_all = gather_slots(run_first(increment, weight, ensemble))
    matrix = run_matrix(
        myself, neighbours, restrict_dest.reshape(1, -1), restrict_local.reshape(1, -1), conv_blocks
    )
    select = run_select(myself, interp_dest.T, interp_local.T, nodes)

    nodes_all = gather_slots(run_nodes(matrix, partial_all))
    sums = member_sum(run_spread(select, ensemble, interp_weight, nodes_all))
    once_applied, partial = run_second(scale, increment, climate, sums, weight, ensemble)
    nodes_all = gather_slots(run_nodes(matrix, gather_slots(partial)))
    sums = member_sum(run_spread(select, ensemble, interp_weight, nodes_all))
    total = jnp.concatenate(
        [sums[2 * i].astype(FULL) + sums[2 * i + 1].astype(FULL) for i in range(2)], axis=1
    )
    return once_applied, climate * once_applied + total * scale


def solution(mesh):
    in_specs = (
        P(None, "col"),
        P("mem", None, "col"),
        P(None, "col"),
        P(),
        P(),
        P("col"),
        P("col", None, None, None),
        P("col", None),
        P(),
        P(),
        P(None, "col"),
    )
    out_specs = (P(None, "col"), P(None, "col"))
    return jax.shard_map(
        per_device, mesh=mesh, in_specs=in_specs, out_specs=out_specs, check_vma=False
    )
```

time: 97.5 us -> 83.6 us (0.86)
  local copies, waits for them, and re-layouts: 9.7 us -> 0.9 us
  waiting for transfers between devices: 37.4 us -> 33.9 us
  Pallas kernels: 17.8 us -> 15.2 us
  starting transfers between devices: 29.3 us -> 31.6 us
    unnamed x35 -> x26, local copies, waits for them, and re-layouts: 8.31 us -> 0.9 us
    ppermute x36, waiting for transfers between devices: 37.4 us -> 33.9 us  [swap(): return lax.ppermute(array, axis, [(i, i ^ mask) for i in range(size)])]
    ppermute x36, starting transfers between devices: 29.3 us -> 31.6 us  [swap(): return lax.ppermute(array, axis, [(i, i ^ mask) for i in range(size)])]
    pallas_call x1 -> x2, Pallas kernels: 2.85 us -> 1.63 us  [the longest x1 1.27 us: run_matrix(): pl.pallas_call(functools.partial(matrix_kernel, slot_masks()), in_specs=[...]
  transfers between devices with their start and end apart: 36 -> 36, of which waited for: 21 -> 20; matrix products, arithmetic and copies ran while one was open for 2% -> 0% of each run, Pallas kernels for 3% -> 2%
where the time goes in v3:
time: 83.6 us; the launch traced here: 83.4 us
  waiting for transfers between devices  33.9 us (41%)
  starting transfers between devices  31.6 us (38%)
  Pallas kernels  15.2 us (18%)
  other arithmetic  1.07 us (1%)
  local copies, waits for them, and re-layouts  0.9 us (1%)
  between operations  0.87 us (1%)
    ppermute x36, waiting for transfers between devices, swap(): return lax.ppermute(array, axis, [(i, i ^ mask) for i in range(size)])  33.9 us
    ppermute x36, starting transfers between devices, swap(): return lax.ppermute(array, axis, [(i, i ^ mask) for i in range(size)])  31.6 us
    pallas_call x2, Pallas kernels, run_spread(): pl.pallas_call(functools.partial(spread_kernel, width, slots), in_specs=w...  6.05 us
    pallas_call x1, Pallas kernels, run_first(): pl.pallas_call(functools.partial(first_kernel, width), in_specs=[pl.Block...  3.7 us
    pallas_call x1, Pallas kernels, run_second(): pl.pallas_call(functools.partial(second_kernel, width, scale), in_specs=w...  2.93 us
  transfers between devices with their start and end apart: 36, of which 20 were waited for; matrix products, arithmetic and copies ran while one was open for 0% of the time, Pallas kernels for 2%

profile of v3, /device:TPU:0, one launch (start us, length us, event | category | flops | bytes accessed | tf_op | source)
XLA Modules:
  0.0 83.4 jit_solution(14018306793640170818)
XLA Ops:
  0.7 0.8 copy-done.4
  1.5 3.7 %tile_sums_first.1.refs_0_ = bf16[256,128]{1,0:T(8,128)(2,1)S(1)} custom-call(f32[8,16384]{1,0:T(8,128)} %state_ref.1, f32[1,16384]{1,0:T(1,128)S(1)} %bitcast.6, bf16[16,8,16384]{2,1,0:T(8,128)(2,1)} %ensemble_ref.5), custom_call_target="tpu_custom_call" | custom-call | tf_op jit(solution)/shard_map/tile_sums_first/pallas_call | solution.py:115
  5.2 5.1 %collective-permute-start.2 = (bf16[256,128]{1,0:T(8,128)(2,1)S(1)}, bf16[256,128]{1,0:T(8,128)(2,1)S(1)}, u32[]{:S(2)}, u32[]{:S(2)}) collective-permute-start(bf16[256,128]{1,0:T(8,128)(2,1)S(1)} %tile_sums_first.1.refs_0_), channel_id=1, source_target_pairs={{0,6},{1,7},{2,4},{3,5},{4,2},{5,3},{6,0},{7,1},{8,14},{9,15},{10,... | collective-permute-start | bytes 196616 | tf_op jit(solution)/shard_map/ppermute | solution.py:21
  10.4 0.6 collective-permute-start
  11.0 1.8 %collective-permute-done.2.refs_3_ = bf16[256,128]{1,0:T(8,128)(2,1)S(1)} collective-permute-done((bf16[256,128]{1,0:T(8,128)(2,1)S(1)}, bf16[256,128]{1,0:T(8,128)(2,1)S(1)}, u32[]{:S(2)}, u32[]{:S(2)}) %collective-permute-start.2) | collective-permute-done | bytes 65568 | tf_op jit(solution)/shard_map/ppermute | solution.py:21
  12.9 3.1 %collective-permute-done.1.refs_2_ = bf16[256,128]{1,0:T(8,128)(2,1)S(1)} collective-permute-done((bf16[256,128]{1,0:T(8,128)(2,1)S(1)}, bf16[256,128]{1,0:T(8,128)(2,1)S(1)}, u32[]{:S(2)}, u32[]{:S(2)}) %collective-permute-start.1) | collective-permute-done | bytes 65568 | tf_op jit(solution)/shard_map/ppermute | solution.py:21
  16.0 0.5 collective-permute-start.4
  16.5 1.3 %node_matrix.1.matrix_ref = bf16[256,2048]{1,0:T(8,128)(2,1)S(1)} custom-call(s32[1]{0:T(128)} %bitcast.1.myself_ref, s32[2,4]{1,0:T(2,128)S(1)} %copy-done.11, s32[1,2048]{1,0:T(1,128)S(1)} %bitcast.10, s32[1,2048]{1,0:T(1,128)S(1)} %bitcast.11, bf16[2,4,128,128]{3,2,1,0:T(8,128)(2,1)S(1)} %copy-done.6), custom_call_target="tpu_custom_call" | custom-call | tf_op jit(solution)/shard_map/node_matrix/pallas_call | solution.py:191
  17.8 0.4 nodes.2.refs_0_
  18.3 2.8 %collective-permute-start.9 = (bf16[256,128]{1,0:T(8,128)(2,1)S(1)}, bf16[256,128]{1,0:T(8,128)(2,1)S(1)}, u32[]{:S(2)}, u32[]{:S(2)}) collective-permute-start(bf16[256,128]{1,0:T(8,128)(2,1)S(1)} %nodes.2.refs_0_), channel_id=1, source_target_pairs={{0,6},{1,7},{2,4},{3,5},{4,2},{5,3},{6,0},{7,1},{8,14},{9,15},{10,... | collective-permute-start | bytes 196616 | tf_op jit(solution)/shard_map/ppermute | solution.py:21
  21.0 1.7 %collective-permute-start.7 = (bf16[256,128]{1,0:T(8,128)(2,1)S(1)}, bf16[256,128]{1,0:T(8,128)(2,1)S(1)}, u32[]{:S(2)}, u32[]{:S(2)}) collective-permute-start(bf16[256,128]{1,0:T(8,128)(2,1)S(1)} %nodes.2.refs_0_), channel_id=1, source_target_pairs={{0,2},{1,3},{2,0},{3,1},{4,6},{5,7},{6,4},{7,5},{8,10},{9,11},{10,... | collective-permute-start | bytes 196616 | tf_op jit(solution)/shard_map/ppermute | solution.py:21
  22.7 2.2 %collective-permute-done.9.refs_3_ = bf16[256,128]{1,0:T(8,128)(2,1)S(1)} collective-permute-done((bf16[256,128]{1,0:T(8,128)(2,1)S(1)}, bf16[256,128]{1,0:T(8,128)(2,1)S(1)}, u32[]{:S(2)}, u32[]{:S(2)}) %collective-permute-start.9) | collective-permute-done | bytes 65568 | tf_op jit(solution)/shard_map/ppermute | solution.py:21
  24.9 2.1 %collective-permute-done.8.refs_2_ = bf16[256,128]{1,0:T(8,128)(2,1)S(1)} collective-permute-done((bf16[256,128]{1,0:T(8,128)(2,1)S(1)}, bf16[256,128]{1,0:T(8,128)(2,1)S(1)}, u32[]{:S(2)}, u32[]{:S(2)}) %collective-permute-start.8) | collective-permute-done | bytes 65568 | tf_op jit(solution)/shard_map/ppermute | solution.py:21
  27.2 0.4 collective-permute-start.11
  27.6 0.4 selection.1.select_ref
  28.0 0.3 collective-permute-done.12.refs_6_
  28.3 0.2 collective-permute-done.11.refs_5_
  28.5 3.0 %spread.2 = (bf16[8,8192]{1,0:T(8,128)(2,1)S(1)}, bf16[8,8192]{1,0:T(8,128)(2,1)S(1)}) custom-call(bf16[16,8,16384]{2,1,0:T(8,128)(2,1)S(1)} %copy-done, bf16[2048,512]{1,0:T(8,128)(2,1)S(1)} %selection.1.select_ref, f32[2,16384]{1,0:T(2,128)S(1)} %copy-done.3, bf16[256,128]{1,0:T(8,128)(2,1)S(1)} %nodes.2.refs_0_, ...), custom_call_target="tpu_custom_call" | custom-call | tf_op jit(solution)/shard_map/spread/pallas_call | solution.py:309
  31.5 1.6 %collective-permute-start.14 = (bf16[8,8192]{1,0:T(8,128)(2,1)S(1)}, bf16[8,8192]{1,0:T(8,128)(2,1)S(1)}, u32[]{:S(2)}, u32[]{:S(2)}) collective-permute-start(bf16[8,8192]{1,0:T(8,128)(2,1)S(1)} %get-tuple-element.8), channel_id=1, source_target_pairs={{0,8},{8,0},{16,24},{24,16},{1,9},{9,1},{17,25},{25,17},{2,10},{10... | collective-permute-start | bytes 393224 | tf_op jit(solution)/shard_map/ppermute | solution.py:21
  33.1 1.5 %collective-permute-start.16 = (bf16[8,8192]{1,0:T(8,128)(2,1)S(1)}, bf16[8,8192]{1,0:T(8,128)(2,1)S(1)}, u32[]{:S(2)}, u32[]{:S(2)}) collective-permute-start(bf16[8,8192]{1,0:T(8,128)(2,1)S(1)} %get-tuple-element.9), channel_id=1, source_target_pairs={{0,16},{8,24},{16,0},{24,8},{1,17},{9,25},{17,1},{25,9},{2,18},{10... | collective-permute-start | bytes 393224 | tf_op jit(solution)/shard_map/ppermute | solution.py:21
  34.6 2.7 %collective-permute-done.14 = bf16[8,8192]{1,0:T(8,128)(2,1)S(1)} collective-permute-done((bf16[8,8192]{1,0:T(8,128)(2,1)S(1)}, bf16[8,8192]{1,0:T(8,128)(2,1)S(1)}, u32[]{:S(2)}, u32[]{:S(2)}) %collective-permute-start.14) | collective-permute-done | bytes 131104 | tf_op jit(solution)/shard_map/ppermute | solution.py:21
  37.4 1.6 %collective-permute-start.15 = (bf16[8,8192]{1,0:T(8,128)(2,1)S(1)}, bf16[8,8192]{1,0:T(8,128)(2,1)S(1)}, u32[]{:S(2)}, u32[]{:S(2)}) collective-permute-start(bf16[8,8192]{1,0:T(8,128)(2,1)S(1)} %add_convert_fusion.3.refs_0_), channel_id=1, source_target_pairs={{0,16},{8,24},{16,0},{24,8},{1,17},{9,25},{17,1},{25,9},{2,18},{10... | collective-permute-start | bytes 393224 | tf_op jit(solution)/shard_map/ppermute | solution.py:21
  39.0 1.6 %collective-permute-start.17 = (bf16[8,8192]{1,0:T(8,128)(2,1)S(1)}, bf16[8,8192]{1,0:T(8,128)(2,1)S(1)}, u32[]{:S(2)}, u32[]{:S(2)}) collective-permute-start(bf16[8,8192]{1,0:T(8,128)(2,1)S(1)} %add_convert_fusion.2.refs_2_), channel_id=1, source_target_pairs={{0,8},{8,0},{16,24},{24,16},{1,9},{9,1},{17,25},{25,17},{2,10},{10... | collective-permute-start | bytes 393224 | tf_op jit(solution)/shard_map/ppermute | solution.py:21
  40.6 1.8 %collective-permute-done.15.refs_1_ = bf16[8,8192]{1,0:T(8,128)(2,1)S(1)} collective-permute-done((bf16[8,8192]{1,0:T(8,128)(2,1)S(1)}, bf16[8,8192]{1,0:T(8,128)(2,1)S(1)}, u32[]{:S(2)}, u32[]{:S(2)}) %collective-permute-start.15) | collective-permute-done | bytes 131104 | tf_op jit(solution)/shard_map/ppermute | solution.py:21
  42.4 1.6 %collective-permute-done.17.refs_3_ = bf16[8,8192]{1,0:T(8,128)(2,1)S(1)} collective-permute-done((bf16[8,8192]{1,0:T(8,128)(2,1)S(1)}, bf16[8,8192]{1,0:T(8,128)(2,1)S(1)}, u32[]{:S(2)}, u32[]{:S(2)}) %collective-permute-start.17) | collective-permute-done | bytes 131104 | tf_op jit(solution)/shard_map/ppermute | solution.py:21
  44.0 2.9 %tile_sums_second.1 = (f32[8,16384]{1,0:T(8,128)}, bf16[256,128]{1,0:T(8,128)(2,1)S(1)}) custom-call(bf16[16,8,16384]{2,1,0:T(8,128)(2,1)S(1)} %copy-done, f32[8,16384]{1,0:T(8,128)S(1)} %copy-done.1, f32[8,16384]{1,0:T(8,128)S(1)} %copy-done.2, f32[1,16384]{1,0:T(1,128)S(1)} %bitcast.7, bf16[8,8192]{1,0:T(8,128)(2,1)S(1)} %add_convert_fusion.3.refs_0_, ...), custom_call_target="tpu_custom_call" | custom-call | tf_op jit(solution)/shard_map/tile_sums_second/pallas_call | solution.py:155
  47.0 2.5 %collective-permute-start.20 = (bf16[256,128]{1,0:T(8,128)(2,1)S(1)}, bf16[256,128]{1,0:T(8,128)(2,1)S(1)}, u32[]{:S(2)}, u32[]{:S(2)}) collective-permute-start(bf16[256,128]{1,0:T(8,128)(2,1)S(1)} %get-tuple-element.11.refs_0_), channel_id=1, source_target_pairs={{0,6},{1,7},{2,4},{3,5},{4,2},{5,3},{6,0},{7,1},{8,14},{9,15},{10,... | collective-permute-start | bytes 196616 | tf_op jit(solution)/shard_map/ppermute | solution.py:21
  49.5 1.8 %collective-permute-start.18 = (bf16[256,128]{1,0:T(8,128)(2,1)S(1)}, bf16[256,128]{1,0:T(8,128)(2,1)S(1)}, u32[]{:S(2)}, u32[]{:S(2)}) collective-permute-start(bf16[256,128]{1,0:T(8,128)(2,1)S(1)} %get-tuple-element.11.refs_0_), channel_id=1, source_target_pairs={{0,2},{1,3},{2,0},{3,1},{4,6},{5,7},{6,4},{7,5},{8,10},{9,11},{10,... | collective-permute-start | bytes 196616 | tf_op jit(solution)/shard_map/ppermute | solution.py:21
  51.4 2.4 %collective-permute-done.20.refs_3_ = bf16[256,128]{1,0:T(8,128)(2,1)S(1)} collective-permute-done((bf16[256,128]{1,0:T(8,128)(2,1)S(1)}, bf16[256,128]{1,0:T(8,128)(2,1)S(1)}, u32[]{:S(2)}, u32[]{:S(2)}) %collective-permute-start.20) | collective-permute-done | bytes 65568 | tf_op jit(solution)/shard_map/ppermute | solution.py:21
  53.8 1.3 %collective-permute-done.19.refs_2_ = bf16[256,128]{1,0:T(8,128)(2,1)S(1)} collective-permute-done((bf16[256,128]{1,0:T(8,128)(2,1)S(1)}, bf16[256,128]{1,0:T(8,128)(2,1)S(1)}, u32[]{:S(2)}, u32[]{:S(2)}) %collective-permute-start.19) | collective-permute-done | bytes 65568 | tf_op jit(solution)/shard_map/ppermute | solution.py:21
  55.1 0.5 collective-permute-start.22
  55.6 0.7 collective-permute-done.23.refs_6_
  56.5 0.4 nodes.3.refs_0_
  56.9 2.2 %collective-permute-start.27 = (bf16[256,128]{1,0:T(8,128)(2,1)S(1)}, bf16[256,128]{1,0:T(8,128)(2,1)S(1)}, u32[]{:S(2)}, u32[]{:S(2)}) collective-permute-start(bf16[256,128]{1,0:T(8,128)(2,1)S(1)} %nodes.3.refs_0_), channel_id=1, source_target_pairs={{0,6},{1,7},{2,4},{3,5},{4,2},{5,3},{6,0},{7,1},{8,14},{9,15},{10,... | collective-permute-start | bytes 196616 | tf_op jit(solution)/shard_map/ppermute | solution.py:21
  59.1 2.3 %collective-permute-start.25 = (bf16[256,128]{1,0:T(8,128)(2,1)S(1)}, bf16[256,128]{1,0:T(8,128)(2,1)S(1)}, u32[]{:S(2)}, u32[]{:S(2)}) collective-permute-start(bf16[256,128]{1,0:T(8,128)(2,1)S(1)} %nodes.3.refs_0_), channel_id=1, source_target_pairs={{0,2},{1,3},{2,0},{3,1},{4,6},{5,7},{6,4},{7,5},{8,10},{9,11},{10,... | collective-permute-start | bytes 196616 | tf_op jit(solution)/shard_map/ppermute | solution.py:21
  61.4 2.5 %collective-permute-done.27.refs_3_ = bf16[256,128]{1,0:T(8,128)(2,1)S(1)} collective-permute-done((bf16[256,128]{1,0:T(8,128)(2,1)S(1)}, bf16[256,128]{1,0:T(8,128)(2,1)S(1)}, u32[]{:S(2)}, u32[]{:S(2)}) %collective-permute-start.27) | collective-permute-done | bytes 65568 | tf_op jit(solution)/shard_map/ppermute | solution.py:21
  63.9 2.1 %collective-permute-done.26.refs_2_ = bf16[256,128]{1,0:T(8,128)(2,1)S(1)} collective-permute-done((bf16[256,128]{1,0:T(8,128)(2,1)S(1)}, bf16[256,128]{1,0:T(8,128)(2,1)S(1)}, u32[]{:S(2)}, u32[]{:S(2)}) %collective-permute-start.26) | collective-permute-done | bytes 65568 | tf_op jit(solution)/shard_map/ppermute | solution.py:21
  66.0 0.5 collective-permute-start.29
  66.5 0.7 collective-permute-done.30.refs_6_
  67.4 3.0 %spread.3 = (bf16[8,8192]{1,0:T(8,128)(2,1)S(1)}, bf16[8,8192]{1,0:T(8,128)(2,1)S(1)}) custom-call(bf16[16,8,16384]{2,1,0:T(8,128)(2,1)S(1)} %copy-done, bf16[2048,512]{1,0:T(8,128)(2,1)S(1)} %selection.1.select_ref, f32[2,16384]{1,0:T(2,128)S(1)} %copy-done.3, bf16[256,128]{1,0:T(8,128)(2,1)S(1)} %nodes.3.refs_0_, ...), custom_call_target="tpu_custom_call" | custom-call | tf_op jit(solution)/shard_map/spread/pallas_call | solution.py:309
  70.4 1.6 %collective-permute-start.32 = (bf16[8,8192]{1,0:T(8,128)(2,1)S(1)}, bf16[8,8192]{1,0:T(8,128)(2,1)S(1)}, u32[]{:S(2)}, u32[]{:S(2)}) collective-permute-start(bf16[8,8192]{1,0:T(8,128)(2,1)S(1)} %get-tuple-element.12), channel_id=1, source_target_pairs={{0,8},{8,0},{16,24},{24,16},{1,9},{9,1},{17,25},{25,17},{2,10},{10... | collective-permute-start | bytes 393224 | tf_op jit(solution)/shard_map/ppermute | solution.py:21
  72.0 0.5 collective-permute-start.34
  72.5 3.8 %collective-permute-done.32 = bf16[8,8192]{1,0:T(8,128)(2,1)S(1)} collective-permute-done((bf16[8,8192]{1,0:T(8,128)(2,1)S(1)}, bf16[8,8192]{1,0:T(8,128)(2,1)S(1)}, u32[]{:S(2)}, u32[]{:S(2)}) %collective-permute-start.32) | collective-permute-done | bytes 131104 | tf_op jit(solution)/shard_map/ppermute | solution.py:21
  76.3 1.2 %collective-permute-start.33 = (bf16[8,8192]{1,0:T(8,128)(2,1)S(1)}, bf16[8,8192]{1,0:T(8,128)(2,1)S(1)}, u32[]{:S(2)}, u32[]{:S(2)}) collective-permute-start(bf16[8,8192]{1,0:T(8,128)(2,1)S(1)} %add_convert_fusion.1), channel_id=1, source_target_pairs={{0,16},{8,24},{16,0},{24,8},{1,17},{9,25},{17,1},{25,9},{2,18},{10... | collective-permute-start | bytes 393224 | tf_op jit(solution)/shard_map/ppermute | solution.py:21
  77.5 1.0 %collective-permute-start.35 = (bf16[8,8192]{1,0:T(8,128)(2,1)S(1)}, bf16[8,8192]{1,0:T(8,128)(2,1)S(1)}, u32[]{:S(2)}, u32[]{:S(2)}) collective-permute-start(bf16[8,8192]{1,0:T(8,128)(2,1)S(1)} %add_convert_fusion), channel_id=1, source_target_pairs={{0,8},{8,0},{16,24},{24,16},{1,9},{9,1},{17,25},{25,17},{2,10},{10... | collective-permute-start | bytes 393224 | tf_op jit(solution)/shard_map/ppermute | solution.py:21
  78.4 2.9 %collective-permute-done.33 = bf16[8,8192]{1,0:T(8,128)(2,1)S(1)} collective-permute-done((bf16[8,8192]{1,0:T(8,128)(2,1)S(1)}, bf16[8,8192]{1,0:T(8,128)(2,1)S(1)}, u32[]{:S(2)}, u32[]{:S(2)}) %collective-permute-start.33) | collective-permute-done | bytes 131104 | tf_op jit(solution)/shard_map/ppermute | solution.py:21
  81.3 1.2 %collective-permute-done.35 = bf16[8,8192]{1,0:T(8,128)(2,1)S(1)} collective-permute-done((bf16[8,8192]{1,0:T(8,128)(2,1)S(1)}, bf16[8,8192]{1,0:T(8,128)(2,1)S(1)}, u32[]{:S(2)}, u32[]{:S(2)}) %collective-permute-start.35) | collective-permute-done | bytes 131104 | tf_op jit(solution)/shard_map/ppermute | solution.py:21
  82.5 0.9 %fusion = f32[8,16384]{1,0:T(8,128)} fusion(f32[8,8192]{1,0:T(8,128)S(1)} %convert_add_fusion, f32[8,8192]{1,0:T(8,128)S(1)} %convert_add_fusion.1, f32[8,16384]{1,0:T(8,128)S(1)} %copy-done.2, f32[8,16384]{1,0:T(8,128)S(1)} %copy-done.12), kind=kLoop, calls=%fused_computation.1 | loop fusion | flops 524288 | bytes 2097152 | tf_op jit(solution)/shard_map/add | solution.py:368
  (65 shorter events, 0.8 us)
Async XLA Ops:
  0.6 15.9 %copy-start.11 = (s32[2,4]{1,0:T(2,128)S(1)}, s32[2,4]{1,0:T(2,128)}, u32[]{:S(2)}) copy-start(s32[2,4]{1,0:T(2,128)} %near_ref.1) | copy-start | bytes 100
  1.5 15.0 %copy-start.6 = (bf16[2,4,128,128]{3,2,1,0:T(8,128)(2,1)S(1)}, bf16[2,4,128,128]{3,2,1,0:T(8,128)(2,1)}, u32[]{:S(2)}) copy-start(bf16[2,4,128,128]{3,2,1,0:T(8,128)(2,1)} %conv_ref.1) | copy-start | bytes 786436
  1.5 15.0 %copy-start.9 = (s32[2048,1]{0,1:T(1,128)S(1)}, s32[2048,1]{0,1:T(1,128)}, u32[]{:S(2)}) copy-start(s32[2048,1]{0,1:T(1,128)} %param.14) | copy-start | bytes 24580
  1.5 15.0 %copy-start.10 = (s32[2048]{0:T(1024)S(1)}, s32[2048]{0:T(1024)}, u32[]{:S(2)}) copy-start(s32[2048]{0:T(1024)} %param.15) | copy-start | bytes 24580
  1.5 26.1 %copy-start.7 = (s32[2048,2]{0,1:T(2,128)S(1)}, s32[2048,2]{0,1:T(2,128)}, u32[]{:S(2)}) copy-start(s32[2048,2]{0,1:T(2,128)} %param.19) | copy-start | bytes 49156
  1.5 26.1 %copy-start.8 = (s32[2048,2]{0,1:T(2,128)S(1)}, s32[2048,2]{0,1:T(2,128)}, u32[]{:S(2)}) copy-start(s32[2048,2]{0,1:T(2,128)} %param.20) | copy-start | bytes 49156
  1.5 27.0 %copy-start.3 = (f32[2,16384]{1,0:T(2,128)S(1)}, f32[2,16384]{1,0:T(2,128)}, u32[]{:S(2)}) copy-start(f32[2,16384]{1,0:T(2,128)} %weight_ref.3) | copy-start | bytes 393220
  5.2 7.6 %collective-permute-start.2 = (bf16[256,128]{1,0:T(8,128)(2,1)S(1)}, bf16[256,128]{1,0:T(8,128)(2,1)S(1)}, u32[]{:S(2)}, u32[]{:S(2)}) collective-permute-start(bf16[256,128]{1,0:T(8,128)(2,1)S(1)} %tile_sums_first.1.refs_0_), channel_id=1, source_target_pairs={{0,6},{1,7},{2,4},{3,5},{4,2},{5,3},{6,0},{7,1},{8,14},{9,15},{10,... | collective-permute-start | bytes 196616 | tf_op jit(solution)/shard_map/ppermute | solution.py:21
  10.4 5.6 %collective-permute-start.1 = (bf16[256,128]{1,0:T(8,128)(2,1)S(1)}, bf16[256,128]{1,0:T(8,128)(2,1)S(1)}, u32[]{:S(2)}, u32[]{:S(2)}) collective-permute-start(bf16[256,128]{1,0:T(8,128)(2,1)S(1)} %tile_sums_first.1.refs_0_), channel_id=1, source_target_pairs={{0,4},{1,5},{2,6},{3,7},{4,0},{5,1},{6,2},{7,3},{8,12},{9,13},{10,... | collective-permute-start | bytes 196616 | tf_op jit(solution)/shard_map/ppermute | solution.py:21
  10.4 5.6 %collective-permute-start = (bf16[256,128]{1,0:T(8,128)(2,1)S(1)}, bf16[256,128]{1,0:T(8,128)(2,1)S(1)}, u32[]{:S(2)}, u32[]{:S(2)}) collective-permute-start(bf16[256,128]{1,0:T(8,128)(2,1)S(1)} %tile_sums_first.1.refs_0_), channel_id=1, source_target_pairs={{0,2},{1,3},{2,0},{3,1},{4,6},{5,7},{6,4},{7,5},{8,10},{9,11},{10,... | collective-permute-start | bytes 196616 | tf_op jit(solution)/shard_map/ppermute | solution.py:21
  11.0 6.8 %collective-permute-start.3 = (bf16[256,128]{1,0:T(8,128)(2,1)S(1)}, bf16[256,128]{1,0:T(8,128)(2,1)S(1)}, u32[]{:S(2)}, u32[]{:S(2)}) collective-permute-start(bf16[256,128]{1,0:T(8,128)(2,1)S(1)} %tile_sums_first.1.refs_0_), channel_id=1, source_target_pairs={{0,1},{1,0},{2,3},{3,2},{4,5},{5,4},{6,7},{7,6},{8,9},{9,8},{10,11... | collective-permute-start | bytes 196616 | tf_op jit(solution)/shard_map/ppermute | solution.py:21
  12.8 4.9 %collective-permute-start.6 = (bf16[256,128]{1,0:T(8,128)(2,1)S(1)}, bf16[256,128]{1,0:T(8,128)(2,1)S(1)}, u32[]{:S(2)}, u32[]{:S(2)}) collective-permute-start(bf16[256,128]{1,0:T(8,128)(2,1)S(1)} %collective-permute-done.2.refs_3_), channel_id=1, source_target_pairs={{0,1},{1,0},{2,3},{3,2},{4,5},{5,4},{6,7},{7,6},{8,9},{9,8},{10,11... | collective-permute-start | bytes 196616 | tf_op jit(solution)/shard_map/ppermute | solution.py:21
  16.0 1.8 %collective-permute-start.5 = (bf16[256,128]{1,0:T(8,128)(2,1)S(1)}, bf16[256,128]{1,0:T(8,128)(2,1)S(1)}, u32[]{:S(2)}, u32[]{:S(2)}) collective-permute-start(bf16[256,128]{1,0:T(8,128)(2,1)S(1)} %collective-permute-done.1.refs_2_), channel_id=1, source_target_pairs={{0,1},{1,0},{2,3},{3,2},{4,5},{5,4},{6,7},{7,6},{8,9},{9,8},{10,11... | collective-permute-start | bytes 196616 | tf_op jit(solution)/shard_map/ppermute | solution.py:21
  16.0 1.8 %collective-permute-start.4 = (bf16[256,128]{1,0:T(8,128)(2,1)S(1)}, bf16[256,128]{1,0:T(8,128)(2,1)S(1)}, u32[]{:S(2)}, u32[]{:S(2)}) collective-permute-start(bf16[256,128]{1,0:T(8,128)(2,1)S(1)} %collective-permute-done.refs_1_), channel_id=1, source_target_pairs={{0,1},{1,0},{2,3},{3,2},{4,5},{5,4},{6,7},{7,6},{8,9},{9,8},{10,11... | collective-permute-start | bytes 196616 | tf_op jit(solution)/shard_map/ppermute | solution.py:21
  16.5 12.0 %copy-start = (bf16[16,8,16384]{2,1,0:T(8,128)(2,1)S(1)}, bf16[16,8,16384]{2,1,0:T(8,128)(2,1)}, u32[]{:S(2)}) copy-start(bf16[16,8,16384]{2,1,0:T(8,128)(2,1)} %ensemble_ref.5) | copy-start | bytes 12582916
  18.3 6.7 %collective-permute-start.9 = (bf16[256,128]{1,0:T(8,128)(2,1)S(1)}, bf16[256,128]{1,0:T(8,128)(2,1)S(1)}, u32[]{:S(2)}, u32[]{:S(2)}) collective-permute-start(bf16[256,128]{1,0:T(8,128)(2,1)S(1)} %nodes.2.refs_0_), channel_id=1, source_target_pairs={{0,6},{1,7},{2,4},{3,5},{4,2},{5,3},{6,0},{7,1},{8,14},{9,15},{10,... | collective-permute-start | bytes 196616 | tf_op jit(solution)/shard_map/ppermute | solution.py:21
  21.0 6.0 %collective-permute-start.8 = (bf16[256,128]{1,0:T(8,128)(2,1)S(1)}, bf16[256,128]{1,0:T(8,128)(2,1)S(1)}, u32[]{:S(2)}, u32[]{:S(2)}) collective-permute-start(bf16[256,128]{1,0:T(8,128)(2,1)S(1)} %nodes.2.refs_0_), channel_id=1, source_target_pairs={{0,4},{1,5},{2,6},{3,7},{4,0},{5,1},{6,2},{7,3},{8,12},{9,13},{10,... | collective-permute-start | bytes 196616 | tf_op jit(solution)/shard_map/ppermute | solution.py:21
  21.0 6.1 %collective-permute-start.7 = (bf16[256,128]{1,0:T(8,128)(2,1)S(1)}, bf16[256,128]{1,0:T(8,128)(2,1)S(1)}, u32[]{:S(2)}, u32[]{:S(2)}) collective-permute-start(bf16[256,128]{1,0:T(8,128)(2,1)S(1)} %nodes.2.refs_0_), channel_id=1, source_target_pairs={{0,2},{1,3},{2,0},{3,1},{4,6},{5,7},{6,4},{7,5},{8,10},{9,11},{10,... | collective-permute-start | bytes 196616 | tf_op jit(solution)/shard_map/ppermute | solution.py:21
  22.7 5.3 %collective-permute-start.10 = (bf16[256,128]{1,0:T(8,128)(2,1)S(1)}, bf16[256,128]{1,0:T(8,128)(2,1)S(1)}, u32[]{:S(2)}, u32[]{:S(2)}) collective-permute-start(bf16[256,128]{1,0:T(8,128)(2,1)S(1)} %nodes.2.refs_0_), channel_id=1, source_target_pairs={{0,1},{1,0},{2,3},{3,2},{4,5},{5,4},{6,7},{7,6},{8,9},{9,8},{10,11... | collective-permute-start | bytes 196616 | tf_op jit(solution)/shard_map/ppermute | solution.py:21
  24.9 3.0 %collective-permute-start.13 = (bf16[256,128]{1,0:T(8,128)(2,1)S(1)}, bf16[256,128]{1,0:T(8,128)(2,1)S(1)}, u32[]{:S(2)}, u32[]{:S(2)}) collective-permute-start(bf16[256,128]{1,0:T(8,128)(2,1)S(1)} %collective-permute-done.9.refs_3_), channel_id=1, source_target_pairs={{0,1},{1,0},{2,3},{3,2},{4,5},{5,4},{6,7},{7,6},{8,9},{9,8},{10,11... | collective-permute-start | bytes 196616 | tf_op jit(solution)/shard_map/ppermute | solution.py:21
  27.0 1.3 %collective-permute-start.12 = (bf16[256,128]{1,0:T(8,128)(2,1)S(1)}, bf16[256,128]{1,0:T(8,128)(2,1)S(1)}, u32[]{:S(2)}, u32[]{:S(2)}) collective-permute-start(bf16[256,128]{1,0:T(8,128)(2,1)S(1)} %collective-permute-done.8.refs_2_), channel_id=1, source_target_pairs={{0,1},{1,0},{2,3},{3,2},{4,5},{5,4},{6,7},{7,6},{8,9},{9,8},{10,11... | collective-permute-start | bytes 196616 | tf_op jit(solution)/shard_map/ppermute | solution.py:21
  27.2 1.3 %collective-permute-start.11 = (bf16[256,128]{1,0:T(8,128)(2,1)S(1)}, bf16[256,128]{1,0:T(8,128)(2,1)S(1)}, u32[]{:S(2)}, u32[]{:S(2)}) collective-permute-start(bf16[256,128]{1,0:T(8,128)(2,1)S(1)} %collective-permute-done.7.refs_1_), channel_id=1, source_target_pairs={{0,1},{1,0},{2,3},{3,2},{4,5},{5,4},{6,7},{7,6},{8,9},{9,8},{10,11... | collective-permute-start | bytes 196616 | tf_op jit(solution)/shard_map/ppermute | solution.py:21
  27.9 16.1 %copy-start.1 = (f32[8,16384]{1,0:T(8,128)S(1)}, f32[8,16384]{1,0:T(8,128)}, u32[]{:S(2)}) copy-start(f32[8,16384]{1,0:T(8,128)} %state_ref.1) | copy-start | bytes 1572868
  27.9 16.1 %copy-start.2 = (f32[8,16384]{1,0:T(8,128)S(1)}, f32[8,16384]{1,0:T(8,128)}, u32[]{:S(2)}) copy-start(f32[8,16384]{1,0:T(8,128)} %climate_ref.1) | copy-start | bytes 1572868
  28.0 16.1 %copy-start.5 = (f32[16384]{0:T(1024)S(1)}, f32[16384]{0:T(1024)}, u32[]{:S(2)}) copy-start(f32[16384]{0:T(1024)} %param.16) | copy-start | bytes 196612
  31.5 5.8 %collective-permute-start.14 = (bf16[8,8192]{1,0:T(8,128)(2,1)S(1)}, bf16[8,8192]{1,0:T(8,128)(2,1)S(1)}, u32[]{:S(2)}, u32[]{:S(2)}) collective-permute-start(bf16[8,8192]{1,0:T(8,128)(2,1)S(1)} %get-tuple-element.8), channel_id=1, source_target_pairs={{0,8},{8,0},{16,24},{24,16},{1,9},{9,1},{17,25},{25,17},{2,10},{10... | collective-permute-start | bytes 393224 | tf_op jit(solution)/shard_map/ppermute | solution.py:21
  33.1 5.9 %collective-permute-start.16 = (bf16[8,8192]{1,0:T(8,128)(2,1)S(1)}, bf16[8,8192]{1,0:T(8,128)(2,1)S(1)}, u32[]{:S(2)}, u32[]{:S(2)}) collective-permute-start(bf16[8,8192]{1,0:T(8,128)(2,1)S(1)} %get-tuple-element.9), channel_id=1, source_target_pairs={{0,16},{8,24},{16,0},{24,8},{1,17},{9,25},{17,1},{25,9},{2,18},{10... | collective-permute-start | bytes 393224 | tf_op jit(solution)/shard_map/ppermute | solution.py:21
  37.4 5.0 %collective-permute-start.15 = (bf16[8,8192]{1,0:T(8,128)(2,1)S(1)}, bf16[8,8192]{1,0:T(8,128)(2,1)S(1)}, u32[]{:S(2)}, u32[]{:S(2)}) collective-permute-start(bf16[8,8192]{1,0:T(8,128)(2,1)S(1)} %add_convert_fusion.3.refs_0_), channel_id=1, source_target_pairs={{0,16},{8,24},{16,0},{24,8},{1,17},{9,25},{17,1},{25,9},{2,18},{10... | collective-permute-start | bytes 393224 | tf_op jit(solution)/shard_map/ppermute | solution.py:21
  39.0 5.0 %collective-permute-start.17 = (bf16[8,8192]{1,0:T(8,128)(2,1)S(1)}, bf16[8,8192]{1,0:T(8,128)(2,1)S(1)}, u32[]{:S(2)}, u32[]{:S(2)}) collective-permute-start(bf16[8,8192]{1,0:T(8,128)(2,1)S(1)} %add_convert_fusion.2.refs_2_), channel_id=1, source_target_pairs={{0,8},{8,0},{16,24},{24,16},{1,9},{9,1},{17,25},{25,17},{2,10},{10... | collective-permute-start | bytes 393224 | tf_op jit(solution)/shard_map/ppermute | solution.py:21
  47.0 6.8 %collective-permute-start.20 = (bf16[256,128]{1,0:T(8,128)(2,1)S(1)}, bf16[256,128]{1,0:T(8,128)(2,1)S(1)}, u32[]{:S(2)}, u32[]{:S(2)}) collective-permute-start(bf16[256,128]{1,0:T(8,128)(2,1)S(1)} %get-tuple-element.11.refs_0_), channel_id=1, source_target_pairs={{0,6},{1,7},{2,4},{3,5},{4,2},{5,3},{6,0},{7,1},{8,14},{9,15},{10,... | collective-permute-start | bytes 196616 | tf_op jit(solution)/shard_map/ppermute | solution.py:21
  49.5 5.6 %collective-permute-start.19 = (bf16[256,128]{1,0:T(8,128)(2,1)S(1)}, bf16[256,128]{1,0:T(8,128)(2,1)S(1)}, u32[]{:S(2)}, u32[]{:S(2)}) collective-permute-start(bf16[256,128]{1,0:T(8,128)(2,1)S(1)} %get-tuple-element.11.refs_0_), channel_id=1, source_target_pairs={{0,4},{1,5},{2,6},{3,7},{4,0},{5,1},{6,2},{7,3},{8,12},{9,13},{10,... | collective-permute-start | bytes 196616 | tf_op jit(solution)/shard_map/ppermute | solution.py:21
  49.5 5.6 %collective-permute-start.18 = (bf16[256,128]{1,0:T(8,128)(2,1)S(1)}, bf16[256,128]{1,0:T(8,128)(2,1)S(1)}, u32[]{:S(2)}, u32[]{:S(2)}) collective-permute-start(bf16[256,128]{1,0:T(8,128)(2,1)S(1)} %get-tuple-element.11.refs_0_), channel_id=1, source_target_pairs={{0,2},{1,3},{2,0},{3,1},{4,6},{5,7},{6,4},{7,5},{8,10},{9,11},{10,... | collective-permute-start | bytes 196616 | tf_op jit(solution)/shard_map/ppermute | solution.py:21
  51.4 4.2 %collective-permute-start.21 = (bf16[256,128]{1,0:T(8,128)(2,1)S(1)}, bf16[256,128]{1,0:T(8,128)(2,1)S(1)}, u32[]{:S(2)}, u32[]{:S(2)}) collective-permute-start(bf16[256,128]{1,0:T(8,128)(2,1)S(1)} %get-tuple-element.11.refs_0_), channel_id=1, source_target_pairs={{0,1},{1,0},{2,3},{3,2},{4,5},{5,4},{6,7},{7,6},{8,9},{9,8},{10,11... | collective-permute-start | bytes 196616 | tf_op jit(solution)/shard_map/ppermute | solution.py:21
  53.8 1.8 %collective-permute-start.24 = (bf16[256,128]{1,0:T(8,128)(2,1)S(1)}, bf16[256,128]{1,0:T(8,128)(2,1)S(1)}, u32[]{:S(2)}, u32[]{:S(2)}) collective-permute-start(bf16[256,128]{1,0:T(8,128)(2,1)S(1)} %collective-permute-done.20.refs_3_), channel_id=1, source_target_pairs={{0,1},{1,0},{2,3},{3,2},{4,5},{5,4},{6,7},{7,6},{8,9},{9,8},{10,11... | collective-permute-start | bytes 196616 | tf_op jit(solution)/shard_map/ppermute | solution.py:21
  55.1 1.3 %collective-permute-start.23 = (bf16[256,128]{1,0:T(8,128)(2,1)S(1)}, bf16[256,128]{1,0:T(8,128)(2,1)S(1)}, u32[]{:S(2)}, u32[]{:S(2)}) collective-permute-start(bf16[256,128]{1,0:T(8,128)(2,1)S(1)} %collective-permute-done.19.refs_2_), channel_id=1, source_target_pairs={{0,1},{1,0},{2,3},{3,2},{4,5},{5,4},{6,7},{7,6},{8,9},{9,8},{10,11... | collective-permute-start | bytes 196616 | tf_op jit(solution)/shard_map/ppermute | solution.py:21
  55.1 1.4 %collective-permute-start.22 = (bf16[256,128]{1,0:T(8,128)(2,1)S(1)}, bf16[256,128]{1,0:T(8,128)(2,1)S(1)}, u32[]{:S(2)}, u32[]{:S(2)}) collective-permute-start(bf16[256,128]{1,0:T(8,128)(2,1)S(1)} %collective-permute-done.18.refs_1_), channel_id=1, source_target_pairs={{0,1},{1,0},{2,3},{3,2},{4,5},{5,4},{6,7},{7,6},{8,9},{9,8},{10,11... | collective-permute-start | bytes 196616 | tf_op jit(solution)/shard_map/ppermute | solution.py:21
  56.9 25.6 %copy-start.12 = (f32[8,16384]{1,0:T(8,128)S(1)}, f32[8,16384]{1,0:T(8,128)}, u32[]{:S(2)}) copy-start(f32[8,16384]{1,0:T(8,128)} %get-tuple-element.6) | copy-start | bytes 1572868
  56.9 6.9 %collective-permute-start.27 = (bf16[256,128]{1,0:T(8,128)(2,1)S(1)}, bf16[256,128]{1,0:T(8,128)(2,1)S(1)}, u32[]{:S(2)}, u32[]{:S(2)}) collective-permute-start(bf16[256,128]{1,0:T(8,128)(2,1)S(1)} %nodes.3.refs_0_), channel_id=1, source_target_pairs={{0,6},{1,7},{2,4},{3,5},{4,2},{5,3},{6,0},{7,1},{8,14},{9,15},{10,... | collective-permute-start | bytes 196616 | tf_op jit(solution)/shard_map/ppermute | solution.py:21
  59.1 6.9 %collective-permute-start.26 = (bf16[256,128]{1,0:T(8,128)(2,1)S(1)}, bf16[256,128]{1,0:T(8,128)(2,1)S(1)}, u32[]{:S(2)}, u32[]{:S(2)}) collective-permute-start(bf16[256,128]{1,0:T(8,128)(2,1)S(1)} %nodes.3.refs_0_), channel_id=1, source_target_pairs={{0,4},{1,5},{2,6},{3,7},{4,0},{5,1},{6,2},{7,3},{8,12},{9,13},{10,... | collective-permute-start | bytes 196616 | tf_op jit(solution)/shard_map/ppermute | solution.py:21
  59.1 6.9 %collective-permute-start.25 = (bf16[256,128]{1,0:T(8,128)(2,1)S(1)}, bf16[256,128]{1,0:T(8,128)(2,1)S(1)}, u32[]{:S(2)}, u32[]{:S(2)}) collective-permute-start(bf16[256,128]{1,0:T(8,128)(2,1)S(1)} %nodes.3.refs_0_), channel_id=1, source_target_pairs={{0,2},{1,3},{2,0},{3,1},{4,6},{5,7},{6,4},{7,5},{8,10},{9,11},{10,... | collective-permute-start | bytes 196616 | tf_op jit(solution)/shard_map/ppermute | solution.py:21
  61.4 5.1 %collective-permute-start.28 = (bf16[256,128]{1,0:T(8,128)(2,1)S(1)}, bf16[256,128]{1,0:T(8,128)(2,1)S(1)}, u32[]{:S(2)}, u32[]{:S(2)}) collective-permute-start(bf16[256,128]{1,0:T(8,128)(2,1)S(1)} %nodes.3.refs_0_), channel_id=1, source_target_pairs={{0,1},{1,0},{2,3},{3,2},{4,5},{5,4},{6,7},{7,6},{8,9},{9,8},{10,11... | collective-permute-start | bytes 196616 | tf_op jit(solution)/shard_map/ppermute | solution.py:21
  63.9 2.6 %collective-permute-start.31 = (bf16[256,128]{1,0:T(8,128)(2,1)S(1)}, bf16[256,128]{1,0:T(8,128)(2,1)S(1)}, u32[]{:S(2)}, u32[]{:S(2)}) collective-permute-start(bf16[256,128]{1,0:T(8,128)(2,1)S(1)} %collective-permute-done.27.refs_3_), channel_id=1, source_target_pairs={{0,1},{1,0},{2,3},{3,2},{4,5},{5,4},{6,7},{7,6},{8,9},{9,8},{10,11... | collective-permute-start | bytes 196616 | tf_op jit(solution)/shard_map/ppermute | solution.py:21
  66.0 1.3 %collective-permute-start.30 = (bf16[256,128]{1,0:T(8,128)(2,1)S(1)}, bf16[256,128]{1,0:T(8,128)(2,1)S(1)}, u32[]{:S(2)}, u32[]{:S(2)}) collective-permute-start(bf16[256,128]{1,0:T(8,128)(2,1)S(1)} %collective-permute-done.26.refs_2_), channel_id=1, source_target_pairs={{0,1},{1,0},{2,3},{3,2},{4,5},{5,4},{6,7},{7,6},{8,9},{9,8},{10,11... | collective-permute-start | bytes 196616 | tf_op jit(solution)/shard_map/ppermute | solution.py:21
  66.0 1.4 %collective-permute-start.29 = (bf16[256,128]{1,0:T(8,128)(2,1)S(1)}, bf16[256,128]{1,0:T(8,128)(2,1)S(1)}, u32[]{:S(2)}, u32[]{:S(2)}) collective-permute-start(bf16[256,128]{1,0:T(8,128)(2,1)S(1)} %collective-permute-done.25.refs_1_), channel_id=1, source_target_pairs={{0,1},{1,0},{2,3},{3,2},{4,5},{5,4},{6,7},{7,6},{8,9},{9,8},{10,11... | collective-permute-start | bytes 196616 | tf_op jit(solution)/shard_map/ppermute | solution.py:21
  70.4 5.8 %collective-permute-start.32 = (bf16[8,8192]{1,0:T(8,128)(2,1)S(1)}, bf16[8,8192]{1,0:T(8,128)(2,1)S(1)}, u32[]{:S(2)}, u32[]{:S(2)}) collective-permute-start(bf16[8,8192]{1,0:T(8,128)(2,1)S(1)} %get-tuple-element.12), channel_id=1, source_target_pairs={{0,8},{8,0},{16,24},{24,16},{1,9},{9,1},{17,25},{25,17},{2,10},{10... | collective-permute-start | bytes 393224 | tf_op jit(solution)/shard_map/ppermute | solution.py:21
  72.0 5.5 %collective-permute-start.34 = (bf16[8,8192]{1,0:T(8,128)(2,1)S(1)}, bf16[8,8192]{1,0:T(8,128)(2,1)S(1)}, u32[]{:S(2)}, u32[]{:S(2)}) collective-permute-start(bf16[8,8192]{1,0:T(8,128)(2,1)S(1)} %get-tuple-element.13), channel_id=1, source_target_pairs={{0,16},{8,24},{16,0},{24,8},{1,17},{9,25},{17,1},{25,9},{2,18},{10... | collective-permute-start | bytes 393224 | tf_op jit(solution)/shard_map/ppermute | solution.py:21
  76.3 5.0 %collective-permute-start.33 = (bf16[8,8192]{1,0:T(8,128)(2,1)S(1)}, bf16[8,8192]{1,0:T(8,128)(2,1)S(1)}, u32[]{:S(2)}, u32[]{:S(2)}) collective-permute-start(bf16[8,8192]{1,0:T(8,128)(2,1)S(1)} %add_convert_fusion.1), channel_id=1, source_target_pairs={{0,16},{8,24},{16,0},{24,8},{1,17},{9,25},{17,1},{25,9},{2,18},{10... | collective-permute-start | bytes 393224 | tf_op jit(solution)/shard_map/ppermute | solution.py:21
  77.5 5.0 %collective-permute-start.35 = (bf16[8,8192]{1,0:T(8,128)(2,1)S(1)}, bf16[8,8192]{1,0:T(8,128)(2,1)S(1)}, u32[]{:S(2)}, u32[]{:S(2)}) collective-permute-start(bf16[8,8192]{1,0:T(8,128)(2,1)S(1)} %add_convert_fusion), channel_id=1, source_target_pairs={{0,8},{8,0},{16,24},{24,16},{1,9},{9,1},{17,25},{25,17},{2,10},{10... | collective-permute-start | bytes 393224 | tf_op jit(solution)/shard_map/ppermute | solution.py:21
  (1 other events, 0.8 us)

commit v4 on v3

v4 whole, which is shorter than its diff:
```python
import functools

import jax
import jax.numpy as jnp
from jax import lax
from jax.experimental import pallas as pl
from jax.experimental.pallas import tpu as pltpu
from jax.sharding import PartitionSpec as P


TILE = 64
LANES = 128
FIRST_BYTES = 55040 * 1024
VMEM_BYTES = 40 * 1024 * 1024
TABLE_BYTES = 32 * 1024 * 1024
HALF = jnp.bfloat16
FULL = jnp.float32


def swap(array, axis, mask):
    size = lax.axis_size(axis)
    return lax.ppermute(array, axis, [(i, i ^ mask) for i in range(size)])


def slot_masks():
    return (0, 2, 4, 6, 1, 3, 5, 7) if lax.axis_size("col") == 8 else None


def slot_source(masks, myself, slot):
    return slot if masks is None else myself ^ masks[slot]


def gather_slots(array):
    if slot_masks() is not None:
        same_core = [array] + [swap(array, "col", mask) for mask in (2, 4, 6)]
        return same_core + [swap(p, "col", 1) for p in same_core]
    stacked = lax.all_gather(array, "col")
    return [stacked[i] for i in range(lax.axis_size("col"))]


def tile_indicator(tiles, columns):
    tile = lax.broadcasted_iota(jnp.int32, (tiles, columns), 0)
    column = lax.broadcasted_iota(jnp.int32, (tiles, columns), 1)
    return (column >= tile * TILE) & (column < tile * TILE + TILE)


def ones_where(mask):
    return jnp.where(mask, 1.0, 0.0).astype(HALF)


def tile_columns(width):
    tiles = width // TILE
    column = lax.broadcasted_iota(jnp.int32, (width, tiles), 0)
    tile = lax.broadcasted_iota(jnp.int32, (width, tiles), 1)
    return ones_where((column >= tile * TILE) & (column < tile * TILE + TILE))


def tile_sums(weighted, ensemble, columns):
    members, levels, width = ensemble.shape
    product = ensemble.astype(FULL) * weighted[None]
    product = product.reshape(members * levels, width).astype(HALF)
    return jnp.dot(product, columns, preferred_element_type=FULL)


def whole(count):
    return [pl.BlockSpec(memory_space=pltpu.VMEM)] * count


def params(limit):
    return pltpu.CompilerParams(vmem_limit_bytes=limit)


def column_sizes(ensemble):
    members, levels, fine = ensemble.shape
    width = min(fine, LANES // 4 * TILE)
    return members, levels, fine, width, fine // width


def chunk_copy(source, target, sems, index, width, i):
    lead = (slice(None),) * (len(source.shape) - 1)
    span = pl.ds(i * width, width)
    return pltpu.make_async_copy(
        source.at[lead + (span,)], target.at[lead + (span,)], sems.at[index, i]
    )


def first_kernel(
    width, state_hbm, weight_hbm, ensemble_hbm, partial_ref, state_ref, weight_ref, ensemble_ref, sems
):
    steps = state_hbm.shape[1] // width
    tiles = width // TILE
    pairs = [(state_hbm, state_ref), (weight_hbm, weight_ref), (ensemble_hbm, ensemble_ref)]

    def copies(i):
        return [
            chunk_copy(source, target, sems, j, width, i)
            for j, (source, target) in enumerate(pairs)
        ]

    for i in range(steps):
        for copy in copies(i):
            copy.start()
    columns = tile_columns(width)
    group = LANES // tiles
    for first in range(0, steps, group):
        sums = []
        for i in range(first, first + group):
            for copy in copies(i):
                copy.wait()
            span = slice(i * width, (i + 1) * width)
            weighted = state_ref[:, span] * weight_ref[:, span]
            sums.append(tile_sums(weighted, ensemble_ref[:, :, span], columns))
        place = slice(first * tiles, first * tiles + LANES)
        partial_ref[:, place] = jnp.concatenate(sums, axis=1).astype(HALF)


def run_first(state, weight, ensemble):
    members, levels, fine, width, steps = column_sizes(ensemble)
    return pl.pallas_call(
        functools.partial(first_kernel, width),
        in_specs=[pl.BlockSpec(memory_space=pltpu.HBM)] * 3,
        out_specs=whole(1)[0],
        out_shape=jax.ShapeDtypeStruct((members * levels, fine // TILE), HALF),
        scratch_shapes=[
            pltpu.VMEM((levels, fine), FULL),
            pltpu.VMEM((1, fine), FULL),
            pltpu.VMEM((members, levels, fine), HALF),
            pltpu.SemaphoreType.DMA((3, steps)),
        ],
        compiler_params=params(FIRST_BYTES),
        name="tile_sums_first",
    )(state, weight, ensemble)


def second_kernel(width, scale, columns_ref, ensemble_ref, state_ref, climate_ref, weight_ref, *refs):
    sum_refs, (state_out, partial_ref) = refs[:4], refs[4:]
    tiles = width // TILE
    steps = state_ref.shape[1] // width
    half = sum_refs[0].shape[1] // width
    group = LANES // tiles
    for first in range(0, steps, group):
        sums = []
        for i in range(first, first + group):
            mine_ref, theirs_ref = sum_refs[i // half * 2 : i // half * 2 + 2]
            span = slice(i * width, (i + 1) * width)
            near = slice(i % half * width, (i % half + 1) * width)
            total = mine_ref[:, near].astype(FULL) + theirs_ref[:, near].astype(FULL)
            state = climate_ref[:, span] * state_ref[:, span] + total * scale
            state_out[:, span] = state
            sums.append(tile_sums(state * weight_ref[:, span], ensemble_ref[:, :, span], columns_ref[...]))
        place = slice(first * tiles, first * tiles + LANES)
        partial_ref[:, place] = jnp.concatenate(sums, axis=1).astype(HALF)


def run_second(scale, columns, state, climate, sums, weight, ensemble):
    members, levels, fine, width, _ = column_sizes(ensemble)
    return pl.pallas_call(
        functools.partial(second_kernel, width, scale),
        in_specs=whole(9),
        out_specs=whole(2),
        out_shape=[
            jax.ShapeDtypeStruct((levels, fine), FULL),
            jax.ShapeDtypeStruct((members * levels, fine // TILE), HALF),
        ],
        compiler_params=params(VMEM_BYTES),
        name="tile_sums_second",
    )(columns, ensemble, state, climate, weight, *sums)


def matrix_kernel(masks, myself_ref, near_ref, dest_ref, local_ref, conv_ref, matrix_ref):
    blocks, neigh, size, _ = conv_ref.shape
    nodes = blocks * size
    rows = [
        jnp.concatenate([conv_ref[b, k] for k in range(neigh)], axis=1) for b in range(blocks)
    ]
    row = lax.broadcasted_iota(jnp.int32, (size, nodes), 0)
    for s in range(dest_ref.shape[1] // nodes):
        source = slot_source(masks, myself_ref[0], s)
        span = pl.ds(pl.multiple_of(source * nodes, nodes), nodes)
        tile_node = dest_ref[:, span] * nodes + local_ref[:, span]
        for b in range(blocks):
            place = jnp.concatenate(
                [ones_where(row == tile_node - near_ref[b, k] * size) for k in range(neigh)], axis=0
            )
            block = jnp.dot(rows[b], place, preferred_element_type=FULL)
            matrix_ref[s * nodes : (s + 1) * nodes, b * size : (b + 1) * size] = block.T.astype(HALF)


def run_matrix(myself, neighbours, dest, local, conv_blocks):
    blocks, _, size, _ = conv_blocks.shape
    scalars = pl.BlockSpec(memory_space=pltpu.SMEM)
    return pl.pallas_call(
        functools.partial(matrix_kernel, slot_masks()),
        in_specs=[scalars, scalars] + whole(3),
        out_specs=whole(1)[0],
        out_shape=jax.ShapeDtypeStruct((dest.shape[1], blocks * size), HALF),
        compiler_params=params(TABLE_BYTES),
        name="node_matrix",
    )(myself, neighbours, dest, local, conv_blocks)


def select_kernel(masks, nodes, myself_ref, dest_ref, local_ref, select_ref):
    span = pl.ds(pl.multiple_of(myself_ref[0] * nodes, nodes), nodes)
    dest, local = (
        jnp.concatenate([ref[k : k + 1, span] for k in range(2)], axis=1)
        for ref in (dest_ref, local_ref)
    )
    row = lax.broadcasted_iota(jnp.int32, (nodes, 2 * nodes), 0)
    for s in range(dest_ref.shape[1] // nodes):
        source = slot_source(masks, myself_ref[0], s)
        select_ref[s * nodes : (s + 1) * nodes, :] = ones_where(
            row == jnp.where(dest == source, local, -1)
        )


def run_select(myself, dest, local, nodes):
    return pl.pallas_call(
        functools.partial(select_kernel, slot_masks(), nodes),
        in_specs=[pl.BlockSpec(memory_space=pltpu.SMEM)] + whole(2),
        out_specs=whole(1)[0],
        out_shape=jax.ShapeDtypeStruct((dest.shape[1], 2 * nodes), HALF),
        compiler_params=params(TABLE_BYTES),
        name="selection",
    )(myself, dest, local)


def slot_product(piece_refs, matrix_ref):
    span = piece_refs[0].shape[1]
    total = jnp.zeros((piece_refs[0].shape[0], matrix_ref.shape[1]), FULL)
    for s, piece in enumerate(piece_refs):
        total = total + jnp.dot(
            piece[...], matrix_ref[s * span : (s + 1) * span, :], preferred_element_type=FULL
        )
    return total


def nodes_kernel(matrix_ref, *refs):
    refs[-1][...] = slot_product(refs[:-1], matrix_ref).astype(HALF)


def run_nodes(matrix, partial_all):
    return pl.pallas_call(
        nodes_kernel,
        in_specs=whole(1 + len(partial_all)),
        out_specs=whole(1)[0],
        out_shape=jax.ShapeDtypeStruct((partial_all[0].shape[0], matrix.shape[1]), HALF),
        compiler_params=params(TABLE_BYTES),
        name="nodes",
    )(matrix, *partial_all)


def expansion_kernel(width, weight_ref, expand_ref, columns_ref):
    columns_ref[...] = tile_columns(width)
    inside = tile_indicator(width // TILE, width)

    def step(i, carry):
        weight = weight_ref[:, pl.ds(pl.multiple_of(i * width, width), width)]
        high = weight.astype(HALF).astype(FULL)
        low = weight - high
        expand_ref[i] = jnp.concatenate(
            [
                jnp.where(inside, source[k : k + 1, :], 0.0).astype(HALF)
                for source in (high, low)
                for k in range(2)
            ],
            axis=0,
        )
        return carry

    lax.fori_loop(0, expand_ref.shape[0], step, 0)


def run_expansion(width, interp_weight):
    return pl.pallas_call(
        functools.partial(expansion_kernel, width),
        in_specs=whole(1),
        out_specs=whole(2),
        out_shape=[
            jax.ShapeDtypeStruct((interp_weight.shape[1] // width, 4 * width // TILE, width), HALF),
            jax.ShapeDtypeStruct((width, width // TILE), HALF),
        ],
        compiler_params=params(TABLE_BYTES),
        name="expansion",
    )(interp_weight)


def spread_kernel(slots, ensemble_ref, select_ref, expand_ref, *refs):
    node_refs, out_refs, values_ref = refs[:slots], refs[slots : slots + 2], refs[slots + 2]
    members, levels, _ = ensemble_ref.shape
    steps, _, width = expand_ref.shape
    tiles = width // TILE
    feature = members * levels
    pairs = select_ref.shape[1]
    values = slot_product(node_refs, select_ref)
    lane = lax.broadcasted_iota(jnp.int32, (feature, LANES), 1)
    group = LANES // tiles
    for i in range(steps):
        first = i // group * LANES
        ends = [values[:, k * pairs // 2 + first : k * pairs // 2 + first + LANES] for k in range(2)]
        left = ends[0]
        for place in range(group):
            shift = (place - i % group) * tiles % LANES
            moved = ends[place % 2] if shift == 0 else pltpu.roll(ends[place % 2], shift, 1)
            left = moved if place == 0 else jnp.where(lane < place * tiles, left, moved)
        values_ref[i] = left.astype(HALF)
    piece = 2 * LANES

    half = steps // 2
    for i in range(steps):
        for c in range(0, width, piece):
            field = jnp.dot(
                values_ref[i], expand_ref[i, :, c : c + piece], preferred_element_type=FULL
            )
            field = field.reshape(members, levels, piece)
            start = i * width + c
            terms = ensemble_ref[:, :, start : start + piece].astype(FULL) * field
            start = i % half * width + c
            out_refs[i // half][:, start : start + piece] = jnp.sum(terms, axis=0).astype(HALF)


def run_spread(select, ensemble, expand, nodes_all):
    members, levels, fine, _, steps = column_sizes(ensemble)
    slots = len(nodes_all)
    return pl.pallas_call(
        functools.partial(spread_kernel, slots),
        in_specs=whole(3 + slots),
        out_specs=whole(2),
        out_shape=[jax.ShapeDtypeStruct((levels, fine // 2), HALF)] * 2,
        scratch_shapes=[pltpu.VMEM((steps, members * levels, LANES), HALF)],
        compiler_params=params(VMEM_BYTES),
        name="spread",
    )(ensemble, select, expand, *nodes_all)


def add_half(one, two):
    return (one.astype(FULL) + two.astype(FULL)).astype(HALF)


def member_sum(halves):
    size = lax.axis_size("mem")
    masks = [1 << i for i in range(size.bit_length() - 1)]
    orders = [masks, masks[::-1]]
    for step in range(len(masks) - 1):
        moved = [swap(part, "mem", order[step]) for part, order in zip(halves, orders)]
        halves = [add_half(part, other) for part, other in zip(halves, moved)]
    moved = [swap(part, "mem", order[-1]) for part, order in zip(halves, orders)]
    return halves[0], moved[0], halves[1], moved[1]


def per_device(
    increment,
    ensemble,
    climate,
    restrict_dest,
    restrict_local,
    restrict_weight,
    conv_blocks,
    neighbours,
    interp_dest,
    interp_local,
    interp_weight,
):
    myself = lax.axis_index("col")[None]
    members = ensemble.shape[0]
    nodes = ensemble.shape[2] // TILE
    scale = 1.0 / (members * lax.axis_size("mem") - 1)
    weight = restrict_weight[None, :]

    partial_all = gather_slots(run_first(increment, weight, ensemble))
    matrix = run_matrix(
        myself, neighbours, restrict_dest.reshape(1, -1), restrict_local.reshape(1, -1), conv_blocks
    )
    select = run_select(myself, interp_dest.T, interp_local.T, nodes)
    expand, columns = run_expansion(column_sizes(ensemble)[3], interp_weight)

    nodes_all = gather_slots(run_nodes(matrix, partial_all))
    sums = member_sum(run_spread(select, ensemble, expand, nodes_all))
    once_applied, partial = run_second(scale, columns, increment, climate, sums, weight, ensemble)
    nodes_all = gather_slots(run_nodes(matrix, gather_slots(partial)))
    sums = member_sum(run_spread(select, ensemble, expand, nodes_all))
    total = jnp.concatenate(
        [sums[2 * i].astype(FULL) + sums[2 * i + 1].astype(FULL) for i in range(2)], axis=1
    )
    return once_applied, climate * once_applied + total * scale


def solution(mesh):
    in_specs = (
        P(None, "col"),
        P("mem", None, "col"),
        P(None, "col"),
        P(),
        P(),
        P("col"),
        P("col", None, None, None),
        P("col", None),
        P(),
        P(),
        P(None, "col"),
    )
    out_specs = (P(None, "col"), P(None, "col"))

    return jax.shard_map(per_device, mesh=mesh, in_specs=in_specs, out_specs=out_specs, check_vma=False)
```

time: 83.6 us -> 80.5 us (0.963)
  Pallas kernels: 15.2 us -> 13.1 us
  waiting for transfers between devices: 33.9 us -> 32.8 us
    pallas_call x2 -> x3, Pallas kernels: 6.05 us -> 4.82 us  [the longest x2 3.45 us: run_spread(): pl.pallas_call(functools.partial(spread_kernel, slots), in_specs=whole(3...]
    ppermute x36, waiting for transfers between devices: 33.9 us -> 32.8 us  [swap(): return lax.ppermute(array, axis, [(i, i ^ mask) for i in range(size)])]
    pallas_call x1, Pallas kernels: 2.93 us -> 1.95 us  [run_second(): pl.pallas_call(functools.partial(second_kernel, width, scale), in_specs=w...]
  transfers between devices with their start and end apart: 36 -> 36, of which waited for: 20 -> 18; matrix products, arithmetic and copies ran while one was open for 0% -> 0% of each run, Pallas kernels for 2% -> 4%
where the time goes in v4:
time: 80.5 us; the launch traced here: 80.3 us
  waiting for transfers between devices  32.8 us (41%)
  starting transfers between devices  31.4 us (39%)
  Pallas kernels  13.1 us (16%)
  other arithmetic  1.07 us (1%)
  between operations  0.93 us (1%)
  local copies, waits for them, and re-layouts  0.9 us (1%)
    ppermute x36, waiting for transfers between devices, swap(): return lax.ppermute(array, axis, [(i, i ^ mask) for i in range(size)])  32.8 us
    ppermute x36, starting transfers between devices, swap(): return lax.ppermute(array, axis, [(i, i ^ mask) for i in range(size)])  31.4 us
    pallas_call x1, Pallas kernels, run_first(): pl.pallas_call(functools.partial(first_kernel, width), in_specs=[pl.Block...  3.89 us
    pallas_call x2, Pallas kernels, run_spread(): pl.pallas_call(functools.partial(spread_kernel, slots), in_specs=whole(3...  3.45 us
    pallas_call x1, Pallas kernels, run_second(): pl.pallas_call(functools.partial(second_kernel, width, scale), in_specs=w...  1.95 us
  transfers between devices with their start and end apart: 36, of which 18 were waited for; matrix products, arithmetic and copies ran while one was open for 0% of the time, Pallas kernels for 4%

profile of v4, /device:TPU:0, one launch (start us, length us, event | category | flops | bytes accessed | tf_op | source)
XLA Modules:
  0.0 80.3 jit_solution(3261081657002290163)
XLA Ops:
  0.7 0.8 %copy-done.3 = f32[16384]{0:T(1024)S(1)} copy-done((f32[16384]{0:T(1024)S(1)}, f32[16384]{0:T(1024)}, u32[]{:S(2)}) %copy-start.3) | copy-done | bytes 65560
  1.5 3.9 %tile_sums_first.1.refs_0_ = bf16[128,256]{1,0:T(8,128)(2,1)S(1)} custom-call(f32[8,16384]{1,0:T(8,128)} %state_ref.1, f32[1,16384]{1,0:T(1,128)S(1)} %bitcast.6, bf16[16,8,16384]{2,1,0:T(8,128)(2,1)} %ensemble_ref.5), custom_call_target="tpu_custom_call" | custom-call | tf_op jit(solution)/shard_map/tile_sums_first/pallas_call | solution.py:119
  5.4 5.1 %collective-permute-start.2 = (bf16[128,256]{1,0:T(8,128)(2,1)S(1)}, bf16[128,256]{1,0:T(8,128)(2,1)S(1)}, u32[]{:S(2)}, u32[]{:S(2)}) collective-permute-start(bf16[128,256]{1,0:T(8,128)(2,1)S(1)} %tile_sums_first.1.refs_0_), channel_id=1, source_target_pairs={{0,6},{1,7},{2,4},{3,5},{4,2},{5,3},{6,0},{7,1},{8,14},{9,15},{10,... | collective-permute-start | bytes 196616 | tf_op jit(solution)/shard_map/ppermute | solution.py:22
  10.6 0.6 collective-permute-start
  11.2 1.8 %collective-permute-done.2.refs_3_ = bf16[128,256]{1,0:T(8,128)(2,1)S(1)} collective-permute-done((bf16[128,256]{1,0:T(8,128)(2,1)S(1)}, bf16[128,256]{1,0:T(8,128)(2,1)S(1)}, u32[]{:S(2)}, u32[]{:S(2)}) %collective-permute-start.2) | collective-permute-done | bytes 65568 | tf_op jit(solution)/shard_map/ppermute | solution.py:22
  13.0 3.1 %collective-permute-done.1.refs_2_ = bf16[128,256]{1,0:T(8,128)(2,1)S(1)} collective-permute-done((bf16[128,256]{1,0:T(8,128)(2,1)S(1)}, bf16[128,256]{1,0:T(8,128)(2,1)S(1)}, u32[]{:S(2)}, u32[]{:S(2)}) %collective-permute-start.1) | collective-permute-done | bytes 65568 | tf_op jit(solution)/shard_map/ppermute | solution.py:22
  16.2 0.5 collective-permute-start.4
  16.7 1.5 %node_matrix.1.matrix_ref = bf16[2048,256]{1,0:T(8,128)(2,1)S(1)} custom-call(s32[1]{0:T(128)} %bitcast.1.myself_ref, s32[2,4]{1,0:T(2,128)S(1)} %copy-done.11, s32[1,2048]{1,0:T(1,128)S(1)} %bitcast.10, s32[1,2048]{1,0:T(1,128)S(1)} %bitcast.11, bf16[2,4,128,128]{3,2,1,0:T(8,128)(2,1)S(1)} %copy-done.5), custom_call_target="tpu_custom_call" | custom-call | tf_op jit(solution)/shard_map/node_matrix/pallas_call | solution.py:192
  18.2 0.3 nodes.2.refs_0_
  18.6 2.8 %collective-permute-start.9 = (bf16[128,256]{1,0:T(8,128)(2,1)S(1)}, bf16[128,256]{1,0:T(8,128)(2,1)S(1)}, u32[]{:S(2)}, u32[]{:S(2)}) collective-permute-start(bf16[128,256]{1,0:T(8,128)(2,1)S(1)} %nodes.2.refs_0_), channel_id=1, source_target_pairs={{0,6},{1,7},{2,4},{3,5},{4,2},{5,3},{6,0},{7,1},{8,14},{9,15},{10,... | collective-permute-start | bytes 196616 | tf_op jit(solution)/shard_map/ppermute | solution.py:22
  21.4 1.7 %collective-permute-start.7 = (bf16[128,256]{1,0:T(8,128)(2,1)S(1)}, bf16[128,256]{1,0:T(8,128)(2,1)S(1)}, u32[]{:S(2)}, u32[]{:S(2)}) collective-permute-start(bf16[128,256]{1,0:T(8,128)(2,1)S(1)} %nodes.2.refs_0_), channel_id=1, source_target_pairs={{0,2},{1,3},{2,0},{3,1},{4,6},{5,7},{6,4},{7,5},{8,10},{9,11},{10,... | collective-permute-start | bytes 196616 | tf_op jit(solution)/shard_map/ppermute | solution.py:22
  23.0 2.2 %collective-permute-done.9.refs_3_ = bf16[128,256]{1,0:T(8,128)(2,1)S(1)} collective-permute-done((bf16[128,256]{1,0:T(8,128)(2,1)S(1)}, bf16[128,256]{1,0:T(8,128)(2,1)S(1)}, u32[]{:S(2)}, u32[]{:S(2)}) %collective-permute-start.9) | collective-permute-done | bytes 65568 | tf_op jit(solution)/shard_map/ppermute | solution.py:22
  25.3 2.1 %collective-permute-done.8.refs_2_ = bf16[128,256]{1,0:T(8,128)(2,1)S(1)} collective-permute-done((bf16[128,256]{1,0:T(8,128)(2,1)S(1)}, bf16[128,256]{1,0:T(8,128)(2,1)S(1)}, u32[]{:S(2)}, u32[]{:S(2)}) %collective-permute-start.8) | collective-permute-done | bytes 65568 | tf_op jit(solution)/shard_map/ppermute | solution.py:22
  27.5 0.4 collective-permute-start.11
  27.9 1.4 %expansion.1 = (bf16[8,128,2048]{2,1,0:T(8,128)(2,1)S(1)}, bf16[2048,32]{1,0:T(8,128)(2,1)S(1)}) custom-call(f32[2,16384]{1,0:T(2,128)S(1)} %copy-done.6), custom_call_target="tpu_custom_call" | custom-call | tf_op jit(solution)/shard_map/expansion/pallas_call | solution.py:274
  29.3 0.4 selection.1.select_ref
  29.7 1.7 %spread.2 = (bf16[8,8192]{1,0:T(8,128)(2,1)S(1)}, bf16[8,8192]{1,0:T(8,128)(2,1)S(1)}) custom-call(bf16[16,8,16384]{2,1,0:T(8,128)(2,1)S(1)} %copy-done, bf16[2048,512]{1,0:T(8,128)(2,1)S(1)} %selection.1.select_ref, bf16[8,128,2048]{2,1,0:T(8,128)(2,1)S(1)} %get-tuple-element.11.expand_ref, bf16[128,256]{1,0:T(8,128)(2,1)S(1)} %nodes.2.refs_0_, ...), custom_call_target="tpu_custom_call" | custom-call | tf_op jit(solution)/shard_map/spread/pallas_call | solution.py:324
  31.5 1.6 %collective-permute-start.14 = (bf16[8,8192]{1,0:T(8,128)(2,1)S(1)}, bf16[8,8192]{1,0:T(8,128)(2,1)S(1)}, u32[]{:S(2)}, u32[]{:S(2)}) collective-permute-start(bf16[8,8192]{1,0:T(8,128)(2,1)S(1)} %get-tuple-element.12), channel_id=1, source_target_pairs={{0,8},{8,0},{16,24},{24,16},{1,9},{9,1},{17,25},{25,17},{2,10},{10... | collective-permute-start | bytes 393224 | tf_op jit(solution)/shard_map/ppermute | solution.py:22
  33.0 1.5 %collective-permute-start.16 = (bf16[8,8192]{1,0:T(8,128)(2,1)S(1)}, bf16[8,8192]{1,0:T(8,128)(2,1)S(1)}, u32[]{:S(2)}, u32[]{:S(2)}) collective-permute-start(bf16[8,8192]{1,0:T(8,128)(2,1)S(1)} %get-tuple-element.13), channel_id=1, source_target_pairs={{0,16},{8,24},{16,0},{24,8},{1,17},{9,25},{17,1},{25,9},{2,18},{10... | collective-permute-start | bytes 393224 | tf_op jit(solution)/shard_map/ppermute | solution.py:22
  34.5 2.5 %collective-permute-done.14 = bf16[8,8192]{1,0:T(8,128)(2,1)S(1)} collective-permute-done((bf16[8,8192]{1,0:T(8,128)(2,1)S(1)}, bf16[8,8192]{1,0:T(8,128)(2,1)S(1)}, u32[]{:S(2)}, u32[]{:S(2)}) %collective-permute-start.14) | collective-permute-done | bytes 131104 | tf_op jit(solution)/shard_map/ppermute | solution.py:22
  37.1 1.6 %collective-permute-start.15 = (bf16[8,8192]{1,0:T(8,128)(2,1)S(1)}, bf16[8,8192]{1,0:T(8,128)(2,1)S(1)}, u32[]{:S(2)}, u32[]{:S(2)}) collective-permute-start(bf16[8,8192]{1,0:T(8,128)(2,1)S(1)} %add_convert_fusion.3.refs_0_), channel_id=1, source_target_pairs={{0,16},{8,24},{16,0},{24,8},{1,17},{9,25},{17,1},{25,9},{2,18},{10... | collective-permute-start | bytes 393224 | tf_op jit(solution)/shard_map/ppermute | solution.py:22
  38.7 1.6 %collective-permute-start.17 = (bf16[8,8192]{1,0:T(8,128)(2,1)S(1)}, bf16[8,8192]{1,0:T(8,128)(2,1)S(1)}, u32[]{:S(2)}, u32[]{:S(2)}) collective-permute-start(bf16[8,8192]{1,0:T(8,128)(2,1)S(1)} %add_convert_fusion.2.refs_2_), channel_id=1, source_target_pairs={{0,8},{8,0},{16,24},{24,16},{1,9},{9,1},{17,25},{25,17},{2,10},{10... | collective-permute-start | bytes 393224 | tf_op jit(solution)/shard_map/ppermute | solution.py:22
  40.2 1.9 %collective-permute-done.15.refs_1_ = bf16[8,8192]{1,0:T(8,128)(2,1)S(1)} collective-permute-done((bf16[8,8192]{1,0:T(8,128)(2,1)S(1)}, bf16[8,8192]{1,0:T(8,128)(2,1)S(1)}, u32[]{:S(2)}, u32[]{:S(2)}) %collective-permute-start.15) | collective-permute-done | bytes 131104 | tf_op jit(solution)/shard_map/ppermute | solution.py:22
  42.1 1.6 %collective-permute-done.17.refs_3_ = bf16[8,8192]{1,0:T(8,128)(2,1)S(1)} collective-permute-done((bf16[8,8192]{1,0:T(8,128)(2,1)S(1)}, bf16[8,8192]{1,0:T(8,128)(2,1)S(1)}, u32[]{:S(2)}, u32[]{:S(2)}) %collective-permute-start.17) | collective-permute-done | bytes 131104 | tf_op jit(solution)/shard_map/ppermute | solution.py:22
  43.7 1.9 %tile_sums_second.1 = (f32[8,16384]{1,0:T(8,128)}, bf16[128,256]{1,0:T(8,128)(2,1)S(1)}) custom-call(bf16[2048,32]{1,0:T(8,128)(2,1)S(1)} %get-tuple-element.10.columns_ref, bf16[16,8,16384]{2,1,0:T(8,128)(2,1)S(1)} %copy-done, f32[8,16384]{1,0:T(8,128)S(1)} %copy-done.1, f32[8,16384]{1,0:T(8,128)S(1)} %copy-done.2, f32[1,16384]{1,0:T(1,128)S(1)} %bitcast.7, ...), custom_call_target="tpu_custom_call" | custom-call | tf_op jit(solution)/shard_map/tile_sums_second/pallas_call | solution.py:157
  45.7 2.4 %collective-permute-start.20 = (bf16[128,256]{1,0:T(8,128)(2,1)S(1)}, bf16[128,256]{1,0:T(8,128)(2,1)S(1)}, u32[]{:S(2)}, u32[]{:S(2)}) collective-permute-start(bf16[128,256]{1,0:T(8,128)(2,1)S(1)} %get-tuple-element.15.refs_0_), channel_id=1, source_target_pairs={{0,6},{1,7},{2,4},{3,5},{4,2},{5,3},{6,0},{7,1},{8,14},{9,15},{10,... | collective-permute-start | bytes 196616 | tf_op jit(solution)/shard_map/ppermute | solution.py:22
  48.1 1.9 %collective-permute-start.18 = (bf16[128,256]{1,0:T(8,128)(2,1)S(1)}, bf16[128,256]{1,0:T(8,128)(2,1)S(1)}, u32[]{:S(2)}, u32[]{:S(2)}) collective-permute-start(bf16[128,256]{1,0:T(8,128)(2,1)S(1)} %get-tuple-element.15.refs_0_), channel_id=1, source_target_pairs={{0,2},{1,3},{2,0},{3,1},{4,6},{5,7},{6,4},{7,5},{8,10},{9,11},{10,... | collective-permute-start | bytes 196616 | tf_op jit(solution)/shard_map/ppermute | solution.py:22
  50.1 1.9 %collective-permute-done.20.refs_3_ = bf16[128,256]{1,0:T(8,128)(2,1)S(1)} collective-permute-done((bf16[128,256]{1,0:T(8,128)(2,1)S(1)}, bf16[128,256]{1,0:T(8,128)(2,1)S(1)}, u32[]{:S(2)}, u32[]{:S(2)}) %collective-permute-start.20) | collective-permute-done | bytes 65568 | tf_op jit(solution)/shard_map/ppermute | solution.py:22
  52.0 1.4 %collective-permute-done.19.refs_2_ = bf16[128,256]{1,0:T(8,128)(2,1)S(1)} collective-permute-done((bf16[128,256]{1,0:T(8,128)(2,1)S(1)}, bf16[128,256]{1,0:T(8,128)(2,1)S(1)}, u32[]{:S(2)}, u32[]{:S(2)}) %collective-permute-start.19) | collective-permute-done | bytes 65568 | tf_op jit(solution)/shard_map/ppermute | solution.py:22
  53.3 0.5 collective-permute-start.22
  53.9 0.7 collective-permute-done.23.refs_6_
  54.6 0.2 collective-permute-done.22.refs_5_
  54.8 0.3 nodes.3.refs_0_
  55.1 2.3 %collective-permute-start.27 = (bf16[128,256]{1,0:T(8,128)(2,1)S(1)}, bf16[128,256]{1,0:T(8,128)(2,1)S(1)}, u32[]{:S(2)}, u32[]{:S(2)}) collective-permute-start(bf16[128,256]{1,0:T(8,128)(2,1)S(1)} %nodes.3.refs_0_), channel_id=1, source_target_pairs={{0,6},{1,7},{2,4},{3,5},{4,2},{5,3},{6,0},{7,1},{8,14},{9,15},{10,... | collective-permute-start | bytes 196616 | tf_op jit(solution)/shard_map/ppermute | solution.py:22
  57.5 2.1 %collective-permute-start.25 = (bf16[128,256]{1,0:T(8,128)(2,1)S(1)}, bf16[128,256]{1,0:T(8,128)(2,1)S(1)}, u32[]{:S(2)}, u32[]{:S(2)}) collective-permute-start(bf16[128,256]{1,0:T(8,128)(2,1)S(1)} %nodes.3.refs_0_), channel_id=1, source_target_pairs={{0,2},{1,3},{2,0},{3,1},{4,6},{5,7},{6,4},{7,5},{8,10},{9,11},{10,... | collective-permute-start | bytes 196616 | tf_op jit(solution)/shard_map/ppermute | solution.py:22
  59.5 2.5 %collective-permute-done.27.refs_3_ = bf16[128,256]{1,0:T(8,128)(2,1)S(1)} collective-permute-done((bf16[128,256]{1,0:T(8,128)(2,1)S(1)}, bf16[128,256]{1,0:T(8,128)(2,1)S(1)}, u32[]{:S(2)}, u32[]{:S(2)}) %collective-permute-start.27) | collective-permute-done | bytes 65568 | tf_op jit(solution)/shard_map/ppermute | solution.py:22
  62.0 2.1 %collective-permute-done.26.refs_2_ = bf16[128,256]{1,0:T(8,128)(2,1)S(1)} collective-permute-done((bf16[128,256]{1,0:T(8,128)(2,1)S(1)}, bf16[128,256]{1,0:T(8,128)(2,1)S(1)}, u32[]{:S(2)}, u32[]{:S(2)}) %collective-permute-start.26) | collective-permute-done | bytes 65568 | tf_op jit(solution)/shard_map/ppermute | solution.py:22
  64.1 0.5 collective-permute-start.29
  64.6 0.7 collective-permute-done.30.refs_6_
  65.5 1.7 %spread.3 = (bf16[8,8192]{1,0:T(8,128)(2,1)S(1)}, bf16[8,8192]{1,0:T(8,128)(2,1)S(1)}) custom-call(bf16[16,8,16384]{2,1,0:T(8,128)(2,1)S(1)} %copy-done, bf16[2048,512]{1,0:T(8,128)(2,1)S(1)} %selection.1.select_ref, bf16[8,128,2048]{2,1,0:T(8,128)(2,1)S(1)} %get-tuple-element.11.expand_ref, bf16[128,256]{1,0:T(8,128)(2,1)S(1)} %nodes.3.refs_0_, ...), custom_call_target="tpu_custom_call" | custom-call | tf_op jit(solution)/shard_map/spread/pallas_call | solution.py:324
  67.3 1.6 %collective-permute-start.32 = (bf16[8,8192]{1,0:T(8,128)(2,1)S(1)}, bf16[8,8192]{1,0:T(8,128)(2,1)S(1)}, u32[]{:S(2)}, u32[]{:S(2)}) collective-permute-start(bf16[8,8192]{1,0:T(8,128)(2,1)S(1)} %get-tuple-element.16), channel_id=1, source_target_pairs={{0,8},{8,0},{16,24},{24,16},{1,9},{9,1},{17,25},{25,17},{2,10},{10... | collective-permute-start | bytes 393224 | tf_op jit(solution)/shard_map/ppermute | solution.py:22
  68.8 0.5 collective-permute-start.34
  69.3 3.8 %collective-permute-done.32 = bf16[8,8192]{1,0:T(8,128)(2,1)S(1)} collective-permute-done((bf16[8,8192]{1,0:T(8,128)(2,1)S(1)}, bf16[8,8192]{1,0:T(8,128)(2,1)S(1)}, u32[]{:S(2)}, u32[]{:S(2)}) %collective-permute-start.32) | collective-permute-done | bytes 131104 | tf_op jit(solution)/shard_map/ppermute | solution.py:22
  73.1 1.2 %collective-permute-start.33 = (bf16[8,8192]{1,0:T(8,128)(2,1)S(1)}, bf16[8,8192]{1,0:T(8,128)(2,1)S(1)}, u32[]{:S(2)}, u32[]{:S(2)}) collective-permute-start(bf16[8,8192]{1,0:T(8,128)(2,1)S(1)} %add_convert_fusion.1), channel_id=1, source_target_pairs={{0,16},{8,24},{16,0},{24,8},{1,17},{9,25},{17,1},{25,9},{2,18},{10... | collective-permute-start | bytes 393224 | tf_op jit(solution)/shard_map/ppermute | solution.py:22
  74.3 0.9 %collective-permute-start.35 = (bf16[8,8192]{1,0:T(8,128)(2,1)S(1)}, bf16[8,8192]{1,0:T(8,128)(2,1)S(1)}, u32[]{:S(2)}, u32[]{:S(2)}) collective-permute-start(bf16[8,8192]{1,0:T(8,128)(2,1)S(1)} %add_convert_fusion), channel_id=1, source_target_pairs={{0,8},{8,0},{16,24},{24,16},{1,9},{9,1},{17,25},{25,17},{2,10},{10... | collective-permute-start | bytes 393224 | tf_op jit(solution)/shard_map/ppermute | solution.py:22
  75.2 2.9 %collective-permute-done.33 = bf16[8,8192]{1,0:T(8,128)(2,1)S(1)} collective-permute-done((bf16[8,8192]{1,0:T(8,128)(2,1)S(1)}, bf16[8,8192]{1,0:T(8,128)(2,1)S(1)}, u32[]{:S(2)}, u32[]{:S(2)}) %collective-permute-start.33) | collective-permute-done | bytes 131104 | tf_op jit(solution)/shard_map/ppermute | solution.py:22
  78.2 1.2 %collective-permute-done.35 = bf16[8,8192]{1,0:T(8,128)(2,1)S(1)} collective-permute-done((bf16[8,8192]{1,0:T(8,128)(2,1)S(1)}, bf16[8,8192]{1,0:T(8,128)(2,1)S(1)}, u32[]{:S(2)}, u32[]{:S(2)}) %collective-permute-start.35) | collective-permute-done | bytes 131104 | tf_op jit(solution)/shard_map/ppermute | solution.py:22
  79.4 0.9 %fusion = f32[8,16384]{1,0:T(8,128)} fusion(f32[8,8192]{1,0:T(8,128)S(1)} %convert_add_fusion, f32[8,8192]{1,0:T(8,128)S(1)} %convert_add_fusion.1, f32[8,16384]{1,0:T(8,128)S(1)} %copy-done.2, f32[8,16384]{1,0:T(8,128)S(1)} %copy-done.12), kind=kLoop, calls=%fused_computation.1 | loop fusion | flops 524288 | bytes 2097152 | tf_op jit(solution)/shard_map/add | solution.py:384
  (66 shorter events, 0.7 us)
Async XLA Ops:
  0.6 16.1 %copy-start.11 = (s32[2,4]{1,0:T(2,128)S(1)}, s32[2,4]{1,0:T(2,128)}, u32[]{:S(2)}) copy-start(s32[2,4]{1,0:T(2,128)} %near_ref.1) | copy-start | bytes 100
  1.5 15.2 %copy-start.5 = (bf16[2,4,128,128]{3,2,1,0:T(8,128)(2,1)S(1)}, bf16[2,4,128,128]{3,2,1,0:T(8,128)(2,1)}, u32[]{:S(2)}) copy-start(bf16[2,4,128,128]{3,2,1,0:T(8,128)(2,1)} %conv_ref.1) | copy-start | bytes 786436
  1.5 15.2 %copy-start.9 = (s32[2048,1]{0,1:T(1,128)S(1)}, s32[2048,1]{0,1:T(1,128)}, u32[]{:S(2)}) copy-start(s32[2048,1]{0,1:T(1,128)} %param.14) | copy-start | bytes 24580
  1.5 15.2 %copy-start.10 = (s32[2048]{0:T(1024)S(1)}, s32[2048]{0:T(1024)}, u32[]{:S(2)}) copy-start(s32[2048]{0:T(1024)} %param.15) | copy-start | bytes 24580
  1.5 26.4 %copy-start.6 = (f32[2,16384]{1,0:T(2,128)S(1)}, f32[2,16384]{1,0:T(2,128)}, u32[]{:S(2)}) copy-start(f32[2,16384]{1,0:T(2,128)} %weight_ref.1) | copy-start | bytes 393220
  1.5 27.7 %copy-start.7 = (s32[2048,2]{0,1:T(2,128)S(1)}, s32[2048,2]{0,1:T(2,128)}, u32[]{:S(2)}) copy-start(s32[2048,2]{0,1:T(2,128)} %param.19) | copy-start | bytes 49156
  1.5 27.7 %copy-start.8 = (s32[2048,2]{0,1:T(2,128)S(1)}, s32[2048,2]{0,1:T(2,128)}, u32[]{:S(2)}) copy-start(s32[2048,2]{0,1:T(2,128)} %param.20) | copy-start | bytes 49156
  5.4 7.6 %collective-permute-start.2 = (bf16[128,256]{1,0:T(8,128)(2,1)S(1)}, bf16[128,256]{1,0:T(8,128)(2,1)S(1)}, u32[]{:S(2)}, u32[]{:S(2)}) collective-permute-start(bf16[128,256]{1,0:T(8,128)(2,1)S(1)} %tile_sums_first.1.refs_0_), channel_id=1, source_target_pairs={{0,6},{1,7},{2,4},{3,5},{4,2},{5,3},{6,0},{7,1},{8,14},{9,15},{10,... | collective-permute-start | bytes 196616 | tf_op jit(solution)/shard_map/ppermute | solution.py:22
  10.6 5.6 %collective-permute-start.1 = (bf16[128,256]{1,0:T(8,128)(2,1)S(1)}, bf16[128,256]{1,0:T(8,128)(2,1)S(1)}, u32[]{:S(2)}, u32[]{:S(2)}) collective-permute-start(bf16[128,256]{1,0:T(8,128)(2,1)S(1)} %tile_sums_first.1.refs_0_), channel_id=1, source_target_pairs={{0,4},{1,5},{2,6},{3,7},{4,0},{5,1},{6,2},{7,3},{8,12},{9,13},{10,... | collective-permute-start | bytes 196616 | tf_op jit(solution)/shard_map/ppermute | solution.py:22
  10.6 5.6 %collective-permute-start = (bf16[128,256]{1,0:T(8,128)(2,1)S(1)}, bf16[128,256]{1,0:T(8,128)(2,1)S(1)}, u32[]{:S(2)}, u32[]{:S(2)}) collective-permute-start(bf16[128,256]{1,0:T(8,128)(2,1)S(1)} %tile_sums_first.1.refs_0_), channel_id=1, source_target_pairs={{0,2},{1,3},{2,0},{3,1},{4,6},{5,7},{6,4},{7,5},{8,10},{9,11},{10,... | collective-permute-start | bytes 196616 | tf_op jit(solution)/shard_map/ppermute | solution.py:22
  11.2 7.0 %collective-permute-start.3 = (bf16[128,256]{1,0:T(8,128)(2,1)S(1)}, bf16[128,256]{1,0:T(8,128)(2,1)S(1)}, u32[]{:S(2)}, u32[]{:S(2)}) collective-permute-start(bf16[128,256]{1,0:T(8,128)(2,1)S(1)} %tile_sums_first.1.refs_0_), channel_id=1, source_target_pairs={{0,1},{1,0},{2,3},{3,2},{4,5},{5,4},{6,7},{7,6},{8,9},{9,8},{10,11... | collective-permute-start | bytes 196616 | tf_op jit(solution)/shard_map/ppermute | solution.py:22
  13.0 5.2 %collective-permute-start.6 = (bf16[128,256]{1,0:T(8,128)(2,1)S(1)}, bf16[128,256]{1,0:T(8,128)(2,1)S(1)}, u32[]{:S(2)}, u32[]{:S(2)}) collective-permute-start(bf16[128,256]{1,0:T(8,128)(2,1)S(1)} %collective-permute-done.2.refs_3_), channel_id=1, source_target_pairs={{0,1},{1,0},{2,3},{3,2},{4,5},{5,4},{6,7},{7,6},{8,9},{9,8},{10,11... | collective-permute-start | bytes 196616 | tf_op jit(solution)/shard_map/ppermute | solution.py:22
  16.2 2.1 %collective-permute-start.5 = (bf16[128,256]{1,0:T(8,128)(2,1)S(1)}, bf16[128,256]{1,0:T(8,128)(2,1)S(1)}, u32[]{:S(2)}, u32[]{:S(2)}) collective-permute-start(bf16[128,256]{1,0:T(8,128)(2,1)S(1)} %collective-permute-done.1.refs_2_), channel_id=1, source_target_pairs={{0,1},{1,0},{2,3},{3,2},{4,5},{5,4},{6,7},{7,6},{8,9},{9,8},{10,11... | collective-permute-start | bytes 196616 | tf_op jit(solution)/shard_map/ppermute | solution.py:22
  16.2 2.1 %collective-permute-start.4 = (bf16[128,256]{1,0:T(8,128)(2,1)S(1)}, bf16[128,256]{1,0:T(8,128)(2,1)S(1)}, u32[]{:S(2)}, u32[]{:S(2)}) collective-permute-start(bf16[128,256]{1,0:T(8,128)(2,1)S(1)} %collective-permute-done.refs_1_), channel_id=1, source_target_pairs={{0,1},{1,0},{2,3},{3,2},{4,5},{5,4},{6,7},{7,6},{8,9},{9,8},{10,11... | collective-permute-start | bytes 196616 | tf_op jit(solution)/shard_map/ppermute | solution.py:22
  16.7 13.0 %copy-start = (bf16[16,8,16384]{2,1,0:T(8,128)(2,1)S(1)}, bf16[16,8,16384]{2,1,0:T(8,128)(2,1)}, u32[]{:S(2)}) copy-start(bf16[16,8,16384]{2,1,0:T(8,128)(2,1)} %ensemble_ref.5) | copy-start | bytes 12582916
  18.6 6.7 %collective-permute-start.9 = (bf16[128,256]{1,0:T(8,128)(2,1)S(1)}, bf16[128,256]{1,0:T(8,128)(2,1)S(1)}, u32[]{:S(2)}, u32[]{:S(2)}) collective-permute-start(bf16[128,256]{1,0:T(8,128)(2,1)S(1)} %nodes.2.refs_0_), channel_id=1, source_target_pairs={{0,6},{1,7},{2,4},{3,5},{4,2},{5,3},{6,0},{7,1},{8,14},{9,15},{10,... | collective-permute-start | bytes 196616 | tf_op jit(solution)/shard_map/ppermute | solution.py:22
  21.3 6.0 %collective-permute-start.8 = (bf16[128,256]{1,0:T(8,128)(2,1)S(1)}, bf16[128,256]{1,0:T(8,128)(2,1)S(1)}, u32[]{:S(2)}, u32[]{:S(2)}) collective-permute-start(bf16[128,256]{1,0:T(8,128)(2,1)S(1)} %nodes.2.refs_0_), channel_id=1, source_target_pairs={{0,4},{1,5},{2,6},{3,7},{4,0},{5,1},{6,2},{7,3},{8,12},{9,13},{10,... | collective-permute-start | bytes 196616 | tf_op jit(solution)/shard_map/ppermute | solution.py:22
  21.4 6.1 %collective-permute-start.7 = (bf16[128,256]{1,0:T(8,128)(2,1)S(1)}, bf16[128,256]{1,0:T(8,128)(2,1)S(1)}, u32[]{:S(2)}, u32[]{:S(2)}) collective-permute-start(bf16[128,256]{1,0:T(8,128)(2,1)S(1)} %nodes.2.refs_0_), channel_id=1, source_target_pairs={{0,2},{1,3},{2,0},{3,1},{4,6},{5,7},{6,4},{7,5},{8,10},{9,11},{10,... | collective-permute-start | bytes 196616 | tf_op jit(solution)/shard_map/ppermute | solution.py:22
  23.0 6.6 %collective-permute-start.10 = (bf16[128,256]{1,0:T(8,128)(2,1)S(1)}, bf16[128,256]{1,0:T(8,128)(2,1)S(1)}, u32[]{:S(2)}, u32[]{:S(2)}) collective-permute-start(bf16[128,256]{1,0:T(8,128)(2,1)S(1)} %nodes.2.refs_0_), channel_id=1, source_target_pairs={{0,1},{1,0},{2,3},{3,2},{4,5},{5,4},{6,7},{7,6},{8,9},{9,8},{10,11... | collective-permute-start | bytes 196616 | tf_op jit(solution)/shard_map/ppermute | solution.py:22
  25.2 4.4 %collective-permute-start.13 = (bf16[128,256]{1,0:T(8,128)(2,1)S(1)}, bf16[128,256]{1,0:T(8,128)(2,1)S(1)}, u32[]{:S(2)}, u32[]{:S(2)}) collective-permute-start(bf16[128,256]{1,0:T(8,128)(2,1)S(1)} %collective-permute-done.9.refs_3_), channel_id=1, source_target_pairs={{0,1},{1,0},{2,3},{3,2},{4,5},{5,4},{6,7},{7,6},{8,9},{9,8},{10,11... | collective-permute-start | bytes 196616 | tf_op jit(solution)/shard_map/ppermute | solution.py:22
  27.3 2.3 %collective-permute-start.12 = (bf16[128,256]{1,0:T(8,128)(2,1)S(1)}, bf16[128,256]{1,0:T(8,128)(2,1)S(1)}, u32[]{:S(2)}, u32[]{:S(2)}) collective-permute-start(bf16[128,256]{1,0:T(8,128)(2,1)S(1)} %collective-permute-done.8.refs_2_), channel_id=1, source_target_pairs={{0,1},{1,0},{2,3},{3,2},{4,5},{5,4},{6,7},{7,6},{8,9},{9,8},{10,11... | collective-permute-start | bytes 196616 | tf_op jit(solution)/shard_map/ppermute | solution.py:22
  27.5 2.2 %collective-permute-start.11 = (bf16[128,256]{1,0:T(8,128)(2,1)S(1)}, bf16[128,256]{1,0:T(8,128)(2,1)S(1)}, u32[]{:S(2)}, u32[]{:S(2)}) collective-permute-start(bf16[128,256]{1,0:T(8,128)(2,1)S(1)} %collective-permute-done.7.refs_1_), channel_id=1, source_target_pairs={{0,1},{1,0},{2,3},{3,2},{4,5},{5,4},{6,7},{7,6},{8,9},{9,8},{10,11... | collective-permute-start | bytes 196616 | tf_op jit(solution)/shard_map/ppermute | solution.py:22
  29.7 14.0 %copy-start.1 = (f32[8,16384]{1,0:T(8,128)S(1)}, f32[8,16384]{1,0:T(8,128)}, u32[]{:S(2)}) copy-start(f32[8,16384]{1,0:T(8,128)} %state_ref.1) | copy-start | bytes 1572868
  29.7 14.0 %copy-start.2 = (f32[8,16384]{1,0:T(8,128)S(1)}, f32[8,16384]{1,0:T(8,128)}, u32[]{:S(2)}) copy-start(f32[8,16384]{1,0:T(8,128)} %climate_ref.1) | copy-start | bytes 1572868
  29.7 14.0 %copy-start.4 = (f32[16384]{0:T(1024)S(1)}, f32[16384]{0:T(1024)}, u32[]{:S(2)}) copy-start(f32[16384]{0:T(1024)} %param.16) | copy-start | bytes 196612
  31.5 5.6 %collective-permute-start.14 = (bf16[8,8192]{1,0:T(8,128)(2,1)S(1)}, bf16[8,8192]{1,0:T(8,128)(2,1)S(1)}, u32[]{:S(2)}, u32[]{:S(2)}) collective-permute-start(bf16[8,8192]{1,0:T(8,128)(2,1)S(1)} %get-tuple-element.12), channel_id=1, source_target_pairs={{0,8},{8,0},{16,24},{24,16},{1,9},{9,1},{17,25},{25,17},{2,10},{10... | collective-permute-start | bytes 393224 | tf_op jit(solution)/shard_map/ppermute | solution.py:22
  33.0 5.6 %collective-permute-start.16 = (bf16[8,8192]{1,0:T(8,128)(2,1)S(1)}, bf16[8,8192]{1,0:T(8,128)(2,1)S(1)}, u32[]{:S(2)}, u32[]{:S(2)}) collective-permute-start(bf16[8,8192]{1,0:T(8,128)(2,1)S(1)} %get-tuple-element.13), channel_id=1, source_target_pairs={{0,16},{8,24},{16,0},{24,8},{1,17},{9,25},{17,1},{25,9},{2,18},{10... | collective-permute-start | bytes 393224 | tf_op jit(solution)/shard_map/ppermute | solution.py:22
  37.1 5.0 %collective-permute-start.15 = (bf16[8,8192]{1,0:T(8,128)(2,1)S(1)}, bf16[8,8192]{1,0:T(8,128)(2,1)S(1)}, u32[]{:S(2)}, u32[]{:S(2)}) collective-permute-start(bf16[8,8192]{1,0:T(8,128)(2,1)S(1)} %add_convert_fusion.3.refs_0_), channel_id=1, source_target_pairs={{0,16},{8,24},{16,0},{24,8},{1,17},{9,25},{17,1},{25,9},{2,18},{10... | collective-permute-start | bytes 393224 | tf_op jit(solution)/shard_map/ppermute | solution.py:22
  38.7 5.0 %collective-permute-start.17 = (bf16[8,8192]{1,0:T(8,128)(2,1)S(1)}, bf16[8,8192]{1,0:T(8,128)(2,1)S(1)}, u32[]{:S(2)}, u32[]{:S(2)}) collective-permute-start(bf16[8,8192]{1,0:T(8,128)(2,1)S(1)} %add_convert_fusion.2.refs_2_), channel_id=1, source_target_pairs={{0,8},{8,0},{16,24},{24,16},{1,9},{9,1},{17,25},{25,17},{2,10},{10... | collective-permute-start | bytes 393224 | tf_op jit(solution)/shard_map/ppermute | solution.py:22
  45.7 6.3 %collective-permute-start.20 = (bf16[128,256]{1,0:T(8,128)(2,1)S(1)}, bf16[128,256]{1,0:T(8,128)(2,1)S(1)}, u32[]{:S(2)}, u32[]{:S(2)}) collective-permute-start(bf16[128,256]{1,0:T(8,128)(2,1)S(1)} %get-tuple-element.15.refs_0_), channel_id=1, source_target_pairs={{0,6},{1,7},{2,4},{3,5},{4,2},{5,3},{6,0},{7,1},{8,14},{9,15},{10,... | collective-permute-start | bytes 196616 | tf_op jit(solution)/shard_map/ppermute | solution.py:22
  48.1 5.2 %collective-permute-start.19 = (bf16[128,256]{1,0:T(8,128)(2,1)S(1)}, bf16[128,256]{1,0:T(8,128)(2,1)S(1)}, u32[]{:S(2)}, u32[]{:S(2)}) collective-permute-start(bf16[128,256]{1,0:T(8,128)(2,1)S(1)} %get-tuple-element.15.refs_0_), channel_id=1, source_target_pairs={{0,4},{1,5},{2,6},{3,7},{4,0},{5,1},{6,2},{7,3},{8,12},{9,13},{10,... | collective-permute-start | bytes 196616 | tf_op jit(solution)/shard_map/ppermute | solution.py:22
  48.1 5.2 %collective-permute-start.18 = (bf16[128,256]{1,0:T(8,128)(2,1)S(1)}, bf16[128,256]{1,0:T(8,128)(2,1)S(1)}, u32[]{:S(2)}, u32[]{:S(2)}) collective-permute-start(bf16[128,256]{1,0:T(8,128)(2,1)S(1)} %get-tuple-element.15.refs_0_), channel_id=1, source_target_pairs={{0,2},{1,3},{2,0},{3,1},{4,6},{5,7},{6,4},{7,5},{8,10},{9,11},{10,... | collective-permute-start | bytes 196616 | tf_op jit(solution)/shard_map/ppermute | solution.py:22
  50.1 3.8 %collective-permute-start.21 = (bf16[128,256]{1,0:T(8,128)(2,1)S(1)}, bf16[128,256]{1,0:T(8,128)(2,1)S(1)}, u32[]{:S(2)}, u32[]{:S(2)}) collective-permute-start(bf16[128,256]{1,0:T(8,128)(2,1)S(1)} %get-tuple-element.15.refs_0_), channel_id=1, source_target_pairs={{0,1},{1,0},{2,3},{3,2},{4,5},{5,4},{6,7},{7,6},{8,9},{9,8},{10,11... | collective-permute-start | bytes 196616 | tf_op jit(solution)/shard_map/ppermute | solution.py:22
  52.0 1.9 %collective-permute-start.24 = (bf16[128,256]{1,0:T(8,128)(2,1)S(1)}, bf16[128,256]{1,0:T(8,128)(2,1)S(1)}, u32[]{:S(2)}, u32[]{:S(2)}) collective-permute-start(bf16[128,256]{1,0:T(8,128)(2,1)S(1)} %collective-permute-done.20.refs_3_), channel_id=1, source_target_pairs={{0,1},{1,0},{2,3},{3,2},{4,5},{5,4},{6,7},{7,6},{8,9},{9,8},{10,11... | collective-permute-start | bytes 196616 | tf_op jit(solution)/shard_map/ppermute | solution.py:22
  53.3 1.3 %collective-permute-start.23 = (bf16[128,256]{1,0:T(8,128)(2,1)S(1)}, bf16[128,256]{1,0:T(8,128)(2,1)S(1)}, u32[]{:S(2)}, u32[]{:S(2)}) collective-permute-start(bf16[128,256]{1,0:T(8,128)(2,1)S(1)} %collective-permute-done.19.refs_2_), channel_id=1, source_target_pairs={{0,1},{1,0},{2,3},{3,2},{4,5},{5,4},{6,7},{7,6},{8,9},{9,8},{10,11... | collective-permute-start | bytes 196616 | tf_op jit(solution)/shard_map/ppermute | solution.py:22
  53.3 1.4 %collective-permute-start.22 = (bf16[128,256]{1,0:T(8,128)(2,1)S(1)}, bf16[128,256]{1,0:T(8,128)(2,1)S(1)}, u32[]{:S(2)}, u32[]{:S(2)}) collective-permute-start(bf16[128,256]{1,0:T(8,128)(2,1)S(1)} %collective-permute-done.18.refs_1_), channel_id=1, source_target_pairs={{0,1},{1,0},{2,3},{3,2},{4,5},{5,4},{6,7},{7,6},{8,9},{9,8},{10,11... | collective-permute-start | bytes 196616 | tf_op jit(solution)/shard_map/ppermute | solution.py:22
  55.1 24.3 %copy-start.12 = (f32[8,16384]{1,0:T(8,128)S(1)}, f32[8,16384]{1,0:T(8,128)}, u32[]{:S(2)}) copy-start(f32[8,16384]{1,0:T(8,128)} %get-tuple-element.8) | copy-start | bytes 1572868
  55.1 6.9 %collective-permute-start.27 = (bf16[128,256]{1,0:T(8,128)(2,1)S(1)}, bf16[128,256]{1,0:T(8,128)(2,1)S(1)}, u32[]{:S(2)}, u32[]{:S(2)}) collective-permute-start(bf16[128,256]{1,0:T(8,128)(2,1)S(1)} %nodes.3.refs_0_), channel_id=1, source_target_pairs={{0,6},{1,7},{2,4},{3,5},{4,2},{5,3},{6,0},{7,1},{8,14},{9,15},{10,... | collective-permute-start | bytes 196616 | tf_op jit(solution)/shard_map/ppermute | solution.py:22
  57.4 6.7 %collective-permute-start.26 = (bf16[128,256]{1,0:T(8,128)(2,1)S(1)}, bf16[128,256]{1,0:T(8,128)(2,1)S(1)}, u32[]{:S(2)}, u32[]{:S(2)}) collective-permute-start(bf16[128,256]{1,0:T(8,128)(2,1)S(1)} %nodes.3.refs_0_), channel_id=1, source_target_pairs={{0,4},{1,5},{2,6},{3,7},{4,0},{5,1},{6,2},{7,3},{8,12},{9,13},{10,... | collective-permute-start | bytes 196616 | tf_op jit(solution)/shard_map/ppermute | solution.py:22
  57.5 6.7 %collective-permute-start.25 = (bf16[128,256]{1,0:T(8,128)(2,1)S(1)}, bf16[128,256]{1,0:T(8,128)(2,1)S(1)}, u32[]{:S(2)}, u32[]{:S(2)}) collective-permute-start(bf16[128,256]{1,0:T(8,128)(2,1)S(1)} %nodes.3.refs_0_), channel_id=1, source_target_pairs={{0,2},{1,3},{2,0},{3,1},{4,6},{5,7},{6,4},{7,5},{8,10},{9,11},{10,... | collective-permute-start | bytes 196616 | tf_op jit(solution)/shard_map/ppermute | solution.py:22
  59.5 5.1 %collective-permute-start.28 = (bf16[128,256]{1,0:T(8,128)(2,1)S(1)}, bf16[128,256]{1,0:T(8,128)(2,1)S(1)}, u32[]{:S(2)}, u32[]{:S(2)}) collective-permute-start(bf16[128,256]{1,0:T(8,128)(2,1)S(1)} %nodes.3.refs_0_), channel_id=1, source_target_pairs={{0,1},{1,0},{2,3},{3,2},{4,5},{5,4},{6,7},{7,6},{8,9},{9,8},{10,11... | collective-permute-start | bytes 196616 | tf_op jit(solution)/shard_map/ppermute | solution.py:22
  62.0 2.6 %collective-permute-start.31 = (bf16[128,256]{1,0:T(8,128)(2,1)S(1)}, bf16[128,256]{1,0:T(8,128)(2,1)S(1)}, u32[]{:S(2)}, u32[]{:S(2)}) collective-permute-start(bf16[128,256]{1,0:T(8,128)(2,1)S(1)} %collective-permute-done.27.refs_3_), channel_id=1, source_target_pairs={{0,1},{1,0},{2,3},{3,2},{4,5},{5,4},{6,7},{7,6},{8,9},{9,8},{10,11... | collective-permute-start | bytes 196616 | tf_op jit(solution)/shard_map/ppermute | solution.py:22
  64.1 1.3 %collective-permute-start.30 = (bf16[128,256]{1,0:T(8,128)(2,1)S(1)}, bf16[128,256]{1,0:T(8,128)(2,1)S(1)}, u32[]{:S(2)}, u32[]{:S(2)}) collective-permute-start(bf16[128,256]{1,0:T(8,128)(2,1)S(1)} %collective-permute-done.26.refs_2_), channel_id=1, source_target_pairs={{0,1},{1,0},{2,3},{3,2},{4,5},{5,4},{6,7},{7,6},{8,9},{9,8},{10,11... | collective-permute-start | bytes 196616 | tf_op jit(solution)/shard_map/ppermute | solution.py:22
  64.1 1.4 %collective-permute-start.29 = (bf16[128,256]{1,0:T(8,128)(2,1)S(1)}, bf16[128,256]{1,0:T(8,128)(2,1)S(1)}, u32[]{:S(2)}, u32[]{:S(2)}) collective-permute-start(bf16[128,256]{1,0:T(8,128)(2,1)S(1)} %collective-permute-done.25.refs_1_), channel_id=1, source_target_pairs={{0,1},{1,0},{2,3},{3,2},{4,5},{5,4},{6,7},{7,6},{8,9},{9,8},{10,11... | collective-permute-start | bytes 196616 | tf_op jit(solution)/shard_map/ppermute | solution.py:22
  67.3 5.8 %collective-permute-start.32 = (bf16[8,8192]{1,0:T(8,128)(2,1)S(1)}, bf16[8,8192]{1,0:T(8,128)(2,1)S(1)}, u32[]{:S(2)}, u32[]{:S(2)}) collective-permute-start(bf16[8,8192]{1,0:T(8,128)(2,1)S(1)} %get-tuple-element.16), channel_id=1, source_target_pairs={{0,8},{8,0},{16,24},{24,16},{1,9},{9,1},{17,25},{25,17},{2,10},{10... | collective-permute-start | bytes 393224 | tf_op jit(solution)/shard_map/ppermute | solution.py:22
  68.8 5.5 %collective-permute-start.34 = (bf16[8,8192]{1,0:T(8,128)(2,1)S(1)}, bf16[8,8192]{1,0:T(8,128)(2,1)S(1)}, u32[]{:S(2)}, u32[]{:S(2)}) collective-permute-start(bf16[8,8192]{1,0:T(8,128)(2,1)S(1)} %get-tuple-element.17), channel_id=1, source_target_pairs={{0,16},{8,24},{16,0},{24,8},{1,17},{9,25},{17,1},{25,9},{2,18},{10... | collective-permute-start | bytes 393224 | tf_op jit(solution)/shard_map/ppermute | solution.py:22
  73.1 5.0 %collective-permute-start.33 = (bf16[8,8192]{1,0:T(8,128)(2,1)S(1)}, bf16[8,8192]{1,0:T(8,128)(2,1)S(1)}, u32[]{:S(2)}, u32[]{:S(2)}) collective-permute-start(bf16[8,8192]{1,0:T(8,128)(2,1)S(1)} %add_convert_fusion.1), channel_id=1, source_target_pairs={{0,16},{8,24},{16,0},{24,8},{1,17},{9,25},{17,1},{25,9},{2,18},{10... | collective-permute-start | bytes 393224 | tf_op jit(solution)/shard_map/ppermute | solution.py:22
  74.3 5.0 %collective-permute-start.35 = (bf16[8,8192]{1,0:T(8,128)(2,1)S(1)}, bf16[8,8192]{1,0:T(8,128)(2,1)S(1)}, u32[]{:S(2)}, u32[]{:S(2)}) collective-permute-start(bf16[8,8192]{1,0:T(8,128)(2,1)S(1)} %add_convert_fusion), channel_id=1, source_target_pairs={{0,8},{8,0},{16,24},{24,16},{1,9},{9,1},{17,25},{25,17},{2,10},{10... | collective-permute-start | bytes 393224 | tf_op jit(solution)/shard_map/ppermute | solution.py:22
  (1 other events, 0.8 us)

commit v5 on v4

--- a/solution.py
+++ b/solution.py
@@ -9,8 +9,10 @@
 
 
 TILE = 64
+EXTRA = 16
+PAIR = 4
 LANES = 128
-FIRST_BYTES = 55040 * 1024
+FIRST_BYTES = 55136 * 1024
 VMEM_BYTES = 40 * 1024 * 1024
 TABLE_BYTES = 32 * 1024 * 1024
 HALF = jnp.bfloat16
@@ -22,20 +24,44 @@
     return lax.ppermute(array, axis, [(i, i ^ mask) for i in range(size)])
 
 
-def slot_masks():
-    return (0, 2, 4, 6, 1, 3, 5, 7) if lax.axis_size("col") == 8 else None
+def is_paired():
+    return lax.axis_size("col") == 8
 
 
 def slot_source(masks, myself, slot):
     return slot if masks is None else myself ^ masks[slot]
 
 
-def gather_slots(array):
-    if slot_masks() is not None:
-        same_core = [array] + [swap(array, "col", mask) for mask in (2, 4, 6)]
-        return same_core + [swap(p, "col", 1) for p in same_core]
+def tile_masks():
+    return (0, 2, 4, 6, 1, 3, 5, 7) if is_paired() else None
+
+
+def node_masks():
+    return (0, 4, 2, 6, 1, 5, 3, 7) if is_paired() else None
+
+
+def gather_all(array):
     stacked = lax.all_gather(array, "col")
     return [stacked[i] for i in range(lax.axis_size("col"))]
+
+
+def gather_tiles(array):
+    if not is_paired():
+        return gather_all(array)
+    same_core = [array] + [swap(array, "col", mask) for mask in (2, 4, 6)]
+    return same_core + [swap(p, "col", 1) for p in same_core]
+
+
+def gather_nodes(array):
+    if not is_paired():
+        return gather_all(array)
+    same_core = [array] + [swap(array, "col", mask) for mask in (4, 2, 6)]
+    return same_core + [swap(p, "col", 1) for p in same_core]
+
+
+def gather_pairs(array):
+    same_core = [array, swap(array, "col", 2)]
+    return same_core + [swap(p, "col", 1) for p in same_core]
 
 
 def tile_indicator(tiles, columns):
@@ -167,12 +193,21 @@
     )(columns, ensemble, state, climate, weight, *sums)
 
 
-def matrix_kernel(masks, myself_ref, near_ref, dest_ref, local_ref, conv_ref, matrix_ref):
+def matrix_kernel(masks, paired, myself_ref, near_ref, dest_ref, local_ref, conv_ref, matrix_ref):
     blocks, neigh, size, _ = conv_ref.shape
     nodes = blocks * size
     rows = [
         jnp.concatenate([conv_ref[b, k] for k in range(neigh)], axis=1) for b in range(blocks)
     ]
+    if paired:
+        numbers = near_ref[near_ref.shape[0] - EXTRA :, :].astype(FULL).astype(jnp.int32)
+        near = {
+            (b, k): jnp.broadcast_to(numbers[b : b + 1, k : k + 1], (1, nodes))
+            for b in range(blocks)
+            for k in range(neigh)
+        }
+    else:
+        near = {(b, k): near_ref[b, k] for b in range(blocks) for k in range(neigh)}
     row = lax.broadcasted_iota(jnp.int32, (size, nodes), 0)
     for s in range(dest_ref.shape[1] // nodes):
         source = slot_source(masks, myself_ref[0], s)
@@ -180,23 +215,23 @@
         tile_node = dest_ref[:, span] * nodes + local_ref[:, span]
         for b in range(blocks):
             place = jnp.concatenate(
-                [ones_where(row == tile_node - near_ref[b, k] * size) for k in range(neigh)], axis=0
+                [ones_where(row == tile_node - near[b, k] * size) for k in range(neigh)], axis=0
             )
             block = jnp.dot(rows[b], place, preferred_element_type=FULL)
             matrix_ref[s * nodes : (s + 1) * nodes, b * size : (b + 1) * size] = block.T.astype(HALF)
 
 
-def run_matrix(myself, neighbours, dest, local, conv_blocks):
+def run_matrix(myself, near, dest, local, conv_blocks, paired):
     blocks, _, size, _ = conv_blocks.shape
     scalars = pl.BlockSpec(memory_space=pltpu.SMEM)
     return pl.pallas_call(
-        functools.partial(matrix_kernel, slot_masks()),
-        in_specs=[scalars, scalars] + whole(3),
+        functools.partial(matrix_kernel, tile_masks(), paired),
+        in_specs=[scalars, whole(1)[0] if paired else scalars] + whole(3),
         out_specs=whole(1)[0],
         out_shape=jax.ShapeDtypeStruct((dest.shape[1], blocks * size), HALF),
         compiler_params=params(TABLE_BYTES),
-        name="node_matrix",
-    )(myself, neighbours, dest, local, conv_blocks)
+        name="pair_matrix" if paired else "node_matrix",
+    )(myself, near, dest, local, conv_blocks)
 
 
 def select_kernel(masks, nodes, myself_ref, dest_ref, local_ref, select_ref):
@@ -215,7 +250,7 @@
 
 def run_select(myself, dest, local, nodes):
     return pl.pallas_call(
-        functools.partial(select_kernel, slot_masks(), nodes),
+        functools.partial(select_kernel, node_masks(), nodes),
         in_specs=[pl.BlockSpec(memory_space=pltpu.SMEM)] + whole(2),
         out_specs=whole(1)[0],
         out_shape=jax.ShapeDtypeStruct((dest.shape[1], 2 * nodes), HALF),
@@ -224,29 +259,64 @@
     )(myself, dest, local)
 
 
-def slot_product(piece_refs, matrix_ref):
+def slot_product(feature, piece_refs, matrix_ref):
     span = piece_refs[0].shape[1]
-    total = jnp.zeros((piece_refs[0].shape[0], matrix_ref.shape[1]), FULL)
+    total = jnp.zeros((feature, matrix_ref.shape[1]), FULL)
     for s, piece in enumerate(piece_refs):
         total = total + jnp.dot(
-            piece[...], matrix_ref[s * span : (s + 1) * span, :], preferred_element_type=FULL
+            piece[0:feature, :],
+            matrix_ref[s * span : (s + 1) * span, :],
+            preferred_element_type=FULL,
         )
     return total
 
 
-def nodes_kernel(matrix_ref, *refs):
-    refs[-1][...] = slot_product(refs[:-1], matrix_ref).astype(HALF)
-
-
-def run_nodes(matrix, partial_all):
+def nodes_kernel(near_ref, matrix_ref, *refs):
+    piece_refs, out_ref = refs[:-1], refs[-1]
+    feature = piece_refs[0].shape[0]
+    out_ref[0:feature, :] = slot_product(feature, piece_refs, matrix_ref).astype(HALF)
+    blocks, neigh = near_ref.shape
+    extra = (EXTRA, out_ref.shape[1])
+    row = lax.broadcasted_iota(jnp.int32, extra, 0)
+    lane = lax.broadcasted_iota(jnp.int32, extra, 1)
+    numbers = jnp.zeros(extra, jnp.int32)
+    for b in range(blocks):
+        for k in range(neigh):
+            numbers = jnp.where((row == b) & (lane == k), near_ref[b, k], numbers)
+    out_ref[feature:, :] = numbers.astype(FULL).astype(HALF)
+
+
+def run_nodes(neighbours, matrix, partial_all):
+    feature = partial_all[0].shape[0]
     return pl.pallas_call(
         nodes_kernel,
-        in_specs=whole(1 + len(partial_all)),
+        in_specs=[pl.BlockSpec(memory_space=pltpu.SMEM)] + whole(1 + len(partial_all)),
         out_specs=whole(1)[0],
-        out_shape=jax.ShapeDtypeStruct((partial_all[0].shape[0], matrix.shape[1]), HALF),
+        out_shape=jax.ShapeDtypeStruct((feature + EXTRA, matrix.shape[1]), HALF),
         compiler_params=params(TABLE_BYTES),
         name="nodes",
-    )(matrix, *partial_all)
+    )(neighbours, matrix, *partial_all)
+
+
+def pair_nodes_kernel(count, *refs):
+    matrix_refs, piece_refs, out_ref = refs[:count], refs[count:-1], refs[-1]
+    width = matrix_refs[0].shape[1]
+    for i, matrix_ref in enumerate(matrix_refs):
+        out_ref[:, i * width : (i + 1) * width] = slot_product(
+            out_ref.shape[0], piece_refs, matrix_ref
+        ).astype(HALF)
+
+
+def run_pair_nodes(matrices, partial_all):
+    feature = partial_all[0].shape[0]
+    return pl.pallas_call(
+        functools.partial(pair_nodes_kernel, len(matrices)),
+        in_specs=whole(len(matrices) + len(partial_all)),
+        out_specs=whole(1)[0],
+        out_shape=jax.ShapeDtypeStruct((feature, sum(m.shape[1] for m in matrices)), HALF),
+        compiler_params=params(TABLE_BYTES),
+        name="pair_nodes",
+    )(*matrices, *partial_all)
 
 
 def expansion_kernel(width, weight_ref, expand_ref, columns_ref):
@@ -291,7 +361,7 @@
     tiles = width // TILE
     feature = members * levels
     pairs = select_ref.shape[1]
-    values = slot_product(node_refs, select_ref)
+    values = slot_product(feature, node_refs, select_ref)
     lane = lax.broadcasted_iota(jnp.int32, (feature, LANES), 1)
     group = LANES // tiles
     for i in range(steps):
@@ -366,17 +436,24 @@
     scale = 1.0 / (members * lax.axis_size("mem") - 1)
     weight = restrict_weight[None, :]
 
-    partial_all = gather_slots(run_first(increment, weight, ensemble))
-    matrix = run_matrix(
-        myself, neighbours, restrict_dest.reshape(1, -1), restrict_local.reshape(1, -1), conv_blocks
-    )
+    tables = [restrict_dest.reshape(1, -1), restrict_local.reshape(1, -1)]
+
+    partial_all = gather_tiles(run_first(increment, weight, ensemble))
+    matrix = run_matrix(myself, neighbours, *tables, conv_blocks, False)
     select = run_select(myself, interp_dest.T, interp_local.T, nodes)
     expand, columns = run_expansion(column_sizes(ensemble)[3], interp_weight)
 
-    nodes_all = gather_slots(run_nodes(matrix, partial_all))
+    nodes_all = gather_nodes(run_nodes(neighbours, matrix, partial_all))
     sums = member_sum(run_spread(select, ensemble, expand, nodes_all))
     once_applied, partial = run_second(scale, columns, increment, climate, sums, weight, ensemble)
-    nodes_all = gather_slots(run_nodes(matrix, gather_slots(partial)))
+    partial_all = gather_tiles(partial)
+    if is_paired():
+        carrier = nodes_all[node_masks().index(PAIR)]
+        conv_pair = swap(conv_blocks, "col", PAIR)
+        matrices = [matrix, run_matrix(myself, carrier, *tables, conv_pair, True)]
+        nodes_all = gather_pairs(run_pair_nodes(matrices, partial_all))
+    else:
+        nodes_all = gather_nodes(run_pair_nodes([matrix], partial_all))
     sums = member_sum(run_spread(select, ensemble, expand, nodes_all))
     total = jnp.concatenate(
         [sums[2 * i].astype(FULL) + sums[2 * i + 1].astype(FULL) for i in range(2)], axis=1

time: 80.5 us -> 82.7 us (1.027)
  waiting for transfers between devices: 32.8 us -> 36.6 us
  starting transfers between devices: 31.4 us -> 28.9 us
  Pallas kernels: 13.1 us -> 14.9 us
  local copies, waits for them, and re-layouts: 0.9 us -> 0.06 us
    ppermute x36 -> x33, waiting for transfers between devices: 32.8 us -> 36.6 us  [swap(): return lax.ppermute(array, axis, [(i, i ^ mask) for i in range(size)])]
    ppermute x36 -> x33, starting transfers between devices: 31.4 us -> 28.9 us  [swap(): return lax.ppermute(array, axis, [(i, i ^ mask) for i in range(size)])]
    pallas_call x4 -> x5, Pallas kernels: 2.47 us -> 4.25 us  [the longest x2 2.57 us: run_matrix(): pl.pallas_call(functools.partial(matrix_kernel, tile_masks(), paired), in...]
    unnamed x26 -> x24, local copies, waits for them, and re-layouts: 0.9 us -> 0.06 us
  transfers between devices with their start and end apart: 36 -> 33, of which waited for: 18 -> 14; matrix products, arithmetic and copies ran while one was open for 0% -> 0% of each run, Pallas kernels for 4% -> 8%
where the time goes in v5:
time: 82.7 us; the launch traced here: 82.6 us
  waiting for transfers between devices  36.6 us (44%)
  starting transfers between devices  28.9 us (35%)
  Pallas kernels  14.9 us (18%)
  other arithmetic  1.07 us (1%)
  between operations  1 us (1%)
    ppermute x33, waiting for transfers between devices, swap(): return lax.ppermute(array, axis, [(i, i ^ mask) for i in range(size)])  36.6 us
    ppermute x33, starting transfers between devices, swap(): return lax.ppermute(array, axis, [(i, i ^ mask) for i in range(size)])  28.9 us
    pallas_call x1, Pallas kernels, run_first(): pl.pallas_call(functools.partial(first_kernel, width), in_specs=[pl.Block...  3.91 us
    pallas_call x2, Pallas kernels, run_spread(): pl.pallas_call(functools.partial(spread_kernel, slots), in_specs=whole(3...  3.46 us
    pallas_call x2, Pallas kernels, run_matrix(): pl.pallas_call(functools.partial(matrix_kernel, tile_masks(), paired), in...  2.57 us
    pallas_call x1, Pallas kernels, run_second(): pl.pallas_call(functools.partial(second_kernel, width, scale), in_specs=w...  1.95 us
  transfers between devices with their start and end apart: 33, of which 14 were waited for; matrix products, arithmetic and copies ran while one was open for 0% of the time, Pallas kernels for 8%

profile of v5, /device:TPU:0, one launch (start us, length us, event | category | flops | bytes accessed | tf_op | source)
XLA Modules:
  0.0 82.6 jit_solution(7160748835599590218)
XLA Ops:
  0.7 3.9 %tile_sums_first.1.refs_0_ = bf16[128,256]{1,0:T(8,128)(2,1)S(1)} custom-call(f32[8,16384]{1,0:T(8,128)} %state_ref.1, f32[1,16384]{1,0:T(1,128)} %bitcast.6, bf16[16,8,16384]{2,1,0:T(8,128)(2,1)} %ensemble_ref.5), custom_call_target="tpu_custom_call" | custom-call | tf_op jit(solution)/shard_map/tile_sums_first/pallas_call | solution.py:145
  4.6 3.1 %collective-permute-start = (bf16[128,256]{1,0:T(8,128)(2,1)S(1)}, bf16[128,256]{1,0:T(8,128)(2,1)S(1)}, u32[]{:S(2)}, u32[]{:S(2)}) collective-permute-start(bf16[128,256]{1,0:T(8,128)(2,1)S(1)} %tile_sums_first.1.refs_0_), channel_id=1, source_target_pairs={{0,2},{1,3},{2,0},{3,1},{4,6},{5,7},{6,4},{7,5},{8,10},{9,11},{10,... | collective-permute-start | bytes 196616 | tf_op jit(solution)/shard_map/ppermute | solution.py:24
  7.7 2.6 %collective-permute-start.1 = (bf16[128,256]{1,0:T(8,128)(2,1)S(1)}, bf16[128,256]{1,0:T(8,128)(2,1)S(1)}, u32[]{:S(2)}, u32[]{:S(2)}) collective-permute-start(bf16[128,256]{1,0:T(8,128)(2,1)S(1)} %tile_sums_first.1.refs_0_), channel_id=1, source_target_pairs={{0,4},{1,5},{2,6},{3,7},{4,0},{5,1},{6,2},{7,3},{8,12},{9,13},{10,... | collective-permute-start | bytes 196616 | tf_op jit(solution)/shard_map/ppermute | solution.py:24
  10.3 0.5 collective-permute-start.4
  10.8 4.2 %collective-permute-done.1.refs_2_ = bf16[128,256]{1,0:T(8,128)(2,1)S(1)} collective-permute-done((bf16[128,256]{1,0:T(8,128)(2,1)S(1)}, bf16[128,256]{1,0:T(8,128)(2,1)S(1)}, u32[]{:S(2)}, u32[]{:S(2)}) %collective-permute-start.1) | collective-permute-done | bytes 65568 | tf_op jit(solution)/shard_map/ppermute | solution.py:24
  15.0 1.4 %collective-permute-done.2.refs_3_ = bf16[128,256]{1,0:T(8,128)(2,1)S(1)} collective-permute-done((bf16[128,256]{1,0:T(8,128)(2,1)S(1)}, bf16[128,256]{1,0:T(8,128)(2,1)S(1)}, u32[]{:S(2)}, u32[]{:S(2)}) %collective-permute-start.2) | collective-permute-done | bytes 65568 | tf_op jit(solution)/shard_map/ppermute | solution.py:24
  16.4 1.5 %node_matrix.1.matrix_ref.refs_0_ = bf16[2048,256]{1,0:T(8,128)(2,1)S(1)} custom-call(s32[1]{0:T(128)} %bitcast.1.myself_ref, s32[2,4]{1,0:T(2,128)S(1)} %copy-done.10, s32[1,2048]{1,0:T(1,128)S(1)} %bitcast.8, s32[1,2048]{1,0:T(1,128)S(1)} %bitcast.10, bf16[2,4,128,128]{3,2,1,0:T(8,128)(2,1)S(1)} %copy-done.4), custom_call_target="tpu_custom_call" | custom-call | tf_op jit(solution)/shard_map/node_matrix/pallas_call | solution.py:227
  18.0 0.9 %nodes.1.refs_0_ = bf16[144,256]{1,0:T(8,128)(2,1)S(1)} custom-call(s32[2,4]{1,0:T(2,128)S(1)} %copy-done.10, bf16[2048,256]{1,0:T(8,128)(2,1)S(1)} %node_matrix.1.matrix_ref.refs_0_, bf16[128,256]{1,0:T(8,128)(2,1)S(1)} %tile_sums_first.1.refs_0_, bf16[128,256]{1,0:T(8,128)(2,1)S(1)} %collective-permute-done.refs_1_, ...), custom_call_target="tpu_custom_call" | custom-call | tf_op jit(solution)/shard_map/nodes/pallas_call | solution.py:291
  18.9 1.6 %collective-permute-start.7 = (bf16[144,256]{1,0:T(8,128)(2,1)S(1)}, bf16[144,256]{1,0:T(8,128)(2,1)S(1)}, u32[]{:S(2)}, u32[]{:S(2)}) collective-permute-start(bf16[144,256]{1,0:T(8,128)(2,1)S(1)} %nodes.1.refs_0_), channel_id=1, source_target_pairs={{0,4},{1,5},{2,6},{3,7},{4,0},{5,1},{6,2},{7,3},{8,12},{9,13},{10,... | collective-permute-start | bytes 221192 | tf_op jit(solution)/shard_map/ppermute | solution.py:24
  20.5 1.3 %collective-permute-start.8 = (bf16[144,256]{1,0:T(8,128)(2,1)S(1)}, bf16[144,256]{1,0:T(8,128)(2,1)S(1)}, u32[]{:S(2)}, u32[]{:S(2)}) collective-permute-start(bf16[144,256]{1,0:T(8,128)(2,1)S(1)} %nodes.1.refs_0_), channel_id=1, source_target_pairs={{0,2},{1,3},{2,0},{3,1},{4,6},{5,7},{6,4},{7,5},{8,10},{9,11},{10,... | collective-permute-start | bytes 221192 | tf_op jit(solution)/shard_map/ppermute | solution.py:24
  21.8 1.6 %collective-permute-start.9 = (bf16[144,256]{1,0:T(8,128)(2,1)S(1)}, bf16[144,256]{1,0:T(8,128)(2,1)S(1)}, u32[]{:S(2)}, u32[]{:S(2)}) collective-permute-start(bf16[144,256]{1,0:T(8,128)(2,1)S(1)} %nodes.1.refs_0_), channel_id=1, source_target_pairs={{0,6},{1,7},{2,4},{3,5},{4,2},{5,3},{6,0},{7,1},{8,14},{9,15},{10,... | collective-permute-start | bytes 221192 | tf_op jit(solution)/shard_map/ppermute | solution.py:24
  23.3 2.2 %collective-permute-done.7.refs_1_.near_ref = bf16[144,256]{1,0:T(8,128)(2,1)S(1)} collective-permute-done((bf16[144,256]{1,0:T(8,128)(2,1)S(1)}, bf16[144,256]{1,0:T(8,128)(2,1)S(1)}, u32[]{:S(2)}, u32[]{:S(2)}) %collective-permute-start.7) | collective-permute-done | bytes 73760 | tf_op jit(solution)/shard_map/ppermute | solution.py:24
  25.5 0.0 collective-permute-start.11
  25.5 1.7 %collective-permute-done.8.refs_2_ = bf16[144,256]{1,0:T(8,128)(2,1)S(1)} collective-permute-done((bf16[144,256]{1,0:T(8,128)(2,1)S(1)}, bf16[144,256]{1,0:T(8,128)(2,1)S(1)}, u32[]{:S(2)}, u32[]{:S(2)}) %collective-permute-start.8) | collective-permute-done | bytes 73760 | tf_op jit(solution)/shard_map/ppermute | solution.py:24
  27.3 0.8 collective-permute-done.9.refs_3_
  28.0 1.4 %expansion.1 = (bf16[8,128,2048]{2,1,0:T(8,128)(2,1)S(1)}, bf16[2048,32]{1,0:T(8,128)(2,1)S(1)}) custom-call(f32[2,16384]{1,0:T(2,128)S(1)} %copy-done.5), custom_call_target="tpu_custom_call" | custom-call | tf_op jit(solution)/shard_map/expansion/pallas_call | solution.py:344
  29.4 0.4 selection.1.select_ref
  29.9 1.7 %spread.2 = (bf16[8,8192]{1,0:T(8,128)(2,1)S(1)}, bf16[8,8192]{1,0:T(8,128)(2,1)S(1)}) custom-call(bf16[16,8,16384]{2,1,0:T(8,128)(2,1)S(1)} %copy-done, bf16[2048,512]{1,0:T(8,128)(2,1)S(1)} %selection.1.select_ref, bf16[8,128,2048]{2,1,0:T(8,128)(2,1)S(1)} %get-tuple-element.11.expand_ref, bf16[144,256]{1,0:T(8,128)(2,1)S(1)} %nodes.1.refs_0_, ...), custom_call_target="tpu_custom_call" | custom-call | tf_op jit(solution)/shard_map/spread/pallas_call | solution.py:394
  31.6 1.6 %collective-permute-start.14 = (bf16[8,8192]{1,0:T(8,128)(2,1)S(1)}, bf16[8,8192]{1,0:T(8,128)(2,1)S(1)}, u32[]{:S(2)}, u32[]{:S(2)}) collective-permute-start(bf16[8,8192]{1,0:T(8,128)(2,1)S(1)} %get-tuple-element.12), channel_id=1, source_target_pairs={{0,8},{8,0},{16,24},{24,16},{1,9},{9,1},{17,25},{25,17},{2,10},{10... | collective-permute-start | bytes 393224 | tf_op jit(solution)/shard_map/ppermute | solution.py:24
  33.2 1.5 %collective-permute-start.16 = (bf16[8,8192]{1,0:T(8,128)(2,1)S(1)}, bf16[8,8192]{1,0:T(8,128)(2,1)S(1)}, u32[]{:S(2)}, u32[]{:S(2)}) collective-permute-start(bf16[8,8192]{1,0:T(8,128)(2,1)S(1)} %get-tuple-element.13), channel_id=1, source_target_pairs={{0,16},{8,24},{16,0},{24,8},{1,17},{9,25},{17,1},{25,9},{2,18},{10... | collective-permute-start | bytes 393224 | tf_op jit(solution)/shard_map/ppermute | solution.py:24
  34.7 2.9 %collective-permute-done.14 = bf16[8,8192]{1,0:T(8,128)(2,1)S(1)} collective-permute-done((bf16[8,8192]{1,0:T(8,128)(2,1)S(1)}, bf16[8,8192]{1,0:T(8,128)(2,1)S(1)}, u32[]{:S(2)}, u32[]{:S(2)}) %collective-permute-start.14) | collective-permute-done | bytes 131104 | tf_op jit(solution)/shard_map/ppermute | solution.py:24
  37.6 1.6 %collective-permute-start.15 = (bf16[8,8192]{1,0:T(8,128)(2,1)S(1)}, bf16[8,8192]{1,0:T(8,128)(2,1)S(1)}, u32[]{:S(2)}, u32[]{:S(2)}) collective-permute-start(bf16[8,8192]{1,0:T(8,128)(2,1)S(1)} %add_convert_fusion.3.refs_0_), channel_id=1, source_target_pairs={{0,16},{8,24},{16,0},{24,8},{1,17},{9,25},{17,1},{25,9},{2,18},{10... | collective-permute-start | bytes 393224 | tf_op jit(solution)/shard_map/ppermute | solution.py:24
  39.3 1.6 %collective-permute-start.17 = (bf16[8,8192]{1,0:T(8,128)(2,1)S(1)}, bf16[8,8192]{1,0:T(8,128)(2,1)S(1)}, u32[]{:S(2)}, u32[]{:S(2)}) collective-permute-start(bf16[8,8192]{1,0:T(8,128)(2,1)S(1)} %add_convert_fusion.2.refs_2_), channel_id=1, source_target_pairs={{0,8},{8,0},{16,24},{24,16},{1,9},{9,1},{17,25},{25,17},{2,10},{10... | collective-permute-start | bytes 393224 | tf_op jit(solution)/shard_map/ppermute | solution.py:24
  40.8 2.1 %collective-permute-start.18 = (bf16[2,4,128,128]{3,2,1,0:T(8,128)(2,1)S(1)}, bf16[2,4,128,128]{3,2,1,0:T(8,128)(2,1)S(1)}, u32[]{:S(2)}, u32[]{:S(2)}) collective-permute-start(bf16[2,4,128,128]{3,2,1,0:T(8,128)(2,1)S(1)} %copy-done.4), channel_id=1, source_target_pairs={{0,4},{1,5},{2,6},{3,7},{4,0},{5,1},{6,2},{7,3},{8,12},{9,13},{10,... | collective-permute-start | bytes 786440 | tf_op jit(solution)/shard_map/ppermute | solution.py:24
  42.9 1.3 %collective-permute-done.17.refs_3_ = bf16[8,8192]{1,0:T(8,128)(2,1)S(1)} collective-permute-done((bf16[8,8192]{1,0:T(8,128)(2,1)S(1)}, bf16[8,8192]{1,0:T(8,128)(2,1)S(1)}, u32[]{:S(2)}, u32[]{:S(2)}) %collective-permute-start.17) | collective-permute-done | bytes 131104 | tf_op jit(solution)/shard_map/ppermute | solution.py:24
  44.3 1.9 %tile_sums_second.1 = (f32[8,16384]{1,0:T(8,128)}, bf16[128,256]{1,0:T(8,128)(2,1)S(1)}) custom-call(bf16[2048,32]{1,0:T(8,128)(2,1)S(1)} %get-tuple-element.10.columns_ref, bf16[16,8,16384]{2,1,0:T(8,128)(2,1)S(1)} %copy-done, f32[8,16384]{1,0:T(8,128)S(1)} %copy-done.1, f32[8,16384]{1,0:T(8,128)S(1)} %copy-done.2, f32[1,16384]{1,0:T(1,128)S(1)} %bitcast.7, ...), custom_call_target="tpu_custom_call" | custom-call | tf_op jit(solution)/shard_map/tile_sums_second/pallas_call | solution.py:183
  46.3 1.1 %collective-permute-start.19 = (bf16[128,256]{1,0:T(8,128)(2,1)S(1)}, bf16[128,256]{1,0:T(8,128)(2,1)S(1)}, u32[]{:S(2)}, u32[]{:S(2)}) collective-permute-start(bf16[128,256]{1,0:T(8,128)(2,1)S(1)} %get-tuple-element.15.refs_2_), channel_id=1, source_target_pairs={{0,2},{1,3},{2,0},{3,1},{4,6},{5,7},{6,4},{7,5},{8,10},{9,11},{10,... | collective-permute-start | bytes 196616 | tf_op jit(solution)/shard_map/ppermute | solution.py:24
  47.4 1.7 %collective-permute-start.20 = (bf16[128,256]{1,0:T(8,128)(2,1)S(1)}, bf16[128,256]{1,0:T(8,128)(2,1)S(1)}, u32[]{:S(2)}, u32[]{:S(2)}) collective-permute-start(bf16[128,256]{1,0:T(8,128)(2,1)S(1)} %get-tuple-element.15.refs_2_), channel_id=1, source_target_pairs={{0,4},{1,5},{2,6},{3,7},{4,0},{5,1},{6,2},{7,3},{8,12},{9,13},{10,... | collective-permute-start | bytes 196616 | tf_op jit(solution)/shard_map/ppermute | solution.py:24
  49.1 1.6 %collective-permute-start.21 = (bf16[128,256]{1,0:T(8,128)(2,1)S(1)}, bf16[128,256]{1,0:T(8,128)(2,1)S(1)}, u32[]{:S(2)}, u32[]{:S(2)}) collective-permute-start(bf16[128,256]{1,0:T(8,128)(2,1)S(1)} %get-tuple-element.15.refs_2_), channel_id=1, source_target_pairs={{0,6},{1,7},{2,4},{3,5},{4,2},{5,3},{6,0},{7,1},{8,14},{9,15},{10,... | collective-permute-start | bytes 196616 | tf_op jit(solution)/shard_map/ppermute | solution.py:24
  50.6 0.1 collective-permute-done.19.refs_3_
  50.8 0.4 collective-permute-start.23
  51.2 8.3 %collective-permute-done.20.refs_4_ = bf16[128,256]{1,0:T(8,128)(2,1)S(1)} collective-permute-done((bf16[128,256]{1,0:T(8,128)(2,1)S(1)}, bf16[128,256]{1,0:T(8,128)(2,1)S(1)}, u32[]{:S(2)}, u32[]{:S(2)}) %collective-permute-start.20) | collective-permute-done | bytes 65568 | tf_op jit(solution)/shard_map/ppermute | solution.py:24
  59.5 0.5 collective-permute-start.25
  60.0 1.1 %pair_matrix.1.refs_1_ = bf16[2048,256]{1,0:T(8,128)(2,1)S(1)} custom-call(s32[1]{0:T(128)} %bitcast.1.myself_ref, bf16[144,256]{1,0:T(8,128)(2,1)S(1)} %collective-permute-done.7.refs_1_.near_ref, s32[1,2048]{1,0:T(1,128)S(1)} %bitcast.9, s32[1,2048]{1,0:T(1,128)S(1)} %bitcast.11, bf16[2,4,128,128]{3,2,1,0:T(8,128)(2,1)S(1)} %collective-permute-done.18.conv_ref), custom_call_target="tpu_custom_call" | custom-call | tf_op jit(solution)/shard_map/pair_matrix/pallas_call | solution.py:227
  61.1 0.5 pair_nodes.1.refs_0_
  61.6 1.0 %collective-permute-start.26 = (bf16[128,512]{1,0:T(8,128)(2,1)S(1)}, bf16[128,512]{1,0:T(8,128)(2,1)S(1)}, u32[]{:S(2)}, u32[]{:S(2)}) collective-permute-start(bf16[128,512]{1,0:T(8,128)(2,1)S(1)} %pair_nodes.1.refs_0_), channel_id=1, source_target_pairs={{0,2},{1,3},{2,0},{3,1},{4,6},{5,7},{6,4},{7,5},{8,10},{9,11},{10,... | collective-permute-start | bytes 393224 | tf_op jit(solution)/shard_map/ppermute | solution.py:24
  62.6 0.1 collective-permute-start.27
  62.7 4.5 %collective-permute-done.26.refs_1_ = bf16[128,512]{1,0:T(8,128)(2,1)S(1)} collective-permute-done((bf16[128,512]{1,0:T(8,128)(2,1)S(1)}, bf16[128,512]{1,0:T(8,128)(2,1)S(1)}, u32[]{:S(2)}, u32[]{:S(2)}) %collective-permute-start.26) | collective-permute-done | bytes 131104 | tf_op jit(solution)/shard_map/ppermute | solution.py:24
  67.2 1.3 %collective-permute-done.28.refs_3_ = bf16[128,512]{1,0:T(8,128)(2,1)S(1)} collective-permute-done((bf16[128,512]{1,0:T(8,128)(2,1)S(1)}, bf16[128,512]{1,0:T(8,128)(2,1)S(1)}, u32[]{:S(2)}, u32[]{:S(2)}) %collective-permute-start.28) | collective-permute-done | bytes 131104 | tf_op jit(solution)/shard_map/ppermute | solution.py:24
  68.6 1.7 %spread.3 = (bf16[8,8192]{1,0:T(8,128)(2,1)S(1)}, bf16[8,8192]{1,0:T(8,128)(2,1)S(1)}) custom-call(bf16[16,8,16384]{2,1,0:T(8,128)(2,1)S(1)} %copy-done, bf16[2048,512]{1,0:T(8,128)(2,1)S(1)} %selection.1.select_ref, bf16[8,128,2048]{2,1,0:T(8,128)(2,1)S(1)} %get-tuple-element.11.expand_ref, bf16[128,512]{1,0:T(8,128)(2,1)S(1)} %pair_nodes.1.refs_0_, ...), custom_call_target="tpu_custom_call" | custom-call | tf_op jit(solution)/shard_map/spread/pallas_call | solution.py:394
  70.3 0.6 collective-permute-start.31
  70.9 1.1 %collective-permute-start.29 = (bf16[8,8192]{1,0:T(8,128)(2,1)S(1)}, bf16[8,8192]{1,0:T(8,128)(2,1)S(1)}, u32[]{:S(2)}, u32[]{:S(2)}) collective-permute-start(bf16[8,8192]{1,0:T(8,128)(2,1)S(1)} %get-tuple-element.16), channel_id=1, source_target_pairs={{0,8},{8,0},{16,24},{24,16},{1,9},{9,1},{17,25},{25,17},{2,10},{10... | collective-permute-start | bytes 393224 | tf_op jit(solution)/shard_map/ppermute | solution.py:24
  72.0 3.9 %collective-permute-done.31 = bf16[8,8192]{1,0:T(8,128)(2,1)S(1)} collective-permute-done((bf16[8,8192]{1,0:T(8,128)(2,1)S(1)}, bf16[8,8192]{1,0:T(8,128)(2,1)S(1)}, u32[]{:S(2)}, u32[]{:S(2)}) %collective-permute-start.31) | collective-permute-done | bytes 131104 | tf_op jit(solution)/shard_map/ppermute | solution.py:24
  75.9 0.6 collective-permute-start.32
  76.6 1.1 %collective-permute-start.30 = (bf16[8,8192]{1,0:T(8,128)(2,1)S(1)}, bf16[8,8192]{1,0:T(8,128)(2,1)S(1)}, u32[]{:S(2)}, u32[]{:S(2)}) collective-permute-start(bf16[8,8192]{1,0:T(8,128)(2,1)S(1)} %add_convert_fusion.1), channel_id=1, source_target_pairs={{0,16},{8,24},{16,0},{24,8},{1,17},{9,25},{17,1},{25,9},{2,18},{10... | collective-permute-start | bytes 393224 | tf_op jit(solution)/shard_map/ppermute | solution.py:24
  77.8 3.2 %collective-permute-done.32 = bf16[8,8192]{1,0:T(8,128)(2,1)S(1)} collective-permute-done((bf16[8,8192]{1,0:T(8,128)(2,1)S(1)}, bf16[8,8192]{1,0:T(8,128)(2,1)S(1)}, u32[]{:S(2)}, u32[]{:S(2)}) %collective-permute-start.32) | collective-permute-done | bytes 131104 | tf_op jit(solution)/shard_map/ppermute | solution.py:24
  81.0 0.7 collective-permute-done.30
  81.7 0.9 %fusion = f32[8,16384]{1,0:T(8,128)} fusion(f32[8,8192]{1,0:T(8,128)S(1)} %convert_add_fusion, f32[8,8192]{1,0:T(8,128)S(1)} %convert_add_fusion.1, f32[8,16384]{1,0:T(8,128)S(1)} %copy-done.2, f32[8,16384]{1,0:T(8,128)S(1)} %copy-done.11), kind=kLoop, calls=%fused_computation.1 | loop fusion | flops 524288 | bytes 2097152 | tf_op jit(solution)/shard_map/add | solution.py:461
  (59 shorter events, 0.3 us)
Async XLA Ops:
  0.6 15.8 %copy-start.10 = (s32[2,4]{1,0:T(2,128)S(1)}, s32[2,4]{1,0:T(2,128)}, u32[]{:S(2)}) copy-start(s32[2,4]{1,0:T(2,128)} %near_ref.3) | copy-start | bytes 100
  0.6 15.8 %copy-start.6 = (s32[2048,1]{0,1:T(1,128)S(1)}, s32[2048,1]{0,1:T(1,128)}, u32[]{:S(2)}) copy-start(s32[2048,1]{0,1:T(1,128)} %param.14) | copy-start | bytes 24580
  0.7 15.8 %copy-start.7 = (s32[2048]{0:T(1024)S(1)}, s32[2048]{0:T(1024)}, u32[]{:S(2)}) copy-start(s32[2048]{0:T(1024)} %param.15) | copy-start | bytes 24580
  0.7 15.8 %copy-start.4 = (bf16[2,4,128,128]{3,2,1,0:T(8,128)(2,1)S(1)}, bf16[2,4,128,128]{3,2,1,0:T(8,128)(2,1)}, u32[]{:S(2)}) copy-start(bf16[2,4,128,128]{3,2,1,0:T(8,128)(2,1)} %conv_ref.1) | copy-start | bytes 786436
  0.7 27.4 %copy-start.5 = (f32[2,16384]{1,0:T(2,128)S(1)}, f32[2,16384]{1,0:T(2,128)}, u32[]{:S(2)}) copy-start(f32[2,16384]{1,0:T(2,128)} %weight_ref.1) | copy-start | bytes 393220
  0.7 28.7 %copy-start.8 = (s32[2048,2]{0,1:T(2,128)S(1)}, s32[2048,2]{0,1:T(2,128)}, u32[]{:S(2)}) copy-start(s32[2048,2]{0,1:T(2,128)} %param.19) | copy-start | bytes 49156
  0.7 28.7 %copy-start.9 = (s32[2048,2]{0,1:T(2,128)S(1)}, s32[2048,2]{0,1:T(2,128)}, u32[]{:S(2)}) copy-start(s32[2048,2]{0,1:T(2,128)} %param.20) | copy-start | bytes 49156
  4.6 5.7 %collective-permute-start = (bf16[128,256]{1,0:T(8,128)(2,1)S(1)}, bf16[128,256]{1,0:T(8,128)(2,1)S(1)}, u32[]{:S(2)}, u32[]{:S(2)}) collective-permute-start(bf16[128,256]{1,0:T(8,128)(2,1)S(1)} %tile_sums_first.1.refs_0_), channel_id=1, source_target_pairs={{0,2},{1,3},{2,0},{3,1},{4,6},{5,7},{6,4},{7,5},{8,10},{9,11},{10,... | collective-permute-start | bytes 196616 | tf_op jit(solution)/shard_map/ppermute | solution.py:24
  7.7 7.3 %collective-permute-start.1 = (bf16[128,256]{1,0:T(8,128)(2,1)S(1)}, bf16[128,256]{1,0:T(8,128)(2,1)S(1)}, u32[]{:S(2)}, u32[]{:S(2)}) collective-permute-start(bf16[128,256]{1,0:T(8,128)(2,1)S(1)} %tile_sums_first.1.refs_0_), channel_id=1, source_target_pairs={{0,4},{1,5},{2,6},{3,7},{4,0},{5,1},{6,2},{7,3},{8,12},{9,13},{10,... | collective-permute-start | bytes 196616 | tf_op jit(solution)/shard_map/ppermute | solution.py:24
  10.3 6.1 %collective-permute-start.2 = (bf16[128,256]{1,0:T(8,128)(2,1)S(1)}, bf16[128,256]{1,0:T(8,128)(2,1)S(1)}, u32[]{:S(2)}, u32[]{:S(2)}) collective-permute-start(bf16[128,256]{1,0:T(8,128)(2,1)S(1)} %tile_sums_first.1.refs_0_), channel_id=1, source_target_pairs={{0,6},{1,7},{2,4},{3,5},{4,2},{5,3},{6,0},{7,1},{8,14},{9,15},{10,... | collective-permute-start | bytes 196616 | tf_op jit(solution)/shard_map/ppermute | solution.py:24
  10.3 7.6 %collective-permute-start.3 = (bf16[128,256]{1,0:T(8,128)(2,1)S(1)}, bf16[128,256]{1,0:T(8,128)(2,1)S(1)}, u32[]{:S(2)}, u32[]{:S(2)}) collective-permute-start(bf16[128,256]{1,0:T(8,128)(2,1)S(1)} %tile_sums_first.1.refs_0_), channel_id=1, source_target_pairs={{0,1},{1,0},{2,3},{3,2},{4,5},{5,4},{6,7},{7,6},{8,9},{9,8},{10,11... | collective-permute-start | bytes 196616 | tf_op jit(solution)/shard_map/ppermute | solution.py:24
  10.3 7.6 %collective-permute-start.4 = (bf16[128,256]{1,0:T(8,128)(2,1)S(1)}, bf16[128,256]{1,0:T(8,128)(2,1)S(1)}, u32[]{:S(2)}, u32[]{:S(2)}) collective-permute-start(bf16[128,256]{1,0:T(8,128)(2,1)S(1)} %collective-permute-done.refs_1_), channel_id=1, source_target_pairs={{0,1},{1,0},{2,3},{3,2},{4,5},{5,4},{6,7},{7,6},{8,9},{9,8},{10,11... | collective-permute-start | bytes 196616 | tf_op jit(solution)/shard_map/ppermute | solution.py:24
  15.0 3.0 %collective-permute-start.5 = (bf16[128,256]{1,0:T(8,128)(2,1)S(1)}, bf16[128,256]{1,0:T(8,128)(2,1)S(1)}, u32[]{:S(2)}, u32[]{:S(2)}) collective-permute-start(bf16[128,256]{1,0:T(8,128)(2,1)S(1)} %collective-permute-done.1.refs_2_), channel_id=1, source_target_pairs={{0,1},{1,0},{2,3},{3,2},{4,5},{5,4},{6,7},{7,6},{8,9},{9,8},{10,11... | collective-permute-start | bytes 196616 | tf_op jit(solution)/shard_map/ppermute | solution.py:24
  16.4 1.6 %collective-permute-start.6 = (bf16[128,256]{1,0:T(8,128)(2,1)S(1)}, bf16[128,256]{1,0:T(8,128)(2,1)S(1)}, u32[]{:S(2)}, u32[]{:S(2)}) collective-permute-start(bf16[128,256]{1,0:T(8,128)(2,1)S(1)} %collective-permute-done.2.refs_3_), channel_id=1, source_target_pairs={{0,1},{1,0},{2,3},{3,2},{4,5},{5,4},{6,7},{7,6},{8,9},{9,8},{10,11... | collective-permute-start | bytes 196616 | tf_op jit(solution)/shard_map/ppermute | solution.py:24
  16.4 13.4 %copy-start = (bf16[16,8,16384]{2,1,0:T(8,128)(2,1)S(1)}, bf16[16,8,16384]{2,1,0:T(8,128)(2,1)}, u32[]{:S(2)}) copy-start(bf16[16,8,16384]{2,1,0:T(8,128)(2,1)} %ensemble_ref.5) | copy-start | bytes 12582916
  18.9 6.6 %collective-permute-start.7 = (bf16[144,256]{1,0:T(8,128)(2,1)S(1)}, bf16[144,256]{1,0:T(8,128)(2,1)S(1)}, u32[]{:S(2)}, u32[]{:S(2)}) collective-permute-start(bf16[144,256]{1,0:T(8,128)(2,1)S(1)} %nodes.1.refs_0_), channel_id=1, source_target_pairs={{0,4},{1,5},{2,6},{3,7},{4,0},{5,1},{6,2},{7,3},{8,12},{9,13},{10,... | collective-permute-start | bytes 221192 | tf_op jit(solution)/shard_map/ppermute | solution.py:24
  20.5 6.7 %collective-permute-start.8 = (bf16[144,256]{1,0:T(8,128)(2,1)S(1)}, bf16[144,256]{1,0:T(8,128)(2,1)S(1)}, u32[]{:S(2)}, u32[]{:S(2)}) collective-permute-start(bf16[144,256]{1,0:T(8,128)(2,1)S(1)} %nodes.1.refs_0_), channel_id=1, source_target_pairs={{0,2},{1,3},{2,0},{3,1},{4,6},{5,7},{6,4},{7,5},{8,10},{9,11},{10,... | collective-permute-start | bytes 221192 | tf_op jit(solution)/shard_map/ppermute | solution.py:24
  21.8 6.3 %collective-permute-start.9 = (bf16[144,256]{1,0:T(8,128)(2,1)S(1)}, bf16[144,256]{1,0:T(8,128)(2,1)S(1)}, u32[]{:S(2)}, u32[]{:S(2)}) collective-permute-start(bf16[144,256]{1,0:T(8,128)(2,1)S(1)} %nodes.1.refs_0_), channel_id=1, source_target_pairs={{0,6},{1,7},{2,4},{3,5},{4,2},{5,3},{6,0},{7,1},{8,14},{9,15},{10,... | collective-permute-start | bytes 221192 | tf_op jit(solution)/shard_map/ppermute | solution.py:24
  23.3 6.5 %collective-permute-start.10 = (bf16[144,256]{1,0:T(8,128)(2,1)S(1)}, bf16[144,256]{1,0:T(8,128)(2,1)S(1)}, u32[]{:S(2)}, u32[]{:S(2)}) collective-permute-start(bf16[144,256]{1,0:T(8,128)(2,1)S(1)} %nodes.1.refs_0_), channel_id=1, source_target_pairs={{0,1},{1,0},{2,3},{3,2},{4,5},{5,4},{6,7},{7,6},{8,9},{9,8},{10,11... | collective-permute-start | bytes 221192 | tf_op jit(solution)/shard_map/ppermute | solution.py:24
  25.5 4.3 %collective-permute-start.11 = (bf16[144,256]{1,0:T(8,128)(2,1)S(1)}, bf16[144,256]{1,0:T(8,128)(2,1)S(1)}, u32[]{:S(2)}, u32[]{:S(2)}) collective-permute-start(bf16[144,256]{1,0:T(8,128)(2,1)S(1)} %collective-permute-done.7.refs_1_.near_ref), channel_id=1, source_target_pairs={{0,1},{1,0},{2,3},{3,2},{4,5},{5,4},{6,7},{7,6},{8,9},{9,8},{10,11... | collective-permute-start | bytes 221192 | tf_op jit(solution)/shard_map/ppermute | solution.py:24
  27.2 2.6 %collective-permute-start.12 = (bf16[144,256]{1,0:T(8,128)(2,1)S(1)}, bf16[144,256]{1,0:T(8,128)(2,1)S(1)}, u32[]{:S(2)}, u32[]{:S(2)}) collective-permute-start(bf16[144,256]{1,0:T(8,128)(2,1)S(1)} %collective-permute-done.8.refs_2_), channel_id=1, source_target_pairs={{0,1},{1,0},{2,3},{3,2},{4,5},{5,4},{6,7},{7,6},{8,9},{9,8},{10,11... | collective-permute-start | bytes 221192 | tf_op jit(solution)/shard_map/ppermute | solution.py:24
  28.0 1.8 %collective-permute-start.13 = (bf16[144,256]{1,0:T(8,128)(2,1)S(1)}, bf16[144,256]{1,0:T(8,128)(2,1)S(1)}, u32[]{:S(2)}, u32[]{:S(2)}) collective-permute-start(bf16[144,256]{1,0:T(8,128)(2,1)S(1)} %collective-permute-done.9.refs_3_), channel_id=1, source_target_pairs={{0,1},{1,0},{2,3},{3,2},{4,5},{5,4},{6,7},{7,6},{8,9},{9,8},{10,11... | collective-permute-start | bytes 221192 | tf_op jit(solution)/shard_map/ppermute | solution.py:24
  29.9 14.4 %copy-start.1 = (f32[8,16384]{1,0:T(8,128)S(1)}, f32[8,16384]{1,0:T(8,128)}, u32[]{:S(2)}) copy-start(f32[8,16384]{1,0:T(8,128)} %state_ref.1) | copy-start | bytes 1572868
  29.9 14.4 %copy-start.2 = (f32[8,16384]{1,0:T(8,128)S(1)}, f32[8,16384]{1,0:T(8,128)}, u32[]{:S(2)}) copy-start(f32[8,16384]{1,0:T(8,128)} %climate_ref.1) | copy-start | bytes 1572868
  29.9 14.4 %copy-start.3 = (f32[16384]{0:T(1024)S(1)}, f32[16384]{0:T(1024)}, u32[]{:S(2)}) copy-start(f32[16384]{0:T(1024)} %param.16) | copy-start | bytes 196612
  31.6 6.0 %collective-permute-start.14 = (bf16[8,8192]{1,0:T(8,128)(2,1)S(1)}, bf16[8,8192]{1,0:T(8,128)(2,1)S(1)}, u32[]{:S(2)}, u32[]{:S(2)}) collective-permute-start(bf16[8,8192]{1,0:T(8,128)(2,1)S(1)} %get-tuple-element.12), channel_id=1, source_target_pairs={{0,8},{8,0},{16,24},{24,16},{1,9},{9,1},{17,25},{25,17},{2,10},{10... | collective-permute-start | bytes 393224 | tf_op jit(solution)/shard_map/ppermute | solution.py:24
  33.2 6.0 %collective-permute-start.16 = (bf16[8,8192]{1,0:T(8,128)(2,1)S(1)}, bf16[8,8192]{1,0:T(8,128)(2,1)S(1)}, u32[]{:S(2)}, u32[]{:S(2)}) collective-permute-start(bf16[8,8192]{1,0:T(8,128)(2,1)S(1)} %get-tuple-element.13), channel_id=1, source_target_pairs={{0,16},{8,24},{16,0},{24,8},{1,17},{9,25},{17,1},{25,9},{2,18},{10... | collective-permute-start | bytes 393224 | tf_op jit(solution)/shard_map/ppermute | solution.py:24
  37.6 5.3 %collective-permute-start.15 = (bf16[8,8192]{1,0:T(8,128)(2,1)S(1)}, bf16[8,8192]{1,0:T(8,128)(2,1)S(1)}, u32[]{:S(2)}, u32[]{:S(2)}) collective-permute-start(bf16[8,8192]{1,0:T(8,128)(2,1)S(1)} %add_convert_fusion.3.refs_0_), channel_id=1, source_target_pairs={{0,16},{8,24},{16,0},{24,8},{1,17},{9,25},{17,1},{25,9},{2,18},{10... | collective-permute-start | bytes 393224 | tf_op jit(solution)/shard_map/ppermute | solution.py:24
  39.3 5.0 %collective-permute-start.17 = (bf16[8,8192]{1,0:T(8,128)(2,1)S(1)}, bf16[8,8192]{1,0:T(8,128)(2,1)S(1)}, u32[]{:S(2)}, u32[]{:S(2)}) collective-permute-start(bf16[8,8192]{1,0:T(8,128)(2,1)S(1)} %add_convert_fusion.2.refs_2_), channel_id=1, source_target_pairs={{0,8},{8,0},{16,24},{24,16},{1,9},{9,1},{17,25},{25,17},{2,10},{10... | collective-permute-start | bytes 393224 | tf_op jit(solution)/shard_map/ppermute | solution.py:24
  40.8 19.2 %collective-permute-start.18 = (bf16[2,4,128,128]{3,2,1,0:T(8,128)(2,1)S(1)}, bf16[2,4,128,128]{3,2,1,0:T(8,128)(2,1)S(1)}, u32[]{:S(2)}, u32[]{:S(2)}) collective-permute-start(bf16[2,4,128,128]{3,2,1,0:T(8,128)(2,1)S(1)} %copy-done.4), channel_id=1, source_target_pairs={{0,4},{1,5},{2,6},{3,7},{4,0},{5,1},{6,2},{7,3},{8,12},{9,13},{10,... | collective-permute-start | bytes 786440 | tf_op jit(solution)/shard_map/ppermute | solution.py:24
  46.3 4.5 %collective-permute-start.19 = (bf16[128,256]{1,0:T(8,128)(2,1)S(1)}, bf16[128,256]{1,0:T(8,128)(2,1)S(1)}, u32[]{:S(2)}, u32[]{:S(2)}) collective-permute-start(bf16[128,256]{1,0:T(8,128)(2,1)S(1)} %get-tuple-element.15.refs_2_), channel_id=1, source_target_pairs={{0,2},{1,3},{2,0},{3,1},{4,6},{5,7},{6,4},{7,5},{8,10},{9,11},{10,... | collective-permute-start | bytes 196616 | tf_op jit(solution)/shard_map/ppermute | solution.py:24
  47.4 12.1 %collective-permute-start.20 = (bf16[128,256]{1,0:T(8,128)(2,1)S(1)}, bf16[128,256]{1,0:T(8,128)(2,1)S(1)}, u32[]{:S(2)}, u32[]{:S(2)}) collective-permute-start(bf16[128,256]{1,0:T(8,128)(2,1)S(1)} %get-tuple-element.15.refs_2_), channel_id=1, source_target_pairs={{0,4},{1,5},{2,6},{3,7},{4,0},{5,1},{6,2},{7,3},{8,12},{9,13},{10,... | collective-permute-start | bytes 196616 | tf_op jit(solution)/shard_map/ppermute | solution.py:24
  49.1 10.4 %collective-permute-start.21 = (bf16[128,256]{1,0:T(8,128)(2,1)S(1)}, bf16[128,256]{1,0:T(8,128)(2,1)S(1)}, u32[]{:S(2)}, u32[]{:S(2)}) collective-permute-start(bf16[128,256]{1,0:T(8,128)(2,1)S(1)} %get-tuple-element.15.refs_2_), channel_id=1, source_target_pairs={{0,6},{1,7},{2,4},{3,5},{4,2},{5,3},{6,0},{7,1},{8,14},{9,15},{10,... | collective-permute-start | bytes 196616 | tf_op jit(solution)/shard_map/ppermute | solution.py:24
  50.6 10.4 %collective-permute-start.22 = (bf16[128,256]{1,0:T(8,128)(2,1)S(1)}, bf16[128,256]{1,0:T(8,128)(2,1)S(1)}, u32[]{:S(2)}, u32[]{:S(2)}) collective-permute-start(bf16[128,256]{1,0:T(8,128)(2,1)S(1)} %get-tuple-element.15.refs_2_), channel_id=1, source_target_pairs={{0,1},{1,0},{2,3},{3,2},{4,5},{5,4},{6,7},{7,6},{8,9},{9,8},{10,11... | collective-permute-start | bytes 196616 | tf_op jit(solution)/shard_map/ppermute | solution.py:24
  50.8 10.3 %collective-permute-start.23 = (bf16[128,256]{1,0:T(8,128)(2,1)S(1)}, bf16[128,256]{1,0:T(8,128)(2,1)S(1)}, u32[]{:S(2)}, u32[]{:S(2)}) collective-permute-start(bf16[128,256]{1,0:T(8,128)(2,1)S(1)} %collective-permute-done.19.refs_3_), channel_id=1, source_target_pairs={{0,1},{1,0},{2,3},{3,2},{4,5},{5,4},{6,7},{7,6},{8,9},{9,8},{10,11... | collective-permute-start | bytes 196616 | tf_op jit(solution)/shard_map/ppermute | solution.py:24
  59.5 1.6 %collective-permute-start.24 = (bf16[128,256]{1,0:T(8,128)(2,1)S(1)}, bf16[128,256]{1,0:T(8,128)(2,1)S(1)}, u32[]{:S(2)}, u32[]{:S(2)}) collective-permute-start(bf16[128,256]{1,0:T(8,128)(2,1)S(1)} %collective-permute-done.20.refs_4_), channel_id=1, source_target_pairs={{0,1},{1,0},{2,3},{3,2},{4,5},{5,4},{6,7},{7,6},{8,9},{9,8},{10,11... | collective-permute-start | bytes 196616 | tf_op jit(solution)/shard_map/ppermute | solution.py:24
  59.5 1.6 %collective-permute-start.25 = (bf16[128,256]{1,0:T(8,128)(2,1)S(1)}, bf16[128,256]{1,0:T(8,128)(2,1)S(1)}, u32[]{:S(2)}, u32[]{:S(2)}) collective-permute-start(bf16[128,256]{1,0:T(8,128)(2,1)S(1)} %collective-permute-done.21.refs_5_), channel_id=1, source_target_pairs={{0,1},{1,0},{2,3},{3,2},{4,5},{5,4},{6,7},{7,6},{8,9},{9,8},{10,11... | collective-permute-start | bytes 196616 | tf_op jit(solution)/shard_map/ppermute | solution.py:24
  61.6 20.1 %copy-start.11 = (f32[8,16384]{1,0:T(8,128)S(1)}, f32[8,16384]{1,0:T(8,128)}, u32[]{:S(2)}) copy-start(f32[8,16384]{1,0:T(8,128)} %get-tuple-element.8) | copy-start | bytes 1572868
  61.6 5.6 %collective-permute-start.26 = (bf16[128,512]{1,0:T(8,128)(2,1)S(1)}, bf16[128,512]{1,0:T(8,128)(2,1)S(1)}, u32[]{:S(2)}, u32[]{:S(2)}) collective-permute-start(bf16[128,512]{1,0:T(8,128)(2,1)S(1)} %pair_nodes.1.refs_0_), channel_id=1, source_target_pairs={{0,2},{1,3},{2,0},{3,1},{4,6},{5,7},{6,4},{7,5},{8,10},{9,11},{10,... | collective-permute-start | bytes 393224 | tf_op jit(solution)/shard_map/ppermute | solution.py:24
  62.6 4.6 %collective-permute-start.27 = (bf16[128,512]{1,0:T(8,128)(2,1)S(1)}, bf16[128,512]{1,0:T(8,128)(2,1)S(1)}, u32[]{:S(2)}, u32[]{:S(2)}) collective-permute-start(bf16[128,512]{1,0:T(8,128)(2,1)S(1)} %pair_nodes.1.refs_0_), channel_id=1, source_target_pairs={{0,1},{1,0},{2,3},{3,2},{4,5},{5,4},{6,7},{7,6},{8,9},{9,8},{10,11... | collective-permute-start | bytes 393224 | tf_op jit(solution)/shard_map/ppermute | solution.py:24
  67.2 1.3 %collective-permute-start.28 = (bf16[128,512]{1,0:T(8,128)(2,1)S(1)}, bf16[128,512]{1,0:T(8,128)(2,1)S(1)}, u32[]{:S(2)}, u32[]{:S(2)}) collective-permute-start(bf16[128,512]{1,0:T(8,128)(2,1)S(1)} %collective-permute-done.26.refs_1_), channel_id=1, source_target_pairs={{0,1},{1,0},{2,3},{3,2},{4,5},{5,4},{6,7},{7,6},{8,9},{9,8},{10,11... | collective-permute-start | bytes 393224 | tf_op jit(solution)/shard_map/ppermute | solution.py:24
  70.3 5.6 %collective-permute-start.31 = (bf16[8,8192]{1,0:T(8,128)(2,1)S(1)}, bf16[8,8192]{1,0:T(8,128)(2,1)S(1)}, u32[]{:S(2)}, u32[]{:S(2)}) collective-permute-start(bf16[8,8192]{1,0:T(8,128)(2,1)S(1)} %get-tuple-element.17), channel_id=1, source_target_pairs={{0,16},{8,24},{16,0},{24,8},{1,17},{9,25},{17,1},{25,9},{2,18},{10... | collective-permute-start | bytes 393224 | tf_op jit(solution)/shard_map/ppermute | solution.py:24
  70.9 5.7 %collective-permute-start.29 = (bf16[8,8192]{1,0:T(8,128)(2,1)S(1)}, bf16[8,8192]{1,0:T(8,128)(2,1)S(1)}, u32[]{:S(2)}, u32[]{:S(2)}) collective-permute-start(bf16[8,8192]{1,0:T(8,128)(2,1)S(1)} %get-tuple-element.16), channel_id=1, source_target_pairs={{0,8},{8,0},{16,24},{24,16},{1,9},{9,1},{17,25},{25,17},{2,10},{10... | collective-permute-start | bytes 393224 | tf_op jit(solution)/shard_map/ppermute | solution.py:24
  75.9 5.0 %collective-permute-start.32 = (bf16[8,8192]{1,0:T(8,128)(2,1)S(1)}, bf16[8,8192]{1,0:T(8,128)(2,1)S(1)}, u32[]{:S(2)}, u32[]{:S(2)}) collective-permute-start(bf16[8,8192]{1,0:T(8,128)(2,1)S(1)} %add_convert_fusion), channel_id=1, source_target_pairs={{0,8},{8,0},{16,24},{24,16},{1,9},{9,1},{17,25},{25,17},{2,10},{10... | collective-permute-start | bytes 393224 | tf_op jit(solution)/shard_map/ppermute | solution.py:24
  76.6 5.0 %collective-permute-start.30 = (bf16[8,8192]{1,0:T(8,128)(2,1)S(1)}, bf16[8,8192]{1,0:T(8,128)(2,1)S(1)}, u32[]{:S(2)}, u32[]{:S(2)}) collective-permute-start(bf16[8,8192]{1,0:T(8,128)(2,1)S(1)} %add_convert_fusion.1), channel_id=1, source_target_pairs={{0,16},{8,24},{16,0},{24,8},{1,17},{9,25},{17,1},{25,9},{2,18},{10... | collective-permute-start | bytes 393224 | tf_op jit(solution)/shard_map/ppermute | solution.py:24
